TPU v7x, 128 devices: a whole 4x4x4 slice. The times are simulated.
128 devices in a mesh: prow: 64 (over z, y, x), pcol: 2 (over core).
Axes of the slice: x: 4, y: 4, z: 4, core: 2. Of those that a mesh axis runs over, the one named last changes fastest.
Arguments:
- matrix: float32 [4, 64, 128, 32, 2, 128], P(None, 'prow', None, None, 'pcol'), may hold values from -6 to 6
- pivots: int32 [2, 128], replicated, may hold values from 0 to 32767, as said below
- upper_inverse: float32 [2, 128, 128], replicated, may hold values from -0.046875 to 0.046875
- lower_inverse: float32 [2, 128, 128], replicated, may hold values from -0.5 to 0.5
Outputs:
- factored: float32 [4, 64, 128, 32, 2, 128], P(None, 'prow', None, None, 'pcol')
Inputs may be any that keep to these rules, and one draw needn't show every extreme that they name: pivots[k, i] lies between k * 128 + i and 32767.
All inputs are finite; a program needn't handle non-finite values.
Results may differ from a plain program's by a relative error of at most 0.0001.
Values sent between devices are 32-bit elements; how exact they have to be, the bound alone decides.
No kernel may reach another device: no remote copies, remote signals or barrier semaphores. Data moves between devices by JAX's collectives and lax.ppermute only.
A program may use at most 128 MiB of HBM per device.

v0:
```python
import jax
import jax.numpy as jnp
from jax import lax
from jax.sharding import PartitionSpec as P

NB = 128


def broadcast(value, axis, source):
    kept = jnp.where(lax.axis_index(axis) == source, value, 0).astype(value.dtype)
    return lax.psum(kept, axis)


def build_permutation(row_pivots, step_index, row_count):

    def swap_one(position, permutation):
        target = step_index * NB + position
        chosen = row_pivots[position]
        at_target = permutation[target]
        at_chosen = permutation[chosen]
        return permutation.at[target].set(at_chosen).at[chosen].set(at_target)

    return lax.fori_loop(0, NB, swap_one, jnp.arange(row_count, dtype=jnp.int32))


def pick_rows(column_part, step_index, permutation, grid_row, grid_rows):
    sources = permutation[step_index * NB : (step_index + 1) * NB]
    owner_row = sources // NB % grid_rows
    local_index = sources // (NB * grid_rows) * NB + sources % NB
    chosen_rows = jnp.take(column_part, local_index, axis=0)
    return jnp.where((owner_row == grid_row)[:, None], chosen_rows, 0.0)


def place_rows(column_part, step_index, permutation, global_rows, incoming, previous):
    moved_from = jnp.take(permutation, global_rows)
    in_block = global_rows // NB == step_index
    displaced = moved_from != global_rows
    row_table = jnp.concatenate([incoming, previous], axis=0)
    row_index = jnp.where(
        in_block,
        global_rows - step_index * NB,
        NB + jnp.clip(moved_from - step_index * NB, 0, NB - 1),
    )
    replaced = jnp.take(row_table, row_index, axis=0)
    return jnp.where((in_block | displaced)[:, None], replaced, column_part)


def swap_rows(column_part, step_index, permutation, global_rows, grid_row, grid_rows):
    picked = pick_rows(column_part, step_index, permutation, grid_row, grid_rows)
    incoming = lax.psum(picked, "prow")
    start_row = step_index // grid_rows * NB
    previous = broadcast(column_part[start_row : start_row + NB], "prow", step_index % grid_rows)
    return (
        place_rows(column_part, step_index, permutation, global_rows, incoming, previous),
        incoming,
    )


def factor_panel(panel_part, step_index, global_rows, upper_factor):
    below = (global_rows // NB > step_index)[:, None]
    triangle = jnp.triu(upper_factor)
    root_column = step_index % lax.axis_size("pcol")
    lower_panel = jnp.where(
        below,
        jnp.dot(
            panel_part,
            triangle,
            precision=lax.Precision.HIGHEST,
            preferred_element_type=jnp.float32,
        ),
        0.0,
    )
    return broadcast(lower_panel, "pcol", root_column)


def upper_block(incoming, global_columns, step_index, lower_factor):
    unit_lower = jnp.tril(lower_factor, -1) + jnp.eye(NB, dtype=jnp.float32)
    right = (global_columns // NB > step_index)[None, :]
    return jnp.where(
        right,
        jnp.dot(
            unit_lower,
            incoming,
            precision=lax.Precision.HIGHEST,
            preferred_element_type=jnp.float32,
        ),
        0.0,
    )


def update_trailing(column_part, global_columns, global_rows, step_index, lower_panel, upper_rows):
    grid_rows = lax.axis_size("prow")
    right = (global_columns // NB > step_index)[None, :]
    below = (global_rows // NB > step_index)[:, None]
    column_part = column_part - jnp.dot(
        lower_panel, upper_rows, precision=lax.Precision.HIGHEST, preferred_element_type=jnp.float32
    )
    start_row = step_index // grid_rows * NB
    block_rows = column_part[start_row : start_row + NB]
    in_block = (global_rows[start_row : start_row + NB] // NB == step_index)[:, None]
    block_rows = jnp.where(in_block & right, upper_rows, block_rows)
    column_part = column_part.at[start_row : start_row + NB].set(block_rows)
    is_panel = (global_columns[:NB] // NB == step_index)[None, :]
    head_part = jnp.where(is_panel & below, lower_panel, column_part[:, :NB])
    column_part = column_part.at[:, :NB].set(head_part)
    return column_part


def local(matrix, pivots, upper_inverse, lower_inverse):
    grid_rows = lax.axis_size("prow")
    grid_cols = lax.axis_size("pcol")
    grid_row = lax.axis_index("prow")
    grid_column = lax.axis_index("pcol")
    local_rows = matrix.shape[0] * NB
    local_columns = matrix.shape[3] * NB
    working = matrix.reshape(local_rows, local_columns)
    row_iota = jnp.arange(local_rows, dtype=jnp.int32)
    global_rows = (row_iota // NB * grid_rows + grid_row) * NB + row_iota % NB
    column_iota = jnp.arange(local_columns, dtype=jnp.int32)
    global_columns = (column_iota // NB * grid_cols + grid_column) * NB + column_iota % NB
    row_count = local_rows * grid_rows
    first_order = build_permutation(pivots[0], 0, row_count)
    second_order = build_permutation(pivots[1], 1, row_count)
    working, incoming = swap_rows(working, 0, first_order, global_rows, grid_row, grid_rows)
    lower_first = factor_panel(working[:, :NB], 0, global_rows, upper_inverse[0])
    upper_first = upper_block(incoming, global_columns, 0, lower_inverse[0])
    working = update_trailing(working, global_columns, global_rows, 0, lower_first, upper_first)
    working, incoming = swap_rows(working, 1, second_order, global_rows, grid_row, grid_rows)
    lower_second = factor_panel(working[:, :NB], 1, global_rows, upper_inverse[1])
    upper_second = upper_block(incoming, global_columns, 1, lower_inverse[1])
    working = update_trailing(working, global_columns, global_rows, 1, lower_second, upper_second)
    return working.reshape(matrix.shape)


def solution(mesh):
    return jax.shard_map(
        local,
        mesh=mesh,
        in_specs=(P(None, "prow", None, None, "pcol", None), P(), P(), P()),
        out_specs=P(None, "prow", None, None, "pcol", None),
        check_vma=False,
    )
```

profile of v0, /device:TPU:1, one launch (start us, length us, event | category | flops | bytes accessed | tf_op | source)
XLA Modules:
  0.0 1510.4 jit_solution(9891370761534507786)
XLA Ops:
  7.3 560.1 %while.37 = (s32[]{:T(128)}, s32[32768]{0:T(1024)S(1)}, s32[128]{0:T(128)S(1)}, s32[]{:T(128)}, s32[]{:T(128)}, /*index=5*/s32[]{:T(128)}, s32[]{:T(128)}) while((s32[]{:T(128)}, s32[32768]{0:T(1024)S(1)}, s32[128]{0:T(128)S(1)}, s32[]{:T(128)}, s32[]{:T(128)}, /*index=5*/s32[]{:T(128)}, s32[]{:T(128)}) %tuple.123), condition=%wide.region_3.5_spmd, body=%wide.region_2.4_spmd.sunk | while | flops 13 | bytes 2247 | solution.py:23
  567.4 14.9 copy.14
  582.3 8.1 fusion
  590.4 3.0 copy.15
  593.3 5.6 gather_fusion.2
  599.0 1.7 select_select_fusion.3
  600.7 3.1 gather_fusion.1
  604.8 593.5 %while.36 = (s32[]{:T(128)}, s32[32768]{0:T(1024)S(1)}, s32[128]{0:T(128)S(1)}, s32[]{:T(128)}, s32[]{:T(128)}, /*index=5*/s32[]{:T(128)}, s32[]{:T(128)}, s32[]{:T(128)}, s32[]{:T(128)}) while((s32[]{:T(128)}, s32[32768]{0:T(1024)S(1)}, s32[128]{0:T(128)S(1)}, s32[]{:T(128)}, s32[]{:T(128)}, /*index=5*/s32[]{:T(128)}, s32[]{:T(128)}, ...), condition=%wide.region_1.2_spmd, body=%wide.region_0.1_spmd.sunk | while | flops 17 | bytes 2309 | solution.py:23
  1198.3 4.6 pad_maximum_fusion
  1203.0 11.1 gather_fusion.3
  1214.0 12.8 select_select_fusion.1
  1226.8 3.4 copy-done.1
  1230.2 1.1 fusion.4
  1231.5 3.5 convolution_select_fusion.1
  1235.0 24.0 %all-reduce.7.cloned.1.call-done = f32[512,128]{1,0:T(8,128)} async-done(((f32[512,128]{1,0:T(8,128)}), f32[512,128]{1,0:T(8,128)}) %all-reduce.7.cloned.1.call-update) | async-done | bytes 262160 | tf_op jit(solution)/shard_map/psum | solution.py:11
  1259.0 22.6 %convolution_subtract_fusion.1 = f32[512,4096]{1,0:T(8,128)} fusion(f32[512,4096]{1,0:T(8,128)} %copy-done.1, f32[512,128]{1,0:T(8,128)} %all-reduce.7.cloned.1.call-done, f32[128,4096]{1,0:T(8,128)S(1)} %convolution_select_fusion.1), kind=kOutput, calls=%fused_computation.14 | convolution fusion | flops 3223322624 | bytes 19136512 | tf_op jit(solution)/shard_map/dot_general | solution.py:95
  1281.6 3.3 fusion.2
  1284.9 2.4 fusion.5
  1287.3 5.6 gather_fusion.4
  1292.9 3.1 slice_select_fusion.1
  1296.0 1.7 select_select_fusion.2
  1297.8 3.1 gather_fusion
  1301.0 135.9 %all-reduce.11.cloned.1.call-done = (f32[128,4096]{1,0:T(8,128)}, f32[128,4096]{1,0:T(8,128)}) async-done(((f32[128,4096]{1,0:T(8,128)}, f32[128,4096]{1,0:T(8,128)}), (f32[128,4096]{1,0:T(8,128)}, f32[128,4096]{1,0:T(8,128)})) %all-reduce.11.cloned.1.call-update) | async-done | bytes 4194320 | tf_op jit(solution)/shard_map/psum | solution.py:11
  1436.9 4.6 pad_maximum_fusion.1
  1441.6 11.0 gather_fusion.5
  1452.6 7.0 select_select_fusion
  1459.6 3.4 copy-done
  1463.0 1.1 fusion.3
  1464.2 3.5 convolution_select_fusion
  1467.7 19.2 %all-reduce.9.cloned.1.call-done = f32[512,128]{1,0:T(8,128)} async-done(((f32[512,128]{1,0:T(8,128)}), f32[512,128]{1,0:T(8,128)}) %all-reduce.9.cloned.1.call-update) | async-done | bytes 262160 | tf_op jit(solution)/shard_map/psum | solution.py:11
  1486.9 9.8 convolution_subtract_fusion
  1498.4 5.2 copy.9
  (1068 shorter events, 706.5 us)
Async XLA Ops:
  6.5 1191.8 %all-reduce.13.cloned.1.call-start = ((), (), s32[]{:S(2)}) async-start(), calls=%async_computation.3 | async-start | bytes 8388608 | tf_op jit(solution)/shard_map/psum | solution.py:11
  600.7 658.4 %all-reduce.7.cloned.1.call-start = ((), (), s32[]{:S(2)}) async-start(), calls=%async_computation | async-start | bytes 524288 | tf_op jit(solution)/shard_map/psum | solution.py:11
  1214.0 16.2 %copy-start.4 = (f32[2,128,128]{2,1,0:T(8,128)S(1)}, f32[2,128,128]{2,1,0:T(8,128)}, u32[]{:S(2)}) copy-start(f32[2,128,128]{2,1,0:T(8,128)} %param.32) | copy-start | bytes 393220
  1214.0 17.4 %copy-start.5 = (f32[2,128,128]{2,1,0:T(8,128)S(1)}, f32[2,128,128]{2,1,0:T(8,128)}, u32[]{:S(2)}) copy-start(f32[2,128,128]{2,1,0:T(8,128)} %param.33) | copy-start | bytes 393220
  1226.8 3.4 copy-start.1
  1231.4 205.5 %all-reduce.11.cloned.1.call-start = ((), (), s32[]{:S(2)}) async-start(), calls=%async_computation.2 | async-start | bytes 8388608 | tf_op jit(solution)/shard_map/psum | solution.py:11
  1281.6 3.3 copy-start.3
  1297.7 189.1 %all-reduce.9.cloned.1.call-start = ((), (), s32[]{:S(2)}) async-start(), calls=%async_computation.1 | async-start | bytes 524288 | tf_op jit(solution)/shard_map/psum | solution.py:11
  1459.6 3.4 copy-start
  1496.7 1.0 copy-start.2
Sparse Core Ops, SparseCore 0:
  600.8 141.4 all-reduce.12
  1231.5 27.4 all-reduce.6
  1297.9 139.0 all-reduce.10
  1464.3 22.5 all-reduce.8
where the time goes:
time: 1530 us; the launch traced here: 1510 us
  loops' own time  451 us (29%)
  other arithmetic  447 us (29%)
  local copies, waits for them, and re-layouts  378 us (25%)
  waiting for transfers between devices  179 us (12%)
  matrix products  41.7 us (3%)
    another operation x2, loops' own time, build_permutation(): lax.fori_loop(0, NB, swap_one, jnp.arange(row_count, dtype=jnp.int32))  451 us
    scatter x512, other arithmetic, swap_one(): return permutation.at[target].set(at_chosen).at[chosen].set(at_target)  395 us
    psum x4, waiting for transfers between devices, broadcast(): return lax.psum(kept, axis)  179 us
    another operation x256, local copies, waits for them, and re-layouts  154 us
    dynamic_slice x256, local copies, waits for them, and re-layouts, swap_one(): chosen = row_pivots[position]  153 us
    dot_general x2, matrix products, update_trailing(): jnp.dot(lower_panel, upper_rows, precision=lax.Precision.HIGHEST, preferr...  32.4 us
  transfers between devices with their start and end apart: 4, of which 3 were waited for; matrix products, arithmetic and copies ran while one was open for 25% of the time, Pallas kernels for 0%

commit v1 on v0

v1 whole, which is shorter than its diff:
```python
import jax
import jax.numpy as jnp
from jax import lax
from jax.experimental import pallas as pl
from jax.experimental.pallas import tpu as pltpu
from jax.sharding import PartitionSpec as P

NB = 128
PICKS = 2 * NB
GROUP = 8
HBM = pl.BlockSpec(memory_space=pl.ANY)
SMEM = pl.BlockSpec(memory_space=pltpu.SMEM)
VMEM = pl.BlockSpec(memory_space=pltpu.VMEM)


def place_of(row, grid_rows):
    block = row // NB
    return block % grid_rows, block // grid_rows * NB + row % NB


def route_kernel(grid_rows, place, pivots, rows_hbm, _, slots_hbm, counts, moved_row, moved_slot, source, sems):
    me = place[0]

    def start(i, carry):
        source[i] = i
        source[pivots[i]] = pivots[i]
        return carry

    lax.fori_loop(0, PICKS, start, 0)

    def reset(i, carry):
        source[i] = i
        return carry

    lax.fori_loop(0, PICKS, reset, 0)

    def exchange(i, carry):
        chosen = pivots[i]
        at_target = source[i]
        at_chosen = source[chosen]
        source[i] = at_chosen
        source[chosen] = at_target
        return carry

    lax.fori_loop(0, PICKS, exchange, 0)

    def copy_of(slot, local):
        return pltpu.make_async_copy(rows_hbm.at[local], slots_hbm.at[slot], sems.at[slot])

    def send(i, carry):
        owner, local = place_of(source[i], grid_rows)

        @pl.when(owner == me)
        def _():
            copy_of(i, local).start()

        return carry

    lax.fori_loop(0, PICKS, send, 0)

    def send_previous(j, carry):
        @pl.when(me == j)
        def _():
            pltpu.make_async_copy(
                rows_hbm.at[pl.ds(0, NB)], slots_hbm.at[pl.ds(PICKS + j * NB, NB)], sems.at[PICKS]
            ).start()

        return carry

    lax.fori_loop(0, 2, send_previous, 0)

    def list_moved(i, count):
        chosen = pivots[i]
        owner, local = place_of(chosen, grid_rows)
        mine = jnp.logical_and(owner == me, chosen >= PICKS)

        @pl.when(mine)
        def _():
            moved_row[count] = local
            moved_slot[count] = PICKS + source[chosen]

        return count + mine.astype(jnp.int32)

    counts[0] = lax.fori_loop(0, PICKS, list_moved, 0)

    def finish(i, carry):
        owner, local = place_of(source[i], grid_rows)

        @pl.when(owner == me)
        def _():
            copy_of(i, local).wait()

        return carry

    lax.fori_loop(0, PICKS, finish, 0)

    @pl.when(me < 2)
    def _():
        pltpu.make_async_copy(
            rows_hbm.at[pl.ds(0, NB)], slots_hbm.at[pl.ds(PICKS, NB)], sems.at[PICKS]
        ).wait()


def route(place, pivots, rows, grid_rows):
    slots = jax.ShapeDtypeStruct((2 * PICKS,) + rows.shape[1:], rows.dtype)
    table = jax.ShapeDtypeStruct((PICKS,), jnp.int32)
    return pl.pallas_call(
        lambda *refs: route_kernel(grid_rows, *refs),
        out_shape=(slots, jax.ShapeDtypeStruct((1,), jnp.int32), table, table),
        in_specs=[SMEM, SMEM, HBM, HBM],
        out_specs=(HBM, SMEM, SMEM, SMEM),
        scratch_shapes=[
            pltpu.SMEM((rows.shape[0] * grid_rows,), jnp.int32),
            pltpu.SemaphoreType.DMA((PICKS + 1,)),
        ],
        input_output_aliases={3: 0},
        name="route",
    )(place, pivots, rows, jnp.zeros(slots.shape, slots.dtype))


def dot(left, right):
    return jnp.dot(left, right, precision=lax.Precision.HIGHEST, preferred_element_type=jnp.float32)


def halves(value):
    high = value.astype(jnp.bfloat16)
    return high, (value - high.astype(jnp.float32)).astype(jnp.bfloat16)


def update_kernel(
    place, counts, moved_row, moved_slot, panel, slot_panel, upper_inverse, lower_inverse,
    rows_hbm, slots_hbm, out_hbm,
    rows, picked, moved, result, own_panel, high, low, row_sems, pick_sems, moved_sems, out_sems,
):
    grid_row, grid_column = place[0], place[1]
    groups = rows.shape[0]

    def fetch(sources, target, sems, count, group):
        columns = pl.ds(group * GROUP, GROUP)
        return pltpu.make_async_copy(
            sources.at[pl.ds(0, count), columns, :], target.at[group], sems.at[group]
        )

    def fetch_moved(i):
        return pltpu.make_async_copy(slots_hbm.at[moved_slot[i]], moved.at[i], moved_sems.at[i])

    for group in range(groups):
        fetch(slots_hbm, picked, pick_sems, PICKS, group).start()
        fetch(rows_hbm, rows, row_sems, rows.shape[1], group).start()

    def start_moved(i, carry):
        fetch_moved(i).start()
        return carry

    lax.fori_loop(0, counts[0], start_moved, 0)

    own_panel[...] = panel[...]

    def patch_panel(i, carry):
        for side in range(2):
            own_panel[side, pl.ds(moved_row[i], 1), :] = slot_panel[side, pl.ds(moved_slot[i], 1), :]
        return carry

    lax.fori_loop(0, counts[0], patch_panel, 0)

    row_at = lax.broadcasted_iota(jnp.int32, (NB, NB), 0)
    column_at = lax.broadcasted_iota(jnp.int32, (NB, NB), 1)
    upper = [jnp.where(row_at <= column_at, upper_inverse[k], 0.0) for k in range(2)]
    lower = [
        jnp.where(row_at > column_at, lower_inverse[k], jnp.where(row_at == column_at, 1.0, 0.0))
        for k in range(2)
    ]
    block_lower = dot(slot_panel[0, NB:PICKS, :], upper[0])
    block_upper = dot(lower[0], slot_panel[1, :NB, :])
    block_second = slot_panel[1, NB:PICKS, :] - dot(block_lower, block_upper)
    mixed = -dot(lower[1], dot(block_lower, lower[0]))
    lower_first = dot(own_panel[0], upper[0])
    lower_second = dot(own_panel[1] - dot(lower_first, block_upper), upper[1])
    weight_first = dot(lower_first, lower[0]) + dot(lower_second, mixed)
    weight_second = dot(lower_second, lower[1])
    first_home, second_home = grid_row == 0, grid_row == 1
    is_home = grid_row < 2

    def at_home(first, second, other):
        top = jnp.where(first_home, first, jnp.where(second_home, second, other[:NB]))
        return jnp.concatenate([top, other[NB:]], axis=0)

    weight = jnp.concatenate(
        [
            at_home(-lower[0], -mixed, weight_first),
            at_home(jnp.zeros_like(lower[1]), -lower[1], weight_second),
        ],
        axis=1,
    )
    high[...], low[...] = halves(weight)
    head = jnp.where(
        grid_column == 0,
        at_home(slot_panel[0, :NB, :], block_lower, lower_first),
        at_home(block_upper, block_second, lower_second),
    )

    def wait_moved(i, carry):
        fetch_moved(i).wait()
        return carry

    lax.fori_loop(0, counts[0], wait_moved, 0)

    def write(group, slot):
        return pltpu.make_async_copy(
            result.at[slot], out_hbm.at[:, pl.ds(group * GROUP, GROUP), :], out_sems.at[slot]
        )

    for group in range(groups):
        slot = group % 2
        fetch(rows_hbm, rows, row_sems, rows.shape[1], group).wait()
        fetch(slots_hbm, picked, pick_sems, PICKS, group).wait()

        def patch(i, carry):
            rows[group, moved_row[i], :, :] = moved[i, pl.ds(group * GROUP, GROUP), :]
            return carry

        lax.fori_loop(0, counts[0], patch, 0)
        if group >= 2:
            write(group - 2, slot).wait()
        for pair in range(GROUP // 2):
            columns = [2 * pair, 2 * pair + 1]
            right = jnp.concatenate([picked[group, :, c, :] for c in columns], axis=1)
            right_high, right_low = halves(right)
            product = jnp.dot(high[...], right_high, preferred_element_type=jnp.float32)
            product += jnp.dot(high[...], right_low, preferred_element_type=jnp.float32)
            product += jnp.dot(low[...], right_high, preferred_element_type=jnp.float32)
            for n, c in enumerate(columns):
                own = rows[group, :, c, :]
                top = jnp.where(is_home, 0.0, own[:NB])
                own = jnp.concatenate([top, own[NB:]], axis=0)
                value = own - product[:, n * NB : (n + 1) * NB]
                if group == 0 and c == 0:
                    value = head
                result[slot, :, c, :] = value
        write(group, slot).start()
    for group in range(max(0, groups - 2), groups):
        write(group, group % 2).wait()


def update(place, counts, moved_row, moved_slot, panel, slot_panel, upper_inverse, lower_inverse, rows, slots):
    local_rows, blocks, _ = rows.shape
    groups = blocks // GROUP
    return pl.pallas_call(
        update_kernel,
        out_shape=jax.ShapeDtypeStruct(rows.shape, rows.dtype),
        in_specs=[SMEM] * 4 + [VMEM] * 4 + [HBM] * 2,
        out_specs=HBM,
        scratch_shapes=[
            pltpu.VMEM((groups, local_rows, GROUP, NB), jnp.float32),
            pltpu.VMEM((groups, PICKS, GROUP, NB), jnp.float32),
            pltpu.VMEM((PICKS, blocks, NB), jnp.float32),
            pltpu.VMEM((2, local_rows, GROUP, NB), jnp.float32),
            pltpu.VMEM((2, local_rows, NB), jnp.float32),
            pltpu.VMEM((local_rows, PICKS), jnp.bfloat16),
            pltpu.VMEM((local_rows, PICKS), jnp.bfloat16),
            pltpu.SemaphoreType.DMA((groups,)),
            pltpu.SemaphoreType.DMA((groups,)),
            pltpu.SemaphoreType.DMA((PICKS,)),
            pltpu.SemaphoreType.DMA((2,)),
        ],
        compiler_params=pltpu.CompilerParams(vmem_limit_bytes=48 << 20),
        name="update",
    )(place, counts, moved_row, moved_slot, panel, slot_panel, upper_inverse, lower_inverse, rows, slots)


def local(matrix, pivots, upper_inverse, lower_inverse):
    grid_rows = lax.axis_size("prow")
    rows = matrix.reshape(matrix.shape[0] * NB, matrix.shape[3], NB)
    place = jnp.stack([lax.axis_index("prow"), lax.axis_index("pcol")]).astype(jnp.int32)
    panel = lax.all_gather(rows[:, 0, :], "pcol", axis=0)
    slots, counts, moved_row, moved_slot = route(place, pivots.reshape(-1), rows, grid_rows)
    slots = lax.psum(slots, "prow")
    slot_panel = lax.all_gather(slots[:, 0, :], "pcol", axis=0)
    out = update(
        place, counts, moved_row, moved_slot, panel, slot_panel, upper_inverse, lower_inverse, rows, slots
    )
    return out.reshape(matrix.shape)


def solution(mesh):
    return jax.shard_map(
        local,
        mesh=mesh,
        in_specs=(P(None, "prow", None, None, "pcol", None), P(), P(), P()),
        out_specs=P(None, "prow", None, None, "pcol", None),
        check_vma=False,
    )
```

time: 1530 us -> 289 us (0.19); the launches traced: 1510 us -> 289 us
  loops' own time: 451 us -> 0 us
  other arithmetic: 447 us -> 0.62 us
  local copies, waits for them, and re-layouts: 378 us -> 8.01 us
  Pallas kernels: 0 us -> 101 us
  matrix products: 41.7 us -> 0 us
  waiting for transfers between devices: 179 us -> 158 us
    another operation x2 -> x0, loops' own time: 451 us -> none  [build_permutation(): lax.fori_loop(0, NB, swap_one, jnp.arange(row_count, dtype=jnp.int32))]
    scatter x516 -> x0, other arithmetic: 402 us -> none  [the longest x512 395 us: swap_one(): return permutation.at[target].set(at_chosen).at[chosen].set(at_target)]
    another operation x256 -> x0, local copies, waits for them, and re-layouts: 154 us -> none
    dynamic_slice x256 -> x0, local copies, waits for them, and re-layouts: 153 us -> none  [swap_one(): chosen = row_pivots[position]]
    pallas_call x0 -> x2, Pallas kernels: none -> 101 us  [the longest x1 78.2 us: route(): pl.pallas_call(lambda *refs: route_kernel(grid_rows, *refs), out_shape=(s...]
    dot_general x6 -> x0, matrix products: 41.7 us -> none  [the longest x2 32.4 us: update_trailing(): jnp.dot(lower_panel, upper_rows, precision=lax.Precision.HIGHEST, preferr...]
    gather x6 -> x0, local copies, waits for them, and re-layouts: 39.6 us -> none  [the longest x2 22.1 us: place_rows(): replaced = jnp.take(row_table, row_index, axis=0)]
    select_n x7 -> x0, other arithmetic: 34.3 us -> none  [the longest x2 19.8 us: place_rows(): return jnp.where((in_block | displaced)[:, None], replaced, column_part)]
  transfers between devices with their start and end apart: 4 -> 1, of which waited for: 3 -> 1; matrix products, arithmetic and copies ran while one was open for 25% -> 1% of each run, Pallas kernels for 0% -> 0%
where the time goes in v1:
time: 289 us
  waiting for transfers between devices  158 us (55%)
  Pallas kernels  101 us (35%)
  between operations  13.5 us (5%)
  local copies, waits for them, and re-layouts  8.01 us (3%)
  blocking collectives  8.01 us (3%)
    psum x1, waiting for transfers between devices, local(): slots = lax.psum(slots, 'prow')  158 us
    pallas_call x1, Pallas kernels, route(): pl.pallas_call(lambda *refs: route_kernel(grid_rows, *refs), out_shape=(s...  78.2 us
    pallas_call x1, Pallas kernels, update(): pl.pallas_call(update_kernel, out_shape=jax.ShapeDtypeStruct(rows.shape,...  22.7 us
  transfers between devices with their start and end apart: 1, of which 1 were waited for; matrix products, arithmetic and copies ran while one was open for 1% of the time, Pallas kernels for 0%

profile of v1, /device:TPU:1, one launch (start us, length us, event | category | flops | bytes accessed | tf_op | source)
XLA Modules:
  0.0 289.4 jit_solution(7081262810894038651)
XLA Ops:
  6.5 0.0 all-reduce.2.cloned.1.call-start
  6.5 0.6 pad_add_fusion.refs_0_.place
  7.2 4.5 %broadcast_in_dim.3.refs_3_ = f32[512,32,128]{2,1,0:T(8,128)} broadcast(f32[]{:T(128)} %constant.9.clone.1), dimensions={} | broadcast | bytes 8388612 | tf_op jit(solution)/shard_map/broadcast_in_dim | solution.py:118
  11.6 78.2 %route.1 = (f32[512,32,128]{2,1,0:T(8,128)}, s32[1]{0:T(128)}, s32[256]{0:T(256)}, s32[256]{0:T(256)}) custom-call(s32[2]{0:T(128)} %pad_add_fusion.refs_0_.place, s32[256]{0:T(256)} %bitcast.14, f32[512,32,128]{2,1,0:T(8,128)} %bitcast.11, f32[512,32,128]{2,1,0:T(8,128)} %broadcast_in_dim.3.refs_3_), custom_call_target="tpu_custom_call", output_to_operand_aliasing={{0}: (3, {})} | custom-call | tf_op jit(solution)/shard_map/route/pallas_call | solution.py:107
  89.8 0.0 copy-start
  89.8 0.0 copy-start.1
  89.8 0.0 copy-start.2
  89.9 0.0 copy-start.3
  89.9 0.0 copy-start.4
  89.9 0.0 all-reduce.2.cloned.1.call-update
  89.9 1.8 slice.8
  91.7 3.2 %all-gather = f32[1024,1,128]{2,1,0:T(1,128)S(1)} all-gather(f32[512,1,128]{2,1,0:T(1,128)S(1)} %slice.8), channel_id=2, replica_groups=mesh['prow'=64,'pcol'=2] {'pcol'}, dimensions={0}, use_global_device_ids=true | all-gather | bytes 786432 | tf_op jit(solution)/shard_map/all_gather | solution.py:275
  94.9 158.4 %all-reduce.2.cloned.1.call-done.slots_hbm = f32[512,32,128]{2,1,0:T(8,128)} async-done(((f32[512,32,128]{2,1,0:T(8,128)}), f32[512,32,128]{2,1,0:T(8,128)}) %all-reduce.2.cloned.1.call-update) | async-done | bytes 8388624 | tf_op jit(solution)/shard_map/psum | solution.py:277
  253.3 1.7 slice.9
  255.1 4.8 %all-gather.1 = f32[1024,1,128]{2,1,0:T(1,128)S(1)} all-gather(f32[512,1,128]{2,1,0:T(1,128)S(1)} %slice.9), channel_id=3, replica_groups=mesh['prow'=64,'pcol'=2] {'pcol'}, dimensions={0}, use_global_device_ids=true | all-gather | bytes 786432 | tf_op jit(solution)/shard_map/all_gather | solution.py:278
  259.8 0.0 copy-done
  259.8 0.0 copy-done.1
  259.8 0.0 copy-done.2
  259.8 0.0 copy-done.3
  259.8 0.0 copy-done.4
  259.9 22.7 %update.1 = f32[512,32,128]{2,1,0:T(8,128)} custom-call(s32[2]{0:T(128)S(1)} %copy-done.2, s32[1]{0:T(128)} %get-tuple-element.9.counts, s32[256]{0:T(256)S(1)} %copy-done.3, s32[256]{0:T(256)S(1)} %copy-done.4, f32[2,512,128]{2,1,0:T(8,128)S(1)} %bitcast.9, f32[2,512,128]{2,1,0:T(8,128)S(1)} %bitcast.10, f32[2,128,128]{2,1,0:T(8,128)S(1)} %copy-done, ...), custom_call_target="tpu_custom_call" | custom-call | tf_op jit(solution)/shard_map/update/pallas_call | solution.py:248
Async XLA Ops:
  6.5 246.8 %all-reduce.2.cloned.1.call-start = ((), (), s32[]{:S(2)}) async-start(), calls=%async_computation | async-start | bytes 16777216 | tf_op jit(solution)/shard_map/psum | solution.py:277
  89.8 170.0 %copy-start = (f32[2,128,128]{2,1,0:T(8,128)S(1)}, f32[2,128,128]{2,1,0:T(8,128)}, u32[]{:S(2)}) copy-start(f32[2,128,128]{2,1,0:T(8,128)} %upper_inverse.1) | copy-start | bytes 393220
  89.8 170.0 %copy-start.1 = (f32[2,128,128]{2,1,0:T(8,128)S(1)}, f32[2,128,128]{2,1,0:T(8,128)}, u32[]{:S(2)}) copy-start(f32[2,128,128]{2,1,0:T(8,128)} %lower_inverse.1) | copy-start | bytes 393220
  89.8 170.0 %copy-start.2 = (s32[2]{0:T(128)S(1)}, s32[2]{0:T(128)}, u32[]{:S(2)}) copy-start(s32[2]{0:T(128)} %pad_add_fusion.refs_0_.place) | copy-start | bytes 28
  89.9 170.0 %copy-start.3 = (s32[256]{0:T(256)S(1)}, s32[256]{0:T(256)}, u32[]{:S(2)}) copy-start(s32[256]{0:T(256)} %get-tuple-element.10.moved_row) | copy-start | bytes 3076
  89.9 170.0 %copy-start.4 = (s32[256]{0:T(256)S(1)}, s32[256]{0:T(256)}, u32[]{:S(2)}) copy-start(s32[256]{0:T(256)} %get-tuple-element.11.moved_slot) | copy-start | bytes 3076
Sparse Core Ops, SparseCore 0:
  90.0 163.2 all-reduce.1

commit v2 on v1

v2 whole, which is shorter than its diff:
```python
import jax
import jax.numpy as jnp
from jax import lax
from jax.experimental import pallas as pl
from jax.experimental.pallas import tpu as pltpu
from jax.sharding import PartitionSpec as P

NB = 128
PICKS = 2 * NB
SIDE = 4
PLANE = SIDE * SIDE
SHARE = PICKS // PLANE
GROUP = 8
OFFSETS = (0, -1, 1, 2)
HBM = pl.BlockSpec(memory_space=pl.ANY)
SMEM = pl.BlockSpec(memory_space=pltpu.SMEM)
VMEM = pl.BlockSpec(memory_space=pltpu.VMEM)


def chip(z, y, x):
    return (z % SIDE * SIDE + y % SIDE) * SIDE + x % SIDE


def moves(dz, dy, dx):
    span = range(SIDE)
    return [(chip(z, y, x), chip(z + dz, y + dy, x + dx)) for z in span for y in span for x in span]


def owner_of(row):
    return (row >> 7) & (SIDE * PLANE - 1)


def local_of(row):
    return ((row >> 13) << 7) | (row & (NB - 1))


def each(count, body, unroll=8):
    def step(i, carry):
        body(i)
        return carry

    lax.fori_loop(0, count, step, 0, unroll=unroll)


def route_kernel(
    place, pivots, rows_hbm,
    send_hbm, pick_row, hub_source, stats, moved_row, moved_first, moved_second, order_first, order_second,
    source, rank_of, begin, sems,
):
    me = place[0]
    plane_at = me % PLANE
    my_y, my_x = plane_at // SIDE, plane_at % SIDE

    def start(i):
        chosen = pivots[i]
        source[chosen] = chosen

    each(PICKS, start)

    def reset(i):
        source[i] = i

    each(PICKS, reset)

    def exchange(i):
        chosen = pivots[i]
        at_target = source[i]
        at_chosen = source[chosen]
        source[i] = at_chosen
        source[chosen] = at_target

    each(PICKS, exchange, 4)

    def clear(o):
        begin[o] = 0

    each(SIDE * PLANE, clear)

    def count(i):
        owner = owner_of(source[i])
        before = begin[owner]
        rank_of[i] = before
        begin[owner] = before + 1

    each(PICKS, count, 4)

    def prefix(o, carry):
        total, most = carry
        held = begin[o]
        begin[o] = total
        return total + held, jnp.maximum(most, held)

    _, most = lax.fori_loop(0, SIDE * PLANE, prefix, (0, 0), unroll=4)
    stats[0] = most
    mine = begin[me]

    def deal(i):
        row = source[i]
        rank = begin[owner_of(row)] + rank_of[i]
        rank_of[i] = rank
        pick_row[rank] = row
        order_first[rank] = i

    each(PICKS, deal, 4)
    last = jnp.where(me == SIDE * PLANE - 1, PICKS, begin[jnp.minimum(me + 1, SIDE * PLANE - 1)])
    sent = jnp.minimum(last - mine, SHARE)

    def copy_of(n, z):
        rank = mine + n
        return pltpu.make_async_copy(
            rows_hbm.at[local_of(pick_row[rank])],
            send_hbm.at[z * PLANE + rank % PLANE],
            sems.at[n * SIDE + z],
        )

    def send(n, carry):
        for z in range(SIDE):
            copy_of(n, z).start()
        return carry

    lax.fori_loop(0, sent, send, 0)

    def hub(t):
        hub_source[t] = owner_of(pick_row[t * PLANE + plane_at])

    each(SHARE, hub)

    def list_moved(i, found):
        chosen = pivots[i]
        is_mine = jnp.logical_and(owner_of(chosen) == me, chosen >= PICKS)

        @pl.when(is_mine)
        def _():
            previous = source[chosen]
            kept = previous % NB
            x = previous // NB + 2 * (kept % 32 // SHARE)
            y = kept // 32
            dx, dy = (x - my_x) % SIDE, (y - my_y) % SIDE
            at_x = jnp.where(dx == 3, 1, jnp.where(dx == 0, 0, dx + 1))
            at_y = jnp.where(dy == 3, 1, jnp.where(dy == 0, 0, dy + 1))
            moved_row[found] = local_of(chosen)
            moved_first[found] = (at_y * SIDE + at_x) * 2 * SHARE + SHARE + kept % SHARE
            moved_second[found] = (at_x * SIDE + at_y) * 2 * SHARE + SHARE + kept % SHARE

        return found + is_mine.astype(jnp.int32)

    stats[1] = lax.fori_loop(0, PICKS, list_moved, 0, unroll=4)

    def tag(i):
        rank_of[order_first[i]] = i

    def keep(i):
        order_second[i] = order_first[i]

    each(PICKS, keep)

    def name_first(t):
        for a, dy in enumerate(OFFSETS):
            for b, dx in enumerate(OFFSETS):
                column = (my_y + dy) % SIDE * SIDE + (my_x + dx) % SIDE
                order_first[(a * SIDE + b) * SHARE + t] = order_second[t * PLANE + column]

    each(SHARE, name_first, 1)

    def finish(n, carry):
        for z in range(SIDE):
            copy_of(n, z).wait()
        return carry

    lax.fori_loop(0, sent, finish, 0)


def route(place, pivots, rows):
    table = jax.ShapeDtypeStruct((PICKS,), jnp.int32)
    small = jax.ShapeDtypeStruct((SHARE,), jnp.int32)
    chips = SIDE * PLANE
    return pl.pallas_call(
        route_kernel,
        out_shape=(
            jax.ShapeDtypeStruct((chips,) + rows.shape[1:], rows.dtype), table, small, small,
            table, table, table, table, table,
        ),
        in_specs=[SMEM, SMEM, HBM],
        out_specs=(HBM,) + (SMEM,) * 8,
        scratch_shapes=[
            pltpu.SMEM((rows.shape[0] * chips,), jnp.int32),
            pltpu.SMEM((PICKS,), jnp.int32),
            pltpu.SMEM((chips,), jnp.int32),
            pltpu.SemaphoreType.DMA((SHARE * SIDE,)),
        ],
        cost_estimate=pl.CostEstimate(flops=0, transcendentals=0, bytes_accessed=30_000_000),
        name="route",
    )(place, pivots, rows)


def round_kernel(at, place, pick_row, rows_hbm, send_hbm, sems):
    me = place[0]

    def copy_of(h, z):
        row = pick_row[at[0] * PLANE + h]
        copy = pltpu.make_async_copy(
            rows_hbm.at[local_of(row)], send_hbm.at[z * PLANE + h], sems.at[h * SIDE + z]
        )
        return owner_of(row) == me, copy

    def go(h):
        for z in range(SIDE):
            held, copy = copy_of(h, z)
            pl.when(held)(copy.start)

    each(PLANE, go, 1)

    def finish(h):
        for z in range(SIDE):
            held, copy = copy_of(h, z)
            pl.when(held)(copy.wait)

    each(PLANE, finish, 1)


def send_round(at, place, pick_row, rows):
    return pl.pallas_call(
        round_kernel,
        out_shape=jax.ShapeDtypeStruct((SIDE * PLANE,) + rows.shape[1:], rows.dtype),
        in_specs=[SMEM, SMEM, SMEM, HBM],
        out_specs=HBM,
        scratch_shapes=[pltpu.SemaphoreType.DMA((PLANE * SIDE,))],
        name="send_round",
    )(at, place, pick_row, rows)


def swap_all(rows):
    return lax.all_to_all(rows, "prow", 0, 0, tiled=True)


def crowded(place, pick_row, hub_source, rows, received):
    def step(t, held):
        sent = send_round(jnp.full((1,), t, jnp.int32), place, pick_row, rows)
        row = lax.dynamic_slice_in_dim(swap_all(sent), hub_source[t], 1, axis=0)
        return lax.dynamic_update_slice_in_dim(held, row, t, axis=0)

    held = lax.fori_loop(0, SHARE, step, jnp.zeros_like(received))
    return held, jnp.arange(SHARE, dtype=jnp.int32)


def pack_kernel(place, index, received, own, first, second, third, left, right, buffer, sems, out_sems):
    z = place[0] // PLANE

    def pick(t):
        return pltpu.make_async_copy(received.at[index[t]], buffer.at[t], sems.at[t])

    each(SHARE, lambda t: pick(t).start())
    for level, held in enumerate((own, first, second, third)):

        @pl.when(z == level)
        def _():
            pltpu.make_async_copy(held, buffer.at[pl.ds(SHARE, SHARE)], sems.at[SHARE]).start()

    each(SHARE, lambda t: pick(t).wait())
    pltpu.make_async_copy(own, buffer.at[pl.ds(SHARE, SHARE)], sems.at[SHARE]).wait()
    half = left.shape[1]
    outs = [
        pltpu.make_async_copy(buffer.at[:, pl.ds(n * half, half), :], out, out_sems.at[n])
        for n, out in enumerate((left, right))
    ]
    for out in outs:
        out.start()
    for out in outs:
        out.wait()


def pack(place, index, received, previous):
    blocks, width = received.shape[1:]
    out = jax.ShapeDtypeStruct((2 * SHARE, blocks // 2, width), received.dtype)
    return pl.pallas_call(
        pack_kernel,
        out_shape=(out, out),
        in_specs=[SMEM, SMEM] + [HBM] * 5,
        out_specs=(HBM, HBM),
        scratch_shapes=[
            pltpu.VMEM((2 * SHARE, blocks, width), received.dtype),
            pltpu.SemaphoreType.DMA((SHARE + 1,)),
            pltpu.SemaphoreType.DMA((2,)),
        ],
        name="pack",
    )(place, index, received, *previous)


def permute(value, pairs):
    return lax.ppermute(value, "prow", pairs)


def spread_previous(block, me):
    y, x = me // SIDE % SIDE, me % SIDE
    quarter = 2 * SHARE
    homes = (0, 1)
    parts = [
        permute(block[quarter * n : quarter * (n + 1)], [(h, chip(0, n, h)) for h in homes])
        for n in range(1, SIDE)
    ]
    held = block[:quarter]
    for n, part in enumerate(parts):
        held = jnp.where(y == n + 1, part, held)
    across = permute(
        held[SHARE:], [(chip(0, n, h), chip(0, n, h + 2)) for n in range(SIDE) for h in homes]
    )
    own = jnp.where(x < 2, held[:SHARE], across)
    plane = [(n, n % PLANE) for n in range(PLANE)]
    return [own] + [permute(own, [(n, z * PLANE + n) for n, _ in plane]) for z in range(1, SIDE)]


def along(axis, offset):
    return moves(0, offset, 0) if axis == "y" else moves(0, 0, offset)


def gather_line(value, axis):
    pieces = [permute(value, along(axis, -offset)) for offset in OFFSETS[1:]]
    return jnp.concatenate([value] + pieces, axis=0)


def gather_plane(value, axis, other):
    line = gather_line(value, axis)
    before = permute(line, along(other, 1))
    after = permute(line, along(other, -1))
    half = line.shape[0] // 2
    far_low = permute(before[:half], along(other, 1))
    far_high = permute(after[half:], along(other, -1))
    return [line, before, after, far_low, far_high]


def dot(left, right):
    return jnp.dot(left, right, precision=lax.Precision.HIGHEST, preferred_element_type=jnp.float32)


def single(left, right):
    return jnp.dot(left, right, preferred_element_type=jnp.float32)


def halves(value):
    high = value.astype(jnp.bfloat16)
    return high, (value - high.astype(jnp.float32)).astype(jnp.bfloat16)


def update_kernel(*refs):
    place, stats, moved_row, moved_first, moved_second = refs[:5]
    panel, slot_panel, order_first, order_second, upper_inverse, lower_inverse = refs[5:11]
    rows_hbm, pieces, out_hbm = refs[11], (refs[12:17], refs[17:22]), refs[22]
    rows, plane, result, own_panel, weights, row_sems, piece_sems, out_sems = refs[23:]
    grid_row, grid_column = place[0], place[1]
    groups, local_rows = rows.shape[:2]
    per_half = groups // 2

    def fetch_rows(group):
        columns = pl.ds(group * GROUP, GROUP)
        return pltpu.make_async_copy(rows_hbm.at[:, columns, :], rows.at[group], row_sems.at[group])

    def fetch_piece(side, n):
        piece = pieces[side][n]
        begin = (0, 8 * SHARE, 16 * SHARE, 24 * SHARE, 28 * SHARE)[n]
        target = plane.at[side, pl.ds(begin, piece.shape[0])]
        return pltpu.make_async_copy(piece, target, piece_sems.at[side, n])

    for side in range(2):
        for n in range(5):
            fetch_piece(side, n).start()
        for group in range(side * per_half, (side + 1) * per_half):
            fetch_rows(group).start()

    own_panel[...] = panel[...]

    def patch_panel(i, carry):
        for side in range(2):
            own_panel[side, pl.ds(moved_row[i], 1), :] = slot_panel[side, pl.ds(moved_first[i], 1), :]
        return carry

    lax.fori_loop(0, stats[1], patch_panel, 0)

    def one_hot(order):
        return lax.broadcasted_iota(jnp.int32, (PICKS, PICKS), 0) == order[...]

    place_first = one_hot(order_first)
    row_at = lax.broadcasted_iota(jnp.int32, (NB, NB), 0)
    column_at = lax.broadcasted_iota(jnp.int32, (NB, NB), 1)
    upper = [jnp.where(row_at <= column_at, upper_inverse[k], 0.0) for k in range(2)]
    lower = [
        jnp.where(row_at > column_at, lower_inverse[k], jnp.where(row_at == column_at, 1.0, 0.0))
        for k in range(2)
    ]
    dealt = [
        jnp.concatenate([slot_panel[k, 2 * SHARE * n : 2 * SHARE * n + SHARE, :] for n in range(PLANE)], axis=0)
        for k in range(2)
    ]
    picked = dot(place_first.astype(jnp.float32), jnp.concatenate(dealt, axis=1))
    block_lower = dot(picked[NB:, :NB], upper[0])
    block_upper = dot(lower[0], picked[:NB, NB:])
    block_second = picked[NB:, NB:] - dot(block_lower, block_upper)
    mixed = -dot(lower[1], dot(block_lower, lower[0]))
    lower_first = dot(own_panel[0], upper[0])
    lower_second = dot(own_panel[1] - dot(lower_first, block_upper), upper[1])
    weight_first = dot(lower_first, lower[0]) + dot(lower_second, mixed)
    weight_second = dot(lower_second, lower[1])
    first_home, second_home = grid_row == 0, grid_row == 1
    is_home = grid_row < 2

    def at_home(first, second, other):
        top = jnp.where(first_home, first, jnp.where(second_home, second, other[:NB]))
        return jnp.concatenate([top, other[NB:]], axis=0)

    weight = jnp.concatenate(
        [
            at_home(-lower[0], -mixed, weight_first),
            at_home(jnp.zeros_like(lower[1]), -lower[1], weight_second),
        ],
        axis=1,
    )
    high, low = halves(weight)
    for side, hot in enumerate((place_first, one_hot(order_second))):
        hot = hot.astype(jnp.bfloat16)
        weights[2 * side] = single(high, hot).astype(jnp.bfloat16)
        weights[2 * side + 1] = single(low, hot).astype(jnp.bfloat16)
    head = jnp.where(
        grid_column == 0,
        at_home(picked[:NB, :NB], block_lower, lower_first),
        at_home(block_upper, block_second, lower_second),
    )

    def write(group, slot):
        return pltpu.make_async_copy(
            result.at[slot], out_hbm.at[:, pl.ds(group * GROUP, GROUP), :], out_sems.at[slot]
        )

    for group in range(groups):
        slot, side = group % 2, group // per_half
        begin = group % per_half * GROUP
        if group % per_half == 0:
            for n in range(5):
                fetch_piece(side, n).wait()
        fetch_rows(group).wait()
        moved = (moved_first, moved_second)[side]

        def patch(i, carry):
            rows[group, moved_row[i], :, :] = plane[side, moved[i], begin : begin + GROUP, :]
            return carry

        lax.fori_loop(0, stats[1], patch, 0)
        if group >= 2:
            write(group - 2, slot).wait()
        for pair in range(GROUP // 2):
            columns = [2 * pair, 2 * pair + 1]
            right = [
                jnp.concatenate(
                    [plane[side, 2 * SHARE * n : 2 * SHARE * n + SHARE, begin + c, :] for n in range(PLANE)],
                    axis=0,
                )
                for c in columns
            ]
            right_high, right_low = halves(jnp.concatenate(right, axis=1))
            product = single(weights[2 * side], right_high)
            product += single(weights[2 * side], right_low)
            product += single(weights[2 * side + 1], right_high)
            for n, c in enumerate(columns):
                own = rows[group, :, c, :]
                top = jnp.where(is_home, 0.0, own[:NB])
                own = jnp.concatenate([top, own[NB:]], axis=0)
                value = own - product[:, n * NB : (n + 1) * NB]
                if group == 0 and c == 0:
                    value = head
                result[slot, :, c, :] = value
        write(group, slot).start()
    for group in range(max(0, groups - 2), groups):
        write(group, group % 2).wait()


def update(tables, panel, slot_panel, orders, upper_inverse, lower_inverse, rows, pieces):
    local_rows, blocks, _ = rows.shape
    groups = blocks // GROUP
    orders = [order.reshape(1, PICKS) for order in orders]
    return pl.pallas_call(
        update_kernel,
        out_shape=jax.ShapeDtypeStruct(rows.shape, rows.dtype),
        in_specs=[SMEM] * 5 + [VMEM] * 6 + [HBM] * 11,
        out_specs=HBM,
        scratch_shapes=[
            pltpu.VMEM((groups, local_rows, GROUP, NB), jnp.float32),
            pltpu.VMEM((2, 2 * PICKS, blocks // 2, NB), jnp.float32),
            pltpu.VMEM((2, local_rows, GROUP, NB), jnp.float32),
            pltpu.VMEM((2, local_rows, NB), jnp.float32),
            pltpu.VMEM((4, local_rows, PICKS), jnp.bfloat16),
            pltpu.SemaphoreType.DMA((groups,)),
            pltpu.SemaphoreType.DMA((2, 5)),
            pltpu.SemaphoreType.DMA((2,)),
        ],
        compiler_params=pltpu.CompilerParams(vmem_limit_bytes=48 << 20),
        cost_estimate=pl.CostEstimate(flops=3_300_000_000, transcendentals=0, bytes_accessed=26_000_000),
        name="update",
    )(*tables, panel, slot_panel, *orders, upper_inverse, lower_inverse, rows, *pieces[0], *pieces[1])


def local(matrix, pivots, upper_inverse, lower_inverse):
    me = lax.axis_index("prow")
    rows = matrix.reshape(matrix.shape[0] * NB, matrix.shape[3], NB)
    place = jnp.stack([me, lax.axis_index("pcol")]).astype(jnp.int32)
    previous = spread_previous(rows[:NB], me)
    panel = lax.all_gather(rows[:, 0, :], "pcol", axis=0)
    sent, pick_row, hub_source, stats, moved_row, moved_first, moved_second, order_first, order = route(
        place, pivots.reshape(-1), rows
    )
    received = swap_all(sent)
    received, index = lax.cond(
        stats[0] <= SHARE,
        lambda: (received, hub_source),
        lambda: crowded(place, pick_row, hub_source, rows, received),
    )
    left, right = pack(place, index, received, previous)
    pieces = gather_plane(left, "x", "y"), gather_plane(right, "y", "x")
    order_second = order_first.reshape(SIDE, SIDE, SHARE).swapaxes(0, 1)
    heads = jnp.concatenate([piece[:, 0, :] for piece in pieces[0]], axis=0)
    slot_panel = lax.all_gather(heads, "pcol", axis=0)
    out = update(
        (place, stats, moved_row, moved_first, moved_second),
        panel, slot_panel, (order_first, order_second), upper_inverse, lower_inverse, rows, pieces,
    )
    return out.reshape(matrix.shape)


def solution(mesh):
    return jax.shard_map(
        local,
        mesh=mesh,
        in_specs=(P(None, "prow", None, None, "pcol", None), P(), P(), P()),
        out_specs=P(None, "prow", None, None, "pcol", None),
        check_vma=False,
    )
```

time: 289 us -> 158 us (0.55)
  waiting for transfers between devices: 158 us -> 31.5 us
  Pallas kernels: 101 us -> 40.2 us
  starting transfers between devices: 0.01 us -> 47.8 us
  between operations: 13.5 us -> 1.2 us
  local copies, waits for them, and re-layouts: 8.01 us -> 19.4 us
  blocking collectives: 8.01 us -> 15.1 us
    psum x1 -> x0, waiting for transfers between devices: 158 us -> none  [local(): slots = lax.psum(slots, 'prow')]
    pallas_call x1 -> x2, Pallas kernels: 78.2 us -> 20.9 us  [the longest x1 18.1 us: route(): pl.pallas_call(route_kernel, out_shape=(jax.ShapeDtypeStruct((chips,) + r...]
    ppermute x0 -> x21, starting transfers between devices: none -> 33.7 us  [permute(): return lax.ppermute(value, 'prow', pairs)]
    ppermute x0 -> x21, waiting for transfers between devices: none -> 31.5 us  [permute(): return lax.ppermute(value, 'prow', pairs)]
    all_to_all x0 -> x1, starting transfers between devices: none -> 14.1 us  [swap_all(): return lax.all_to_all(rows, 'prow', 0, 0, tiled=True)]
    unnamed x10 -> x33, local copies, waits for them, and re-layouts: 0.03 us -> 6.16 us
    broadcast_in_dim x1 -> x0, local copies, waits for them, and re-layouts: 4.47 us -> none  [route(): jnp.zeros(slots.shape, slots.dtype)]
    all_gather x1, blocking collectives: 3.23 us -> 6.92 us  [local(): panel = lax.all_gather(rows[:, 0, :], 'pcol', axis=0)]
  transfers between devices with their start and end apart: 1 -> 22, of which waited for: 1 -> 7; matrix products, arithmetic and copies ran while one was open for 1% -> 10% of each run, Pallas kernels for 0% -> 12%
where the time goes in v2:
time: 158 us; the launch traced here: 157 us
  starting transfers between devices  47.8 us (30%)
  Pallas kernels  40.2 us (25%)
  waiting for transfers between devices  31.5 us (20%)
  local copies, waits for them, and re-layouts  19.4 us (12%)
  blocking collectives  15.1 us (10%)
    ppermute x21, starting transfers between devices, permute(): return lax.ppermute(value, 'prow', pairs)  33.7 us
    ppermute x21, waiting for transfers between devices, permute(): return lax.ppermute(value, 'prow', pairs)  31.5 us
    pallas_call x1, Pallas kernels, update(): pl.pallas_call(update_kernel, out_shape=jax.ShapeDtypeStruct(rows.shape,...  19.3 us
    pallas_call x1, Pallas kernels, route(): pl.pallas_call(route_kernel, out_shape=(jax.ShapeDtypeStruct((chips,) + r...  18.1 us
    all_to_all x1, starting transfers between devices, swap_all(): return lax.all_to_all(rows, 'prow', 0, 0, tiled=True)  14.1 us
    all_gather x1, blocking collectives, local(): slot_panel = lax.all_gather(heads, 'pcol', axis=0)  8.21 us
    all_gather x1, blocking collectives, local(): panel = lax.all_gather(rows[:, 0, :], 'pcol', axis=0)  6.92 us
    unnamed x33, local copies, waits for them, and re-layouts  6.16 us
  transfers between devices with their start and end apart: 22, of which 7 were waited for; matrix products, arithmetic and copies ran while one was open for 10% of the time, Pallas kernels for 12%

profile of v2, /device:TPU:1, one launch (start us, length us, event | category | flops | bytes accessed | tf_op | source)
XLA Modules:
  0.0 156.7 jit_solution(3332226330042094378)
XLA Ops:
  0.0 2.3 %slice_bitcast_fusion.1 = (f32[32,32,128]{2,1,0:T(8,128)}, f32[32,32,128]{2,1,0:T(8,128)S(1)}, f32[32,32,128]{2,1,0:T(8,128)S(1)}) fusion(f32[4,1,128,32,1,128]{5,3,2,4,1,0:T(8,128)} %bitcast.52), kind=kLoop, calls=%fused_computation.5 | loop fusion | bytes 3145728 | tf_op jit(solution)/shard_map/slice | solution.py:298
  2.3 4.0 %collective-permute-start.2 = (f32[32,32,128]{2,1,0:T(8,128)}, f32[32,32,128]{2,1,0:T(8,128)S(1)}, u32[]{:S(2)}, u32[]{:S(2)}) collective-permute-start(f32[32,32,128]{2,1,0:T(8,128)} %get-tuple-element.160), channel_id=1, source_target_pairs={{0,8},{2,10},{1,9},{3,11}} | collective-permute-start | bytes 1572872 | tf_op jit(solution)/shard_map/ppermute | solution.py:290
  6.3 2.3 %collective-permute-start.1 = (f32[32,32,128]{2,1,0:T(8,128)S(1)}, f32[32,32,128]{2,1,0:T(8,128)S(1)}, u32[]{:S(2)}, u32[]{:S(2)}) collective-permute-start(f32[32,32,128]{2,1,0:T(8,128)S(1)} %get-tuple-element.161), channel_id=1, source_target_pairs={{0,16},{2,18},{1,17},{3,19}} | collective-permute-start | bytes 1572872 | tf_op jit(solution)/shard_map/ppermute | solution.py:290
  8.7 2.1 %collective-permute-start = (f32[32,32,128]{2,1,0:T(8,128)S(1)}, f32[32,32,128]{2,1,0:T(8,128)}, u32[]{:S(2)}, u32[]{:S(2)}) collective-permute-start(f32[32,32,128]{2,1,0:T(8,128)S(1)} %get-tuple-element.162), channel_id=1, source_target_pairs={{0,24},{2,26},{1,25},{3,27}} | collective-permute-start | bytes 1572872 | tf_op jit(solution)/shard_map/ppermute | solution.py:290
  10.8 18.1 %route.1 = (f32[64,32,128]{2,1,0:T(8,128)}, s32[256]{0:T(256)S(1)}, s32[16]{0:T(128)S(1)}, s32[16]{0:T(128)}, s32[256]{0:T(256)}, /*index=5*/s32[256]{0:T(256)}, s32[256]{0:T(256)}, s32[256]{0:T(256)}, s32[256]{0:T(256)}) custom-call(s32[2]{0:T(128)S(1)} %pad_add_fusion.place.refs_0_, s32[256]{0:T(256)} %bitcast.61, f32[512,32,128]{2,1,0:T(8,128)} %bitcast.53), custom_call_target="tpu_custom_call" | custom-call | bytes 30000000 | tf_op jit(solution)/shard_map/route/pallas_call | solution.py:177
  28.9 14.1 %all-to-all-start.1 = ((f32[64,32,128]{2,1,0:T(8,128)}), f32[64,32,128]{2,1,0:T(8,128)S(1)}, u32[]{:S(2)}, u32[]{:S(2)}) async-start(f32[64,32,128]{2,1,0:T(8,128)} %get-tuple-element.142), calls=%async_computation.1 | async-start | bytes 2097152 | tf_op jit(solution)/shard_map/all_to_all | solution.py:233
  43.1 1.3 fusion.2
  44.4 4.4 %collective-permute-start.3 = (f32[16,32,128]{2,1,0:T(8,128)S(1)}, f32[16,32,128]{2,1,0:T(8,128)S(1)}, u32[]{:S(2)}, u32[]{:S(2)}) collective-permute-start(f32[16,32,128]{2,1,0:T(8,128)S(1)} %slice.96), channel_id=1, source_target_pairs={{0,4},{2,6},{8,12},{10,14},{16,20},{18,22},{24,28},{26,30},{1,5},{... | collective-permute-start | bytes 786440 | tf_op jit(solution)/shard_map/ppermute | solution.py:290
  48.8 10.1 %collective-permute-done.3 = f32[16,32,128]{2,1,0:T(8,128)S(1)} collective-permute-done((f32[16,32,128]{2,1,0:T(8,128)S(1)}, f32[16,32,128]{2,1,0:T(8,128)S(1)}, u32[]{:S(2)}, u32[]{:S(2)}) %collective-permute-start.3) | collective-permute-done | bytes 262176 | tf_op jit(solution)/shard_map/ppermute | solution.py:290
  59.0 1.3 collective-permute-start.6
  60.3 1.3 collective-permute-start.5
  61.6 1.3 collective-permute-start.4
  64.6 1.3 collective-permute-done.5.second
  65.9 5.6 %collective-permute-done.4.first = f32[16,32,128]{2,1,0:T(8,128)S(1)} collective-permute-done((f32[16,32,128]{2,1,0:T(8,128)S(1)}, f32[16,32,128]{2,1,0:T(8,128)S(1)}, u32[]{:S(2)}, u32[]{:S(2)}) %collective-permute-start.4) | collective-permute-done | bytes 262176 | tf_op jit(solution)/shard_map/ppermute | solution.py:290
  72.3 2.9 %pack.1 = (f32[32,16,128]{2,1,0:T(8,128)}, f32[32,16,128]{2,1,0:T(8,128)}) custom-call(s32[2]{0:T(128)S(1)} %pad_add_fusion.place.refs_0_, s32[16]{0:T(128)S(1)} %get-tuple-element.143.index, f32[64,32,128]{2,1,0:T(8,128)S(1)} %get-tuple-element.144.received, f32[16,32,128]{2,1,0:T(8,128)} %copy-done.8, f32[16,32,128]{2,1,0:T(8,128)} %copy-done.11, ...), custom_call_target="tpu_custom_call" | custom-call | tf_op jit(solution)/shard_map/pack/pallas_call | solution.py:275
  75.2 1.8 %fusion.6 = (f32[32,16,128]{2,0,1:T(8,128)S(1)}, f32[128,16,128]{2,0,1:T(8,128)}) fusion(f32[32,16,128]{2,1,0:T(8,128)} %get-tuple-element.145), kind=kLoop, calls=%fused_computation.26 | loop fusion | bytes 786432 | tf_op jit(solution)/shard_map/pack/pallas_call | solution.py:275
  77.5 3.1 %collective-permute-start.8 = (f32[32,16,128]{2,0,1:T(8,128)S(1)}, f32[32,16,128]{2,0,1:T(8,128)S(1)}, u32[]{:S(2)}, u32[]{:S(2)}) collective-permute-start(f32[32,16,128]{2,0,1:T(8,128)S(1)} %get-tuple-element.163), channel_id=1, source_target_pairs={{0,6},{2,0},{4,2},{6,4},{8,14},{10,8},{12,10},{14,12},{16,22},{18,... | collective-permute-start | bytes 786440 | tf_op jit(solution)/shard_map/ppermute | solution.py:290
  80.6 2.7 %collective-permute-start.16 = (f32[32,16,128]{2,1,0:T(8,128)}, f32[32,16,128]{2,1,0:T(8,128)S(1)}, u32[]{:S(2)}, u32[]{:S(2)}) collective-permute-start(f32[32,16,128]{2,1,0:T(8,128)} %get-tuple-element.147), channel_id=1, source_target_pairs={{0,16},{2,18},{4,20},{6,22},{8,24},{10,26},{12,28},{14,30},{16,0},... | collective-permute-start | bytes 786440 | tf_op jit(solution)/shard_map/ppermute | solution.py:290
  84.2 1.2 collective-permute-start.9
  85.4 1.7 %constant_dynamic-update-slice_fusion.9 = f32[128,16,128]{2,1,0:T(8,128)} fusion(f32[32,16,128]{2,1,0:T(8,128)} %get-tuple-element.147), kind=kLoop, calls=%fused_computation.24 | loop fusion | bytes 524288
  89.1 2.5 %collective-permute-done.9 = f32[32,16,128]{2,0,1:T(8,128)S(1)} collective-permute-done((f32[32,16,128]{2,0,1:T(8,128)S(1)}, f32[32,16,128]{2,0,1:T(8,128)S(1)}, u32[]{:S(2)}, u32[]{:S(2)}) %collective-permute-start.9) | collective-permute-done | bytes 262176 | tf_op jit(solution)/shard_map/ppermute | solution.py:290
  92.4 1.8 %copy.40.refs_12_ = f32[128,16,128]{2,1,0:T(8,128)S(1)} copy(f32[128,16,128]{2,0,1:T(8,128)} %constant_dynamic-update-slice_fusion) | data formatting | bytes 2097152 | tf_op jit(solution)/shard_map/concatenate | solution.py:318
  95.2 1.8 %collective-permute-start.11 = (f32[128,16,128]{2,1,0:T(8,128)S(1)}, f32[128,16,128]{2,1,0:T(8,128)S(1)}, u32[]{:S(2)}, u32[]{:S(2)}) collective-permute-start(f32[128,16,128]{2,1,0:T(8,128)S(1)} %copy.40.refs_12_), channel_id=1, source_target_pairs={{0,24},{2,26},{4,28},{6,30},{8,0},{10,2},{12,4},{14,6},{16,8},{18,... | collective-permute-start | bytes 3145736 | tf_op jit(solution)/shard_map/ppermute | solution.py:290
  99.1 1.1 collective-permute-start.18
  100.6 2.4 %slice.90 = f32[512,1,128]{2,1,0:T(1,128)} slice(f32[512,32,128]{2,1,0:T(8,128)} %bitcast.56), slice={[0:512], [0:1], [0:128]} | slice | bytes 524288 | tf_op jit(solution)/shard_map/slice | solution.py:504
  103.2 6.9 %all-gather = f32[1024,1,128]{2,1,0:T(1,128)S(1)} all-gather(f32[512,1,128]{2,1,0:T(1,128)} %slice.90), channel_id=2, replica_groups=mesh['prow'=64,'pcol'=2] {'pcol'}, dimensions={0}, use_global_device_ids=true | all-gather | bytes 786432 | tf_op jit(solution)/shard_map/all_gather | solution.py:504
  110.1 7.8 %collective-permute-done.11.refs_14_ = f32[128,16,128]{2,1,0:T(8,128)S(1)} collective-permute-done((f32[128,16,128]{2,1,0:T(8,128)S(1)}, f32[128,16,128]{2,1,0:T(8,128)S(1)}, u32[]{:S(2)}, u32[]{:S(2)}) %collective-permute-start.11) | collective-permute-done | bytes 1048608 | tf_op jit(solution)/shard_map/ppermute | solution.py:290
  122.6 1.1 slice.104
  123.6 1.1 collective-permute-start.19
  125.4 3.2 %collective-permute-done.13.refs_16_ = f32[64,16,128]{2,1,0:T(8,128)S(1)} collective-permute-done((f32[64,16,128]{2,1,0:T(8,128)S(1)}, f32[64,16,128]{2,1,0:T(8,128)S(1)}, u32[]{:S(2)}, u32[]{:S(2)}) %collective-permute-start.13) | collective-permute-done | bytes 524320 | tf_op jit(solution)/shard_map/ppermute | solution.py:290
  129.0 8.2 %all-gather.1 = f32[1024,128]{1,0:T(8,128)S(1)} all-gather(f32[512,128]{1,0:T(8,128)S(1)} %constant_dynamic-update-slice_fusion.4), channel_id=3, replica_groups=mesh['prow'=64,'pcol'=2] {'pcol'}, dimensions={0}, use_global_device_ids=true | all-gather | bytes 786432 | tf_op jit(solution)/shard_map/all_gather | solution.py:518
  137.2 19.3 %update.1 = f32[512,32,128]{2,1,0:T(8,128)} custom-call(s32[2]{0:T(128)S(1)} %pad_add_fusion.place.refs_0_, s32[16]{0:T(128)S(1)} %copy-done.6, s32[256]{0:T(256)S(1)} %copy-done.3, s32[256]{0:T(256)S(1)} %copy-done.4, s32[256]{0:T(256)S(1)} %copy-done.5, f32[2,512,128]{2,1,0:T(8,128)S(1)} %bitcast.48, f32[2,512,128]{2,1,0:T(8,128)S(1)} %bitcast.49, ...), custom_call_target="tpu_custom_call" | custom-call | flops 3300000000 | bytes 26000000 | tf_op jit(solution)/shard_map/update/pallas_call | solution.py:478
  (75 shorter events, 15.4 us)
Async XLA Ops:
  2.3 40.8 %collective-permute-start.2 = (f32[32,32,128]{2,1,0:T(8,128)}, f32[32,32,128]{2,1,0:T(8,128)S(1)}, u32[]{:S(2)}, u32[]{:S(2)}) collective-permute-start(f32[32,32,128]{2,1,0:T(8,128)} %get-tuple-element.160), channel_id=1, source_target_pairs={{0,8},{2,10},{1,9},{3,11}} | collective-permute-start | bytes 1572872 | tf_op jit(solution)/shard_map/ppermute | solution.py:290
  6.3 36.7 %collective-permute-start.1 = (f32[32,32,128]{2,1,0:T(8,128)S(1)}, f32[32,32,128]{2,1,0:T(8,128)S(1)}, u32[]{:S(2)}, u32[]{:S(2)}) collective-permute-start(f32[32,32,128]{2,1,0:T(8,128)S(1)} %get-tuple-element.161), channel_id=1, source_target_pairs={{0,16},{2,18},{1,17},{3,19}} | collective-permute-start | bytes 1572872 | tf_op jit(solution)/shard_map/ppermute | solution.py:290
  8.7 34.4 %collective-permute-start = (f32[32,32,128]{2,1,0:T(8,128)S(1)}, f32[32,32,128]{2,1,0:T(8,128)}, u32[]{:S(2)}, u32[]{:S(2)}) collective-permute-start(f32[32,32,128]{2,1,0:T(8,128)S(1)} %get-tuple-element.162), channel_id=1, source_target_pairs={{0,24},{2,26},{1,25},{3,27}} | collective-permute-start | bytes 1572872 | tf_op jit(solution)/shard_map/ppermute | solution.py:290
  28.9 34.7 %all-to-all-start.1 = ((f32[64,32,128]{2,1,0:T(8,128)}), f32[64,32,128]{2,1,0:T(8,128)S(1)}, u32[]{:S(2)}, u32[]{:S(2)}) async-start(f32[64,32,128]{2,1,0:T(8,128)} %get-tuple-element.142), calls=%async_computation.1 | async-start | bytes 2097152 | tf_op jit(solution)/shard_map/all_to_all | solution.py:233
  44.4 14.6 %collective-permute-start.3 = (f32[16,32,128]{2,1,0:T(8,128)S(1)}, f32[16,32,128]{2,1,0:T(8,128)S(1)}, u32[]{:S(2)}, u32[]{:S(2)}) collective-permute-start(f32[16,32,128]{2,1,0:T(8,128)S(1)} %slice.96), channel_id=1, source_target_pairs={{0,4},{2,6},{8,12},{10,14},{16,20},{18,22},{24,28},{26,30},{1,5},{... | collective-permute-start | bytes 786440 | tf_op jit(solution)/shard_map/ppermute | solution.py:290
  59.0 5.6 %collective-permute-start.6 = (f32[16,32,128]{2,1,0:T(8,128)S(1)}, f32[16,32,128]{2,1,0:T(8,128)S(1)}, u32[]{:S(2)}, u32[]{:S(2)}) collective-permute-start(f32[16,32,128]{2,1,0:T(8,128)S(1)} %slice_select_fusion.own), channel_id=1, source_target_pairs={{0,96},{2,98},{4,100},{6,102},{8,104},{10,106},{12,108},{14,110},{... | collective-permute-start | bytes 786440 | tf_op jit(solution)/shard_map/ppermute | solution.py:290
  60.3 5.6 %collective-permute-start.5 = (f32[16,32,128]{2,1,0:T(8,128)S(1)}, f32[16,32,128]{2,1,0:T(8,128)S(1)}, u32[]{:S(2)}, u32[]{:S(2)}) collective-permute-start(f32[16,32,128]{2,1,0:T(8,128)S(1)} %slice_select_fusion.own), channel_id=1, source_target_pairs={{0,64},{2,66},{4,68},{6,70},{8,72},{10,74},{12,76},{14,78},{16,80}... | collective-permute-start | bytes 786440 | tf_op jit(solution)/shard_map/ppermute | solution.py:290
  61.6 9.9 %collective-permute-start.4 = (f32[16,32,128]{2,1,0:T(8,128)S(1)}, f32[16,32,128]{2,1,0:T(8,128)S(1)}, u32[]{:S(2)}, u32[]{:S(2)}) collective-permute-start(f32[16,32,128]{2,1,0:T(8,128)S(1)} %slice_select_fusion.own), channel_id=1, source_target_pairs={{0,32},{2,34},{4,36},{6,38},{8,40},{10,42},{12,44},{14,46},{16,48}... | collective-permute-start | bytes 786440 | tf_op jit(solution)/shard_map/ppermute | solution.py:290
  63.7 39.3 %copy-start.2 = (s32[256]{0:T(256)S(1)}, s32[256]{0:T(256)}, u32[]{:S(2)}) copy-start(s32[256]{0:T(256)} %get-tuple-element.146) | copy-start | bytes 3076
  64.6 6.9 %copy-start.9 = (f32[16,32,128]{2,1,0:T(8,128)}, f32[16,32,128]{2,1,0:T(8,128)S(1)}, u32[]{:S(2)}) copy-start(f32[16,32,128]{2,1,0:T(8,128)S(1)} %collective-permute-done.6.third) | copy-start | bytes 786436
  65.9 5.6 %copy-start.10 = (f32[16,32,128]{2,1,0:T(8,128)}, f32[16,32,128]{2,1,0:T(8,128)S(1)}, u32[]{:S(2)}) copy-start(f32[16,32,128]{2,1,0:T(8,128)S(1)} %collective-permute-done.5.second) | copy-start | bytes 786436
  75.1 62.1 %copy-start = (f32[2,128,128]{2,1,0:T(8,128)S(1)}, f32[2,128,128]{2,1,0:T(8,128)}, u32[]{:S(2)}) copy-start(f32[2,128,128]{2,1,0:T(8,128)} %refs_9_.1) | copy-start | bytes 393220
  75.1 62.1 %copy-start.1 = (f32[2,128,128]{2,1,0:T(8,128)S(1)}, f32[2,128,128]{2,1,0:T(8,128)}, u32[]{:S(2)}) copy-start(f32[2,128,128]{2,1,0:T(8,128)} %refs_10_.1) | copy-start | bytes 393220
  75.2 62.1 %copy-start.3 = (s32[256]{0:T(256)S(1)}, s32[256]{0:T(256)}, u32[]{:S(2)}) copy-start(s32[256]{0:T(256)} %get-tuple-element.137.refs_2_) | copy-start | bytes 3076
  75.2 62.1 %copy-start.4 = (s32[256]{0:T(256)S(1)}, s32[256]{0:T(256)}, u32[]{:S(2)}) copy-start(s32[256]{0:T(256)} %get-tuple-element.138.refs_3_) | copy-start | bytes 3076
  75.2 62.1 %copy-start.5 = (s32[256]{0:T(256)S(1)}, s32[256]{0:T(256)}, u32[]{:S(2)}) copy-start(s32[256]{0:T(256)} %get-tuple-element.139.refs_4_) | copy-start | bytes 3076
  75.2 62.1 %copy-start.6 = (s32[16]{0:T(128)S(1)}, s32[16]{0:T(128)}, u32[]{:S(2)}) copy-start(s32[16]{0:T(128)} %get-tuple-element.136.refs_1_) | copy-start | bytes 196
  77.0 10.1 %collective-permute-start.7 = (f32[32,16,128]{2,0,1:T(8,128)S(1)}, f32[32,16,128]{2,0,1:T(8,128)S(1)}, u32[]{:S(2)}, u32[]{:S(2)}) collective-permute-start(f32[32,16,128]{2,0,1:T(8,128)S(1)} %get-tuple-element.163), channel_id=1, source_target_pairs={{0,2},{2,4},{4,6},{6,0},{8,10},{10,12},{12,14},{14,8},{16,18},{18,... | collective-permute-start | bytes 786440 | tf_op jit(solution)/shard_map/ppermute | solution.py:290
  77.5 10.9 %collective-permute-start.8 = (f32[32,16,128]{2,0,1:T(8,128)S(1)}, f32[32,16,128]{2,0,1:T(8,128)S(1)}, u32[]{:S(2)}, u32[]{:S(2)}) collective-permute-start(f32[32,16,128]{2,0,1:T(8,128)S(1)} %get-tuple-element.163), channel_id=1, source_target_pairs={{0,6},{2,0},{4,2},{6,4},{8,14},{10,8},{12,10},{14,12},{16,22},{18,... | collective-permute-start | bytes 786440 | tf_op jit(solution)/shard_map/ppermute | solution.py:290
  80.6 17.7 %collective-permute-start.16 = (f32[32,16,128]{2,1,0:T(8,128)}, f32[32,16,128]{2,1,0:T(8,128)S(1)}, u32[]{:S(2)}, u32[]{:S(2)}) collective-permute-start(f32[32,16,128]{2,1,0:T(8,128)} %get-tuple-element.147), channel_id=1, source_target_pairs={{0,16},{2,18},{4,20},{6,22},{8,24},{10,26},{12,28},{14,30},{16,0},... | collective-permute-start | bytes 786440 | tf_op jit(solution)/shard_map/ppermute | solution.py:290
  83.3 14.3 %collective-permute-start.15 = (f32[32,16,128]{2,1,0:T(8,128)}, f32[32,16,128]{2,1,0:T(8,128)S(1)}, u32[]{:S(2)}, u32[]{:S(2)}) collective-permute-start(f32[32,16,128]{2,1,0:T(8,128)} %get-tuple-element.147), channel_id=1, source_target_pairs={{0,24},{2,26},{4,28},{6,30},{8,0},{10,2},{12,4},{14,6},{16,8},{18,... | collective-permute-start | bytes 786440 | tf_op jit(solution)/shard_map/ppermute | solution.py:290
  84.2 7.4 %collective-permute-start.9 = (f32[32,16,128]{2,0,1:T(8,128)S(1)}, f32[32,16,128]{2,0,1:T(8,128)S(1)}, u32[]{:S(2)}, u32[]{:S(2)}) collective-permute-start(f32[32,16,128]{2,0,1:T(8,128)S(1)} %get-tuple-element.163), channel_id=1, source_target_pairs={{0,4},{2,6},{4,0},{6,2},{8,12},{10,14},{12,8},{14,10},{16,20},{18,... | collective-permute-start | bytes 786440 | tf_op jit(solution)/shard_map/ppermute | solution.py:290
  87.1 9.9 %collective-permute-start.14 = (f32[32,16,128]{2,1,0:T(8,128)}, f32[32,16,128]{2,1,0:T(8,128)S(1)}, u32[]{:S(2)}, u32[]{:S(2)}) collective-permute-start(f32[32,16,128]{2,1,0:T(8,128)} %get-tuple-element.147), channel_id=1, source_target_pairs={{0,8},{2,10},{4,12},{6,14},{8,16},{10,18},{12,20},{14,22},{16,24},... | collective-permute-start | bytes 786440 | tf_op jit(solution)/shard_map/ppermute | solution.py:290
  94.2 24.8 %collective-permute-start.10 = (f32[128,16,128]{2,0,1:T(8,128)}, f32[128,16,128]{2,0,1:T(8,128)S(1)}, u32[]{:S(2)}, u32[]{:S(2)}) collective-permute-start(f32[128,16,128]{2,0,1:T(8,128)} %constant_dynamic-update-slice_fusion), channel_id=1, source_target_pairs={{0,8},{2,10},{4,12},{6,14},{8,16},{10,18},{12,20},{14,22},{16,24},... | collective-permute-start | bytes 3145736 | tf_op jit(solution)/shard_map/ppermute | solution.py:290
  95.2 22.8 %collective-permute-start.11 = (f32[128,16,128]{2,1,0:T(8,128)S(1)}, f32[128,16,128]{2,1,0:T(8,128)S(1)}, u32[]{:S(2)}, u32[]{:S(2)}) collective-permute-start(f32[128,16,128]{2,1,0:T(8,128)S(1)} %copy.40.refs_12_), channel_id=1, source_target_pairs={{0,24},{2,26},{4,28},{6,30},{8,0},{10,2},{12,4},{14,6},{16,8},{18,... | collective-permute-start | bytes 3145736 | tf_op jit(solution)/shard_map/ppermute | solution.py:290
  99.1 21.7 %collective-permute-start.18 = (f32[128,16,128]{2,1,0:T(8,128)}, f32[128,16,128]{2,1,0:T(8,128)}, u32[]{:S(2)}, u32[]{:S(2)}) collective-permute-start(f32[128,16,128]{2,1,0:T(8,128)} %constant_dynamic-update-slice_fusion.6.refs_17_), channel_id=1, source_target_pairs={{0,6},{2,0},{4,2},{6,4},{8,14},{10,8},{12,10},{14,12},{16,22},{18,... | collective-permute-start | bytes 3145736 | tf_op jit(solution)/shard_map/ppermute | solution.py:290
  100.2 22.3 %collective-permute-start.17 = (f32[128,16,128]{2,1,0:T(8,128)}, f32[128,16,128]{2,1,0:T(8,128)}, u32[]{:S(2)}, u32[]{:S(2)}) collective-permute-start(f32[128,16,128]{2,1,0:T(8,128)} %constant_dynamic-update-slice_fusion.6.refs_17_), channel_id=1, source_target_pairs={{0,2},{2,4},{4,6},{6,0},{8,10},{10,12},{12,14},{14,8},{16,18},{18,... | collective-permute-start | bytes 3145736 | tf_op jit(solution)/shard_map/ppermute | solution.py:290
  117.9 19.3 %copy-start.7 = (f32[128,16,128]{2,1,0:T(8,128)}, f32[128,16,128]{2,1,0:T(8,128)S(1)}, u32[]{:S(2)}) copy-start(f32[128,16,128]{2,1,0:T(8,128)S(1)} %collective-permute-done.11.refs_14_) | copy-start | bytes 3145732
  118.0 10.6 %collective-permute-start.13 = (f32[64,16,128]{2,1,0:T(8,128)S(1)}, f32[64,16,128]{2,1,0:T(8,128)S(1)}, u32[]{:S(2)}, u32[]{:S(2)}) collective-permute-start(f32[64,16,128]{2,1,0:T(8,128)S(1)} %slice.102), channel_id=1, source_target_pairs={{0,24},{2,26},{4,28},{6,30},{8,0},{10,2},{12,4},{14,6},{16,8},{18,... | collective-permute-start | bytes 1572872 | tf_op jit(solution)/shard_map/ppermute | solution.py:290
  119.0 9.6 %collective-permute-start.12 = (f32[64,16,128]{2,0,1:T(8,128)S(1)}, f32[64,16,128]{2,0,1:T(8,128)S(1)}, u32[]{:S(2)}, u32[]{:S(2)}) collective-permute-start(f32[64,16,128]{2,0,1:T(8,128)S(1)} %slice.100), channel_id=1, source_target_pairs={{0,8},{2,10},{4,12},{6,14},{8,16},{10,18},{12,20},{14,22},{16,24},... | collective-permute-start | bytes 1572872 | tf_op jit(solution)/shard_map/ppermute | solution.py:290
  121.8 15.3 %collective-permute-start.20 = (f32[64,16,128]{2,1,0:T(8,128)S(1)}, f32[64,16,128]{2,1,0:T(8,128)S(1)}, u32[]{:S(2)}, u32[]{:S(2)}) collective-permute-start(f32[64,16,128]{2,1,0:T(8,128)S(1)} %slice.105), channel_id=1, source_target_pairs={{0,6},{2,0},{4,2},{6,4},{8,14},{10,8},{12,10},{14,12},{16,22},{18,... | collective-permute-start | bytes 1572872 | tf_op jit(solution)/shard_map/ppermute | solution.py:290
  123.6 13.5 %collective-permute-start.19 = (f32[64,16,128]{2,1,0:T(8,128)S(1)}, f32[64,16,128]{2,1,0:T(8,128)S(1)}, u32[]{:S(2)}, u32[]{:S(2)}) collective-permute-start(f32[64,16,128]{2,1,0:T(8,128)S(1)} %slice.104), channel_id=1, source_target_pairs={{0,2},{2,4},{4,6},{6,0},{8,10},{10,12},{12,14},{14,8},{16,18},{18,... | collective-permute-start | bytes 1572872 | tf_op jit(solution)/shard_map/ppermute | solution.py:290
  (2 other events, 5.3 us)

commit v3 on v2

v3 whole, which is shorter than its diff:
```python
import jax
import jax.numpy as jnp
from jax import lax
from jax.experimental import pallas as pl
from jax.experimental.pallas import tpu as pltpu
from jax.sharding import PartitionSpec as P

NB = 128
PICKS = 2 * NB
SIDE = 4
PLANE = SIDE * SIDE
SHARE = PICKS // PLANE
QUARTER = NB // SIDE
GROUP = 8
OFFSETS = (0, -1, 1, 2)
HBM = pl.BlockSpec(memory_space=pl.ANY)
SMEM = pl.BlockSpec(memory_space=pltpu.SMEM)
VMEM = pl.BlockSpec(memory_space=pltpu.VMEM)
SMALL = pltpu.CompilerParams(vmem_limit_bytes=4 << 20)


def chip(z, y, x):
    return (z % SIDE * SIDE + y % SIDE) * SIDE + x % SIDE


def moves(dz, dy, dx):
    span = range(SIDE)
    return [(chip(z, y, x), chip(z + dz, y + dy, x + dx)) for z in span for y in span for x in span]


def owner_of(row):
    return (row >> 7) & (SIDE * PLANE - 1)


def local_of(row):
    return ((row >> 13) << 7) | (row & (NB - 1))


def each(count, body, unroll=8):
    def step(i, carry):
        body(i)
        return carry

    lax.fori_loop(0, count, step, 0, unroll=unroll)


def exchange_kernel(pivots, picked, kept, source):
    def start(i):
        chosen = pivots[i]
        source[chosen] = chosen
        source[i] = i

    each(PICKS, start)

    def exchange(i):
        chosen = pivots[i]
        at_target = source[i]
        at_chosen = source[chosen]
        source[i] = at_chosen
        source[chosen] = at_target

    each(PICKS, exchange)

    def keep(i):
        picked[i] = source[i]
        kept[i] = source[pivots[i]]

    each(PICKS, keep)


def exchange(pivots, row_count):
    table = jax.ShapeDtypeStruct((PICKS,), jnp.int32)
    return pl.pallas_call(
        exchange_kernel,
        out_shape=(table, table),
        in_specs=[SMEM],
        out_specs=(SMEM, SMEM),
        scratch_shapes=[pltpu.SMEM((row_count,), jnp.int32)],
        cost_estimate=pl.CostEstimate(flops=0, transcendentals=0, bytes_accessed=60_000_000),
        compiler_params=SMALL,
        name="exchange",
    )(pivots)


def ranks_of(picked):
    owner = owner_of(picked)
    earlier = owner[None, :] < owner[:, None]
    same = owner[None, :] == owner[:, None]
    index = jnp.arange(PICKS)
    ahead = jnp.logical_or(earlier, jnp.logical_and(same, index[None, :] < index[:, None]))
    rank = jnp.sum(ahead.astype(jnp.int32), axis=1)
    return rank, jnp.max(jnp.sum(same.astype(jnp.int32), axis=1))


def deal_kernel(
    place, picked, rank, rows_hbm, send_hbm, pick_row, hub_source, own, held, held_sems, sems
):
    me = place[0]

    def note(i, count):
        row = picked[i]
        pick_row[rank[i]] = row
        own[count] = i
        return count + (owner_of(row) == me).astype(jnp.int32)

    count = jnp.minimum(lax.fori_loop(0, PICKS, note, 0, unroll=16), SHARE)

    def fetch(n):
        return pltpu.make_async_copy(rows_hbm.at[local_of(picked[own[n]])], held.at[n], held_sems.at[n])

    def copy_of(n, z):
        column = rank[own[n]] % PLANE
        return pltpu.make_async_copy(held.at[n], send_hbm.at[z * PLANE + column], sems.at[n * SIDE + z])

    def loop(body):
        def step(n, carry):
            body(n)
            return carry

        lax.fori_loop(0, count, step, 0)

    def send(n):
        fetch(n).wait()
        for z in range(SIDE):
            copy_of(n, z).start()

    def finish(n):
        for z in range(SIDE):
            copy_of(n, z).wait()

    def hub(t):
        hub_source[t] = owner_of(pick_row[t * PLANE + me % PLANE])

    loop(lambda n: fetch(n).start())
    each(SHARE, hub, 16)
    loop(send)
    loop(finish)


def deal(place, picked, rank, rows):
    chips = SIDE * PLANE
    return pl.pallas_call(
        deal_kernel,
        out_shape=(
            jax.ShapeDtypeStruct((chips,) + rows.shape[1:], rows.dtype),
            jax.ShapeDtypeStruct((PICKS,), jnp.int32),
            jax.ShapeDtypeStruct((SHARE,), jnp.int32),
        ),
        in_specs=[SMEM, SMEM, SMEM, HBM],
        out_specs=(HBM, SMEM, SMEM),
        scratch_shapes=[
            pltpu.SMEM((PICKS + 1,), jnp.int32),
            pltpu.VMEM((SHARE,) + rows.shape[1:], rows.dtype),
            pltpu.SemaphoreType.DMA((SHARE,)),
            pltpu.SemaphoreType.DMA((SHARE * SIDE,)),
        ],
        cost_estimate=pl.CostEstimate(flops=0, transcendentals=0, bytes_accessed=30_000_000),
        compiler_params=SMALL,
        name="deal",
    )(place, picked, rank, rows)


def table_kernel(place, pivots, kept, rank, moved, orders, order):
    me = place[0]
    my_y, my_x = me // SIDE % SIDE, me % SIDE

    def invert(i):
        order[rank[i]] = i

    each(PICKS, invert, 16)

    def at_offset(there, here):
        apart = (there - here) % SIDE
        return jnp.where(apart == 3, 1, jnp.where(apart == 0, 0, apart + 1))

    def list_moved(i, count):
        chosen = pivots[i]
        moved[count] = i
        is_mine = jnp.logical_and(owner_of(chosen) == me, chosen >= PICKS)
        return count + is_mine.astype(jnp.int32)

    count = lax.fori_loop(0, PICKS, list_moved, 0, unroll=16)
    moved[4 * PICKS] = count

    def name_moved(n, carry):
        i = moved[n]
        home, held = kept[i] // NB, kept[i] % NB
        x, y, t = home + 2 * (held % QUARTER // SHARE), held // QUARTER, held % SHARE
        at_x, at_y = at_offset(x, my_x), at_offset(y, my_y)
        moved[n] = local_of(pivots[i])
        moved[PICKS + n] = (at_y * SIDE + at_x) * SHARE + t
        moved[2 * PICKS + n] = (at_x * SIDE + at_y) * SHARE + t
        moved[3 * PICKS + n] = (y * SIDE + x) * 2 * SHARE + SHARE + t
        return carry

    lax.fori_loop(0, count, name_moved, 0)

    for a, dy in enumerate(OFFSETS):
        for b, dx in enumerate(OFFSETS):
            column = (my_y + dy) % SIDE * SIDE + (my_x + dx) % SIDE
            for t in range(SHARE):
                pick = order[t * PLANE + column]
                orders[(a * SIDE + b) * SHARE + t] = pick
                orders[PICKS + (b * SIDE + a) * SHARE + t] = pick
                orders[2 * PICKS + column * SHARE + t] = pick


def tables(place, pivots, kept, rank):
    return pl.pallas_call(
        table_kernel,
        out_shape=[jax.ShapeDtypeStruct((n,), jnp.int32) for n in (4 * PICKS + 1, 3 * PICKS)],
        in_specs=[SMEM] * 4,
        out_specs=[SMEM] * 2,
        scratch_shapes=[pltpu.SMEM((PICKS,), jnp.int32)],
        cost_estimate=pl.CostEstimate(flops=0, transcendentals=0, bytes_accessed=20_000_000),
        compiler_params=SMALL,
        name="tables",
    )(place, pivots, kept, rank)


def round_kernel(at, place, pick_row, rows_hbm, send_hbm, sems):
    me = place[0]

    def copy_of(h, z):
        row = pick_row[at[0] * PLANE + h]
        copy = pltpu.make_async_copy(
            rows_hbm.at[local_of(row)], send_hbm.at[z * PLANE + h], sems.at[h * SIDE + z]
        )
        return owner_of(row) == me, copy

    def go(h):
        for z in range(SIDE):
            held, copy = copy_of(h, z)
            pl.when(held)(copy.start)

    each(PLANE, go, 1)

    def finish(h):
        for z in range(SIDE):
            held, copy = copy_of(h, z)
            pl.when(held)(copy.wait)

    each(PLANE, finish, 1)


def send_round(at, place, pick_row, rows):
    return pl.pallas_call(
        round_kernel,
        out_shape=jax.ShapeDtypeStruct((SIDE * PLANE,) + rows.shape[1:], rows.dtype),
        in_specs=[SMEM, SMEM, SMEM, HBM],
        out_specs=HBM,
        scratch_shapes=[pltpu.SemaphoreType.DMA((PLANE * SIDE,))],
        compiler_params=SMALL,
        name="send_round",
    )(at, place, pick_row, rows)


def swap_all(rows):
    return lax.all_to_all(rows, "prow", 0, 0, tiled=True)


def crowded(place, pick_row, hub_source, rows, received):
    def step(t, held):
        sent = send_round(jnp.full((1,), t, jnp.int32), place, pick_row, rows)
        row = lax.dynamic_slice_in_dim(swap_all(sent), hub_source[t], 1, axis=0)
        return lax.dynamic_update_slice_in_dim(held, row, t, axis=0)

    held = lax.fori_loop(0, SHARE, step, jnp.zeros_like(received))
    return held, jnp.arange(SHARE, dtype=jnp.int32)


def pack_kernel(place, index, received, *refs):
    copies, left, right, heads, buffer, edge, sems, out_sems = refs[:SIDE], *refs[SIDE:]
    z = place[0] // PLANE

    def pick(t):
        return pltpu.make_async_copy(received.at[index[t]], buffer.at[t], sems.at[t])

    def previous(held):
        return pltpu.make_async_copy(held, buffer.at[pl.ds(SHARE, SHARE)], sems.at[SHARE])

    each(SHARE, lambda t: pick(t).start())
    for level, held in enumerate(copies):
        pl.when(z == level)(lambda held=held: previous(held).start())
    each(SHARE, lambda t: pick(t).wait())
    previous(copies[0]).wait()
    edge[...] = buffer[:, 0, :]
    half = left.shape[1]
    outs = [
        pltpu.make_async_copy(buffer.at[:, pl.ds(n * half, half), :], out, out_sems.at[n])
        for n, out in enumerate((left, right))
    ]
    outs += [
        pltpu.make_async_copy(edge, heads.at[pl.ds(n * 2 * SHARE, 2 * SHARE)], out_sems.at[2 + n])
        for n in range(PLANE)
    ]
    for out in outs:
        out.start()
    for out in outs:
        out.wait()


def pack(place, index, received, copies):
    blocks, width = received.shape[1:]
    half = jax.ShapeDtypeStruct((2 * SHARE, blocks // 2, width), received.dtype)
    return pl.pallas_call(
        pack_kernel,
        out_shape=(half, half, jax.ShapeDtypeStruct((PLANE * 2 * SHARE, width), received.dtype)),
        in_specs=[SMEM, SMEM] + [HBM] * (1 + SIDE),
        out_specs=(HBM,) * 3,
        scratch_shapes=[
            pltpu.VMEM((2 * SHARE, blocks, width), received.dtype),
            pltpu.VMEM((2 * SHARE, width), received.dtype),
            pltpu.SemaphoreType.DMA((SHARE + 1,)),
            pltpu.SemaphoreType.DMA((2 + PLANE,)),
        ],
        compiler_params=SMALL,
        name="pack",
    )(place, index, received, *copies)


def permute(value, pairs):
    return lax.ppermute(value, "prow", pairs)


def along(axis, offset):
    return moves(0, offset, 0) if axis == "y" else moves(0, 0, offset)


def leave_home(block, me):
    held = block[:QUARTER]
    y = me // SIDE % SIDE
    parts = [
        permute(block[QUARTER * n : QUARTER * (n + 1)], [(h, chip(0, n, h)) for h in range(2)])
        for n in range(1, SIDE)
    ]
    for n, part in enumerate(parts):
        held = jnp.where(y == n + 1, part, held)
    return held


def climb(held, me):
    across = permute(held[SHARE:], [(chip(0, n, h), chip(0, n, h + 2)) for n in range(SIDE) for h in range(2)])
    own = jnp.where(me % SIDE < 2, held[:SHARE], across)
    return [own] + [permute(own, [(n, z * PLANE + n) for n in range(PLANE)]) for z in range(1, SIDE)]


def gather_line(value, axis):
    return jnp.concatenate([value] + [permute(value, along(axis, -offset)) for offset in OFFSETS[1:]], axis=0)


def neighbours(line, axis):
    return permute(line, along(axis, 1)), permute(line, along(axis, -1))


def gather_across(line, hops, axis):
    before, after = hops
    half = line.shape[0] // 2
    far_low, far_high = permute(before[:half], along(axis, 1)), permute(after[half:], along(axis, -1))
    return [line, before, after, far_low, far_high]


def dot(left, right):
    return jnp.dot(left, right, precision=lax.Precision.HIGHEST, preferred_element_type=jnp.float32)


def single(left, right):
    return jnp.dot(left, right, preferred_element_type=jnp.float32)


def halves(value):
    high = value.astype(jnp.bfloat16)
    return high, (value - high.astype(jnp.float32)).astype(jnp.bfloat16)


def weigh_kernel(
    place, moved, panel, head, orders, upper_inverse, lower_inverse,
    weights_hbm, edge_hbm, own_panel, weights, edge, sems,
):
    grid_row, grid_column = place[0], place[1]
    own_panel[...] = panel[...]

    def patch(i, carry):
        for side in range(2):
            own_panel[side, pl.ds(moved[i], 1), :] = head[side, pl.ds(moved[3 * PICKS + i], 1), :]
        return carry

    lax.fori_loop(0, moved[4 * PICKS], patch, 0)

    hot = [
        lax.broadcasted_iota(jnp.int32, (PICKS, PICKS), 0) == orders[n : n + 1, :] for n in range(3)
    ]
    row_at = lax.broadcasted_iota(jnp.int32, (NB, NB), 0)
    column_at = lax.broadcasted_iota(jnp.int32, (NB, NB), 1)
    upper = [jnp.where(row_at <= column_at, upper_inverse[k], 0.0) for k in range(2)]
    lower = [
        jnp.where(row_at > column_at, lower_inverse[k], jnp.where(row_at == column_at, 1.0, 0.0))
        for k in range(2)
    ]
    dealt = [
        jnp.concatenate([head[k, 2 * SHARE * n : 2 * SHARE * n + SHARE, :] for n in range(PLANE)], axis=0)
        for k in range(2)
    ]
    picked = dot(hot[2].astype(jnp.float32), jnp.concatenate(dealt, axis=1))
    block_lower = dot(picked[NB:, :NB], upper[0])
    block_upper = dot(lower[0], picked[:NB, NB:])
    block_second = picked[NB:, NB:] - dot(block_lower, block_upper)
    mixed = -dot(lower[1], dot(block_lower, lower[0]))
    lower_first = dot(own_panel[0], upper[0])
    lower_second = dot(own_panel[1] - dot(lower_first, block_upper), upper[1])
    weight_first = dot(lower_first, lower[0]) + dot(lower_second, mixed)
    weight_second = dot(lower_second, lower[1])
    first_home, second_home = grid_row == 0, grid_row == 1

    def at_home(first, second, other):
        top = jnp.where(first_home, first, jnp.where(second_home, second, other[:NB]))
        return jnp.concatenate([top, other[NB:]], axis=0)

    weight = jnp.concatenate(
        [
            at_home(-lower[0], -mixed, weight_first),
            at_home(jnp.zeros_like(lower[1]), -lower[1], weight_second),
        ],
        axis=1,
    )
    high, low = halves(weight)
    for side in range(2):
        place_at = hot[side].astype(jnp.bfloat16)
        weights[2 * side] = single(high, place_at).astype(jnp.bfloat16)
        weights[2 * side + 1] = single(low, place_at).astype(jnp.bfloat16)
    edge[...] = jnp.where(
        grid_column == 0,
        at_home(picked[:NB, :NB], block_lower, lower_first),
        at_home(block_upper, block_second, lower_second),
    )
    outs = [
        pltpu.make_async_copy(weights, weights_hbm, sems.at[0]),
        pltpu.make_async_copy(edge, edge_hbm, sems.at[1]),
    ]
    for out in outs:
        out.start()
    for out in outs:
        out.wait()


def weigh(place, moved, panel, head, orders, upper_inverse, lower_inverse):
    local_rows = panel.shape[1]
    return pl.pallas_call(
        weigh_kernel,
        out_shape=(
            jax.ShapeDtypeStruct((4, local_rows, PICKS), jnp.bfloat16),
            jax.ShapeDtypeStruct((local_rows, NB), jnp.float32),
        ),
        in_specs=[SMEM] * 2 + [VMEM] * 5,
        out_specs=(HBM, HBM),
        scratch_shapes=[
            pltpu.VMEM((2, local_rows, NB), jnp.float32),
            pltpu.VMEM((4, local_rows, PICKS), jnp.bfloat16),
            pltpu.VMEM((local_rows, NB), jnp.float32),
            pltpu.SemaphoreType.DMA((2,)),
        ],
        compiler_params=pltpu.CompilerParams(vmem_limit_bytes=24 << 20),
        cost_estimate=pl.CostEstimate(flops=1_200_000_000, transcendentals=0, bytes_accessed=20_000_000),
        name="weigh",
    )(place, moved, panel, head, orders.reshape(3, PICKS), upper_inverse, lower_inverse)


def update_kernel(*refs):
    place, moved, weights_hbm, edge_hbm, rows_hbm = refs[:5]
    pieces, out_hbm = (refs[5:10], refs[10:15]), refs[15]
    rows, plane, kept, result, weights, edge = refs[16:22]
    row_sems, piece_sems, kept_sems, out_sems, weight_sems = refs[22:]
    groups, half = rows.shape[0], plane.shape[3]
    is_home = place[0] < 2
    found = moved[4 * PICKS]
    begins = (0, 4, 8, 12, 14, 16)

    def fetch_rows(group):
        columns = pl.ds(group * GROUP, GROUP)
        return pltpu.make_async_copy(rows_hbm.at[:, columns, :], rows.at[group], row_sems.at[group])

    def fetch_piece(side, n):
        source = pieces[side][n].at[:, pl.ds(0, SHARE)]
        target = plane.at[side, pl.ds(begins[n], begins[n + 1] - begins[n])]
        return pltpu.make_async_copy(source, target, piece_sems.at[side, n])

    def kept_half(i, side, source):
        return pltpu.make_async_copy(source, kept.at[side, i], kept_sems.at[side, i])

    def start_kept(i, carry):
        for side in range(2):
            at = moved[(1 + side) * PICKS + i]
            there = at // SHARE
            for n, piece in enumerate(pieces[side]):

                @pl.when(jnp.logical_and(there >= begins[n], there < begins[n + 1]))
                def _():
                    chunk = jnp.clip(there - begins[n], 0, begins[n + 1] - begins[n] - 1)
                    kept_half(i, side, piece.at[chunk, SHARE + at % SHARE]).start()

        return carry

    def wait_kept(i, carry):
        for side in range(2):
            kept_half(i, side, pieces[side][0].at[0, 0]).wait()
        return carry

    def write(group, slot):
        return pltpu.make_async_copy(
            result.at[slot], out_hbm.at[:, pl.ds(group * GROUP, GROUP), :], out_sems.at[slot]
        )

    factors = [
        pltpu.make_async_copy(weights_hbm, weights, weight_sems.at[0]),
        pltpu.make_async_copy(edge_hbm, edge, weight_sems.at[1]),
    ]
    for factor in factors:
        factor.start()
    for side in range(2):
        for n in range(5):
            fetch_piece(side, n).start()
        for group in range(side * groups // 2, (side + 1) * groups // 2):
            fetch_rows(group).start()
        if side == 0:
            lax.fori_loop(0, found, start_kept, 0)

    for group in range(groups):
        slot, side = group % 2, group * GROUP // half
        begin = group * GROUP % half
        if begin == 0:
            for n in range(5):
                fetch_piece(side, n).wait()
        if group == 0:
            lax.fori_loop(0, found, wait_kept, 0)
            for factor in factors:
                factor.wait()
        fetch_rows(group).wait()

        def patch(i, carry):
            rows[group, moved[i], :, :] = kept[side, i, begin : begin + GROUP, :]
            return carry

        lax.fori_loop(0, found, patch, 0)
        if group >= 2:
            write(group - 2, slot).wait()
        picked = plane[side, :, :, begin : begin + GROUP, :].reshape(PICKS, GROUP, NB)
        picked = pltpu.einshape("rcl->crl", picked)
        products = []
        for pair in range(GROUP // 2):
            right_high, right_low = halves(jnp.concatenate([picked[2 * pair], picked[2 * pair + 1]], axis=1))
            product = single(weights[2 * side], right_high)
            product += single(weights[2 * side], right_low)
            product += single(weights[2 * side + 1], right_high)
            products += [product[:, :NB], product[:, NB:]]
        product = pltpu.einshape("crl->rcl", jnp.stack(products, axis=0))
        result[slot, :NB] = jnp.where(is_home, 0.0, rows[group, :NB]) - product[:NB]
        result[slot, NB:] = rows[group, NB:] - product[NB:]
        if group == 0:
            result[slot, :, 0, :] = edge[...]
        write(group, slot).start()
    for group in range(max(0, groups - 2), groups):
        write(group, group % 2).wait()


def update(place, moved, weights, edge, rows, pieces):
    local_rows, blocks, _ = rows.shape
    groups = blocks // GROUP
    pieces = [piece.reshape((-1, 2 * SHARE) + piece.shape[1:]) for side in pieces for piece in side]
    return pl.pallas_call(
        update_kernel,
        out_shape=jax.ShapeDtypeStruct(rows.shape, rows.dtype),
        in_specs=[SMEM] * 2 + [HBM] * 13,
        out_specs=HBM,
        scratch_shapes=[
            pltpu.VMEM((groups, local_rows, GROUP, NB), jnp.float32),
            pltpu.VMEM((2, PLANE, SHARE, blocks // 2, NB), jnp.float32),
            pltpu.VMEM((2, PICKS, blocks // 2, NB), jnp.float32),
            pltpu.VMEM((2, local_rows, GROUP, NB), jnp.float32),
            pltpu.VMEM((4, local_rows, PICKS), jnp.bfloat16),
            pltpu.VMEM((local_rows, NB), jnp.float32),
            pltpu.SemaphoreType.DMA((groups,)),
            pltpu.SemaphoreType.DMA((2, 5)),
            pltpu.SemaphoreType.DMA((2, PICKS)),
            pltpu.SemaphoreType.DMA((2,)),
            pltpu.SemaphoreType.DMA((2,)),
        ],
        compiler_params=pltpu.CompilerParams(vmem_limit_bytes=56 << 20),
        cost_estimate=pl.CostEstimate(flops=3_300_000_000, transcendentals=0, bytes_accessed=26_000_000),
        name="update",
    )(place, moved, weights, edge, rows, *pieces)


def local(matrix, pivots, upper_inverse, lower_inverse):
    me = lax.axis_index("prow")
    rows = matrix.reshape(matrix.shape[0] * NB, matrix.shape[3], NB)
    place = jnp.stack([me, lax.axis_index("pcol")]).astype(jnp.int32)
    pivots = pivots.reshape(-1)
    panel = lax.all_gather(rows[:, 0, :], "pcol", axis=0)
    held = leave_home(rows[:NB], me)
    picked, kept = exchange(pivots, rows.shape[0] * SIDE * PLANE)
    rank, most = ranks_of(picked)
    sent, pick_row, hub_source = deal(place, picked, rank, rows)
    received = swap_all(sent)
    copies = climb(held, me)
    moved, orders = tables(place, pivots, kept, rank)
    received, index = lax.cond(
        most <= SHARE,
        lambda: (received, hub_source),
        lambda: crowded(place, pick_row, hub_source, rows, received),
    )
    index, orders = lax.optimization_barrier((index, orders))
    left, right, head = pack(place, index, received, copies)
    planes = [list(range(z * PLANE, (z + 1) * PLANE)) for z in range(SIDE)]
    head = lax.all_to_all(head, "prow", 0, 0, tiled=True, axis_index_groups=planes)
    lines = gather_line(left, "x"), gather_line(right, "y")
    hops = neighbours(lines[0], "y"), neighbours(lines[1], "x")
    *hops, head = lax.optimization_barrier((*hops, head))
    head = lax.all_gather(head, "pcol", axis=0)
    pieces = [gather_across(*parts) for parts in zip(lines, hops, "yx")]
    weights, edge = weigh(place, moved, panel, head, orders, upper_inverse, lower_inverse)
    out = update(place, moved, weights, edge, rows, pieces)
    return out.reshape(matrix.shape)


def solution(mesh):
    return jax.shard_map(
        local,
        mesh=mesh,
        in_specs=(P(None, "prow", None, None, "pcol", None), P(), P(), P()),
        out_specs=P(None, "prow", None, None, "pcol", None),
        check_vma=False,
    )
```

time: 158 us -> 146 us (0.924)
  blocking collectives: 15.1 us -> 33.4 us
  waiting for transfers between devices: 31.5 us -> 20.5 us
  local copies, waits for them, and re-layouts: 19.4 us -> 12.3 us
  Pallas kernels: 40.2 us -> 33.5 us
  starting transfers between devices: 47.8 us -> 41.8 us
    all_to_all x0 -> x1, blocking collectives: none -> 24.5 us  [local(): lax.all_to_all(head, 'prow', 0, 0, tiled=True, axis_index_groups=planes)]
    ppermute x21, waiting for transfers between devices: 31.5 us -> 20.5 us  [permute(): return lax.ppermute(value, 'prow', pairs)]
    all_to_all x1, starting transfers between devices: 14.1 us -> 6.38 us  [swap_all(): return lax.all_to_all(rows, 'prow', 0, 0, tiled=True)]
    all_gather x1, blocking collectives: 8.21 us -> 2.17 us  [local(): head = lax.all_gather(head, 'pcol', axis=0)]
    pallas_call x1, Pallas kernels: 19.3 us -> 15.6 us  [update(): pl.pallas_call(update_kernel, out_shape=jax.ShapeDtypeStruct(rows.shape,...]
    concatenate x4 -> x2, local copies, waits for them, and re-layouts: 3.29 us -> 0.04 us  [gather_line(): jnp.concatenate([value] + [permute(value, along(axis, -offset)) for offse...]
    pallas_call x2 -> x5, Pallas kernels: 20.9 us -> 17.9 us  [the longest x1 4.46 us: weigh(): pl.pallas_call(weigh_kernel, out_shape=(jax.ShapeDtypeStruct((4, local_ro...]
    unnamed x33 -> x32, local copies, waits for them, and re-layouts: 6.16 us -> 3.51 us
  transfers between devices with their start and end apart: 22 -> 22, of which waited for: 7 -> 4; matrix products, arithmetic and copies ran while one was open for 10% -> 4% of each run, Pallas kernels for 12% -> 11%
where the time goes in v3:
time: 146 us; the launch traced here: 145 us
  starting transfers between devices  41.8 us (29%)
  Pallas kernels  33.5 us (23%)
  blocking collectives  33.4 us (23%)
  waiting for transfers between devices  20.5 us (14%)
  local copies, waits for them, and re-layouts  12.3 us (8%)
  other arithmetic  2.29 us (2%)
    ppermute x21, starting transfers between devices, permute(): return lax.ppermute(value, 'prow', pairs)  35.4 us
    all_to_all x1, blocking collectives, local(): lax.all_to_all(head, 'prow', 0, 0, tiled=True, axis_index_groups=planes)  24.5 us
    ppermute x21, waiting for transfers between devices, permute(): return lax.ppermute(value, 'prow', pairs)  20.5 us
    pallas_call x1, Pallas kernels, update(): pl.pallas_call(update_kernel, out_shape=jax.ShapeDtypeStruct(rows.shape,...  15.6 us
    all_gather x1, blocking collectives, local(): panel = lax.all_gather(rows[:, 0, :], 'pcol', axis=0)  6.69 us
    all_to_all x1, starting transfers between devices, swap_all(): return lax.all_to_all(rows, 'prow', 0, 0, tiled=True)  6.38 us
    pallas_call x1, Pallas kernels, weigh(): pl.pallas_call(weigh_kernel, out_shape=(jax.ShapeDtypeStruct((4, local_ro...  4.46 us
    pallas_call x1, Pallas kernels, deal(): pl.pallas_call(deal_kernel, out_shape=(jax.ShapeDtypeStruct((chips,) + ro...  4.26 us
  transfers between devices with their start and end apart: 22, of which 4 were waited for; matrix products, arithmetic and copies ran while one was open for 4% of the time, Pallas kernels for 11%

profile of v3, /device:TPU:1, one launch (start us, length us, event | category | flops | bytes accessed | tf_op | source)
XLA Modules:
  0.0 144.9 jit_solution(8420355481966293210)
XLA Ops:
  0.0 2.5 %slice_bitcast_fusion.1 = (f32[32,32,128]{2,1,0:T(8,128)}, f32[32,32,128]{2,1,0:T(8,128)}, f32[32,32,128]{2,1,0:T(8,128)S(1)}) fusion(f32[4,1,128,32,1,128]{5,3,2,4,1,0:T(8,128)} %bitcast.47), kind=kLoop, calls=%fused_computation.5 | loop fusion | bytes 3145728 | tf_op jit(solution)/shard_map/slice | solution.py:334
  2.5 4.0 %collective-permute-start.2 = (f32[32,32,128]{2,1,0:T(8,128)}, f32[32,32,128]{2,1,0:T(8,128)S(1)}, u32[]{:S(2)}, u32[]{:S(2)}) collective-permute-start(f32[32,32,128]{2,1,0:T(8,128)} %get-tuple-element.180), channel_id=1, source_target_pairs={{0,8},{2,10},{1,9},{3,11}} | collective-permute-start | bytes 1572872 | tf_op jit(solution)/shard_map/ppermute | solution.py:323
  6.5 2.3 %collective-permute-start.1 = (f32[32,32,128]{2,1,0:T(8,128)}, f32[32,32,128]{2,1,0:T(8,128)S(1)}, u32[]{:S(2)}, u32[]{:S(2)}) collective-permute-start(f32[32,32,128]{2,1,0:T(8,128)} %get-tuple-element.181), channel_id=1, source_target_pairs={{0,16},{2,18},{1,17},{3,19}} | collective-permute-start | bytes 1572872 | tf_op jit(solution)/shard_map/ppermute | solution.py:323
  8.8 2.1 %collective-permute-start = (f32[32,32,128]{2,1,0:T(8,128)S(1)}, f32[32,32,128]{2,1,0:T(8,128)}, u32[]{:S(2)}, u32[]{:S(2)}) collective-permute-start(f32[32,32,128]{2,1,0:T(8,128)S(1)} %get-tuple-element.182), channel_id=1, source_target_pairs={{0,24},{2,26},{1,25},{3,27}} | collective-permute-start | bytes 1572872 | tf_op jit(solution)/shard_map/ppermute | solution.py:323
  11.6 3.7 %exchange.1 = (s32[256]{0:T(256)S(1)}, s32[256]{0:T(256)S(1)}) custom-call(s32[256]{0:T(256)S(1)} %bitcast.45), custom_call_target="tpu_custom_call" | custom-call | bytes 60000000 | tf_op jit(solution)/shard_map/exchange/pallas_call | solution.py:73
  15.7 4.3 %deal.1 = (f32[64,32,128]{2,1,0:T(8,128)}, s32[256]{0:T(256)S(1)}, s32[16]{0:T(128)S(1)}) custom-call(s32[2]{0:T(128)S(1)} %pad_add_fusion.place.refs_0_, s32[256]{0:T(256)S(1)} %get-tuple-element.146.picked, s32[256]{0:T(256)S(1)} %get-tuple-element.167.rank, f32[512,32,128]{2,1,0:T(8,128)} %bitcast.48), custom_call_target="tpu_custom_call" | custom-call | bytes 30000000 | tf_op jit(solution)/shard_map/deal/pallas_call | solution.py:142
  19.9 6.4 %all-to-all-start.1 = ((f32[64,32,128]{2,1,0:T(8,128)}), f32[64,32,128]{2,1,0:T(8,128)S(1)}, u32[]{:S(2)}, u32[]{:S(2)}) async-start(f32[64,32,128]{2,1,0:T(8,128)} %get-tuple-element.150), calls=%async_computation.1 | async-start | bytes 2097152 | tf_op jit(solution)/shard_map/all_to_all | solution.py:259
  26.4 2.5 %collective-permute-done.1 = f32[32,32,128]{2,1,0:T(8,128)S(1)} collective-permute-done((f32[32,32,128]{2,1,0:T(8,128)}, f32[32,32,128]{2,1,0:T(8,128)S(1)}, u32[]{:S(2)}, u32[]{:S(2)}) %collective-permute-start.1) | collective-permute-done | bytes 524320 | tf_op jit(solution)/shard_map/ppermute | solution.py:323
  28.8 1.3 fusion.2
  30.1 2.0 %collective-permute-start.3 = (f32[16,32,128]{2,1,0:T(8,128)S(1)}, f32[16,32,128]{2,1,0:T(8,128)S(1)}, u32[]{:S(2)}, u32[]{:S(2)}) collective-permute-start(f32[16,32,128]{2,1,0:T(8,128)S(1)} %slice.72), channel_id=1, source_target_pairs={{0,4},{2,6},{8,12},{10,14},{16,20},{18,22},{24,28},{26,30},{1,5},{... | collective-permute-start | bytes 786440 | tf_op jit(solution)/shard_map/ppermute | solution.py:323
  32.2 8.5 %collective-permute-done.3 = f32[16,32,128]{2,1,0:T(8,128)S(1)} collective-permute-done((f32[16,32,128]{2,1,0:T(8,128)S(1)}, f32[16,32,128]{2,1,0:T(8,128)S(1)}, u32[]{:S(2)}, u32[]{:S(2)}) %collective-permute-start.3) | collective-permute-done | bytes 262176 | tf_op jit(solution)/shard_map/ppermute | solution.py:323
  40.6 1.3 collective-permute-start.6
  42.0 1.3 collective-permute-start.5
  43.3 1.3 collective-permute-start.4
  45.9 3.1 %tables.1 = (s32[1025]{0:T(1024)S(1)}, s32[768]{0:T(1024)S(1)}) custom-call(s32[2]{0:T(128)S(1)} %pad_add_fusion.place.refs_0_, s32[256]{0:T(256)S(1)} %bitcast.46, s32[256]{0:T(256)S(1)} %get-tuple-element.145.kept, s32[256]{0:T(256)S(1)} %get-tuple-element.167.rank), custom_call_target="tpu_custom_call" | custom-call | bytes 20000000 | tf_op jit(solution)/shard_map/tables/pallas_call | solution.py:209
  50.1 1.5 %collective-permute-done.4.refs_1_ = f32[16,32,128]{2,1,0:T(8,128)S(1)} collective-permute-done((f32[16,32,128]{2,1,0:T(8,128)S(1)}, f32[16,32,128]{2,1,0:T(8,128)S(1)}, u32[]{:S(2)}, u32[]{:S(2)}) %collective-permute-start.4) | collective-permute-done | bytes 262176 | tf_op jit(solution)/shard_map/ppermute | solution.py:323
  51.5 2.3 %pack.1 = (f32[32,16,128]{2,1,0:T(8,128)S(1)}, f32[32,16,128]{2,1,0:T(8,128)S(1)}, f32[512,128]{1,0:T(8,128)S(1)}) custom-call(s32[2]{0:T(128)S(1)} %pad_add_fusion.place.refs_0_, s32[16]{0:T(128)S(1)} %get-tuple-element.153.index, f32[64,32,128]{2,1,0:T(8,128)} %get-tuple-element.154.received, f32[16,32,128]{2,1,0:T(8,128)S(1)} %slice_select_fusion.refs_0_, ...), custom_call_target="tpu_custom_call" | custom-call | tf_op jit(solution)/shard_map/pack/pallas_call | solution.py:306
  53.8 3.9 %collective-permute-start.12 = (f32[32,16,128]{2,1,0:T(8,128)S(1)}, f32[32,16,128]{2,1,0:T(8,128)S(1)}, u32[]{:S(2)}, u32[]{:S(2)}) collective-permute-start(f32[32,16,128]{2,1,0:T(8,128)S(1)} %get-tuple-element.156), channel_id=1, source_target_pairs={{0,8},{2,10},{4,12},{6,14},{8,16},{10,18},{12,20},{14,22},{16,24},... | collective-permute-start | bytes 786440 | tf_op jit(solution)/shard_map/ppermute | solution.py:323
  57.7 3.7 %collective-permute-start.9 = (f32[32,16,128]{2,1,0:T(8,128)S(1)}, f32[32,16,128]{2,1,0:T(8,128)S(1)}, u32[]{:S(2)}, u32[]{:S(2)}) collective-permute-start(f32[32,16,128]{2,1,0:T(8,128)S(1)} %get-tuple-element.155), channel_id=1, source_target_pairs={{0,4},{2,6},{4,0},{6,2},{8,12},{10,14},{12,8},{14,10},{16,20},{18,... | collective-permute-start | bytes 786440 | tf_op jit(solution)/shard_map/ppermute | solution.py:323
  62.0 2.4 %collective-permute-start.14 = (f32[32,16,128]{2,1,0:T(8,128)S(1)}, f32[32,16,128]{2,1,0:T(8,128)S(1)}, u32[]{:S(2)}, u32[]{:S(2)}) collective-permute-start(f32[32,16,128]{2,1,0:T(8,128)S(1)} %get-tuple-element.156), channel_id=1, source_target_pairs={{0,16},{2,18},{4,20},{6,22},{8,24},{10,26},{12,28},{14,30},{16,0},... | collective-permute-start | bytes 786440 | tf_op jit(solution)/shard_map/ppermute | solution.py:323
  65.5 8.0 %collective-permute-done.13 = f32[32,16,128]{2,1,0:T(8,128)S(1)} collective-permute-done((f32[32,16,128]{2,1,0:T(8,128)S(1)}, f32[32,16,128]{2,1,0:T(8,128)S(1)}, u32[]{:S(2)}, u32[]{:S(2)}) %collective-permute-start.13) | collective-permute-done | bytes 262176 | tf_op jit(solution)/shard_map/ppermute | solution.py:323
  74.1 1.0 collective-permute-start.15
  75.3 3.6 %collective-permute-start.11 = (f32[128,16,128]{2,1,0:T(8,128)S(1)}, f32[128,16,128]{2,1,0:T(8,128)S(1)}, u32[]{:S(2)}, u32[]{:S(2)}) collective-permute-start(f32[128,16,128]{2,1,0:T(8,128)S(1)} %constant_dynamic-update-slice_fusion), channel_id=1, source_target_pairs={{0,24},{2,26},{4,28},{6,30},{8,0},{10,2},{12,4},{14,6},{16,8},{18,... | collective-permute-start | bytes 3145736 | tf_op jit(solution)/shard_map/ppermute | solution.py:323
  78.9 24.5 %all_to_all.27 = f32[16,32,128]{2,1,0:T(8,128)S(1)} all-to-all(f32[16,32,128]{2,1,0:T(8,128)S(1)} %bitcast.44), channel_id=1, replica_groups={{0,2,4,6,8,10,12,14,16,18,20,22,24,26,28,30},{32,34,36,38,40,42,44,46,4..., dimensions={0} | all-to-all | bytes 524288 | tf_op jit(solution)/shard_map/all_to_all | solution.py:614
  104.5 1.1 slice.62
  108.1 2.8 %collective-permute-start.20 = (f32[64,16,128]{2,1,0:T(8,128)}, f32[64,16,128]{2,1,0:T(8,128)}, u32[]{:S(2)}, u32[]{:S(2)}) collective-permute-start(f32[64,16,128]{2,1,0:T(8,128)} %slice.65), channel_id=1, source_target_pairs={{0,6},{2,0},{4,2},{6,4},{8,14},{10,8},{12,10},{14,12},{16,22},{18,... | collective-permute-start | bytes 1572872 | tf_op jit(solution)/shard_map/ppermute | solution.py:323
  110.9 1.5 %collective-permute-start.17 = (f32[64,16,128]{2,1,0:T(8,128)}, f32[64,16,128]{2,1,0:T(8,128)}, u32[]{:S(2)}, u32[]{:S(2)}) collective-permute-start(f32[64,16,128]{2,1,0:T(8,128)} %slice.62), channel_id=1, source_target_pairs={{0,8},{2,10},{4,12},{6,14},{8,16},{10,18},{12,20},{14,22},{16,24},... | collective-permute-start | bytes 1572872 | tf_op jit(solution)/shard_map/ppermute | solution.py:323
  112.4 1.7 %slice.66 = f32[512,1,128]{2,1,0:T(1,128)S(1)} slice(f32[512,32,128]{2,1,0:T(8,128)} %bitcast.51), slice={[0:512], [0:1], [0:128]} | slice | bytes 524288 | tf_op jit(solution)/shard_map/slice | solution.py:598
  114.1 6.7 %all-gather = f32[1024,1,128]{2,1,0:T(1,128)S(1)} all-gather(f32[512,1,128]{2,1,0:T(1,128)S(1)} %slice.66), channel_id=2, replica_groups=mesh['prow'=64,'pcol'=2] {'pcol'}, dimensions={0}, use_global_device_ids=true | all-gather | bytes 786432 | tf_op jit(solution)/shard_map/all_gather | solution.py:598
  120.8 2.2 %all-gather.1 = f32[1024,128]{1,0:T(8,128)S(1)} all-gather(f32[512,128]{1,0:T(8,128)S(1)} %bitcast.59), channel_id=3, replica_groups=mesh['prow'=64,'pcol'=2] {'pcol'}, dimensions={0}, use_global_device_ids=true | all-gather | bytes 786432 | tf_op jit(solution)/shard_map/all_gather | solution.py:618
  123.0 4.5 %weigh.1 = (bf16[4,512,256]{2,1,0:T(8,128)(2,1)S(1)}, f32[512,128]{1,0:T(8,128)S(1)}) custom-call(s32[2]{0:T(128)S(1)} %pad_add_fusion.place.refs_0_, s32[1025]{0:T(1024)S(1)} %get-tuple-element.147.moved.refs_1_, f32[2,512,128]{2,1,0:T(8,128)S(1)} %bitcast.42, f32[2,512,128]{2,1,0:T(8,128)S(1)} %bitcast.43, s32[3,256]{1,0:T(4,128)S(1)} %reshape.53.orders, ...), custom_call_target="tpu_custom_call" | custom-call | flops 1200000000 | bytes 20000000 | tf_op jit(solution)/shard_map/weigh/pallas_call | solution.py:448
  129.2 15.6 %update.1 = f32[512,32,128]{2,1,0:T(8,128)} custom-call(s32[2]{0:T(128)S(1)} %pad_add_fusion.place.refs_0_, s32[1025]{0:T(1024)} %copy-done.2, bf16[4,512,256]{2,1,0:T(8,128)(2,1)} %copy-done, f32[512,128]{1,0:T(8,128)} %copy-done.1, f32[512,32,128]{2,1,0:T(8,128)} %bitcast.52, f32[4,32,16,128]{3,2,1,0:T(8,128)} %bitcast.57, f32[4,32,16,128]{3,2,1,0:T(8,128)} %bitcast.56, ...), custom_call_target="tpu_custom_call" | custom-call | flops 3300000000 | bytes 26000000 | tf_op jit(solution)/shard_map/update/pallas_call | solution.py:569
  (72 shorter events, 11.2 us)
Async XLA Ops:
  0.0 45.9 %copy-start.4 = (s32[2,128]{1,0:T(2,128)S(1)}, s32[2,128]{1,0:T(2,128)}, u32[]{:S(2)}) copy-start(s32[2,128]{1,0:T(2,128)} %param.9) | copy-start | bytes 3076
  2.5 23.9 %collective-permute-start.2 = (f32[32,32,128]{2,1,0:T(8,128)}, f32[32,32,128]{2,1,0:T(8,128)S(1)}, u32[]{:S(2)}, u32[]{:S(2)}) collective-permute-start(f32[32,32,128]{2,1,0:T(8,128)} %get-tuple-element.180), channel_id=1, source_target_pairs={{0,8},{2,10},{1,9},{3,11}} | collective-permute-start | bytes 1572872 | tf_op jit(solution)/shard_map/ppermute | solution.py:323
  6.5 22.3 %collective-permute-start.1 = (f32[32,32,128]{2,1,0:T(8,128)}, f32[32,32,128]{2,1,0:T(8,128)S(1)}, u32[]{:S(2)}, u32[]{:S(2)}) collective-permute-start(f32[32,32,128]{2,1,0:T(8,128)} %get-tuple-element.181), channel_id=1, source_target_pairs={{0,16},{2,18},{1,17},{3,19}} | collective-permute-start | bytes 1572872 | tf_op jit(solution)/shard_map/ppermute | solution.py:323
  8.8 20.0 %collective-permute-start = (f32[32,32,128]{2,1,0:T(8,128)S(1)}, f32[32,32,128]{2,1,0:T(8,128)}, u32[]{:S(2)}, u32[]{:S(2)}) collective-permute-start(f32[32,32,128]{2,1,0:T(8,128)S(1)} %get-tuple-element.182), channel_id=1, source_target_pairs={{0,24},{2,26},{1,25},{3,27}} | collective-permute-start | bytes 1572872 | tf_op jit(solution)/shard_map/ppermute | solution.py:323
  19.9 29.1 %all-to-all-start.1 = ((f32[64,32,128]{2,1,0:T(8,128)}), f32[64,32,128]{2,1,0:T(8,128)S(1)}, u32[]{:S(2)}, u32[]{:S(2)}) async-start(f32[64,32,128]{2,1,0:T(8,128)} %get-tuple-element.150), calls=%async_computation.1 | async-start | bytes 2097152 | tf_op jit(solution)/shard_map/all_to_all | solution.py:259
  30.1 10.5 %collective-permute-start.3 = (f32[16,32,128]{2,1,0:T(8,128)S(1)}, f32[16,32,128]{2,1,0:T(8,128)S(1)}, u32[]{:S(2)}, u32[]{:S(2)}) collective-permute-start(f32[16,32,128]{2,1,0:T(8,128)S(1)} %slice.72), channel_id=1, source_target_pairs={{0,4},{2,6},{8,12},{10,14},{16,20},{18,22},{24,28},{26,30},{1,5},{... | collective-permute-start | bytes 786440 | tf_op jit(solution)/shard_map/ppermute | solution.py:323
  40.6 9.4 %collective-permute-start.6 = (f32[16,32,128]{2,1,0:T(8,128)S(1)}, f32[16,32,128]{2,1,0:T(8,128)S(1)}, u32[]{:S(2)}, u32[]{:S(2)}) collective-permute-start(f32[16,32,128]{2,1,0:T(8,128)S(1)} %slice_select_fusion.refs_0_), channel_id=1, source_target_pairs={{0,96},{2,98},{4,100},{6,102},{8,104},{10,106},{12,108},{14,110},{... | collective-permute-start | bytes 786440 | tf_op jit(solution)/shard_map/ppermute | solution.py:323
  42.0 8.1 %collective-permute-start.5 = (f32[16,32,128]{2,1,0:T(8,128)S(1)}, f32[16,32,128]{2,1,0:T(8,128)S(1)}, u32[]{:S(2)}, u32[]{:S(2)}) collective-permute-start(f32[16,32,128]{2,1,0:T(8,128)S(1)} %slice_select_fusion.refs_0_), channel_id=1, source_target_pairs={{0,64},{2,66},{4,68},{6,70},{8,72},{10,74},{12,76},{14,78},{16,80}... | collective-permute-start | bytes 786440 | tf_op jit(solution)/shard_map/ppermute | solution.py:323
  43.3 8.3 %collective-permute-start.4 = (f32[16,32,128]{2,1,0:T(8,128)S(1)}, f32[16,32,128]{2,1,0:T(8,128)S(1)}, u32[]{:S(2)}, u32[]{:S(2)}) collective-permute-start(f32[16,32,128]{2,1,0:T(8,128)S(1)} %slice_select_fusion.refs_0_), channel_id=1, source_target_pairs={{0,32},{2,34},{4,36},{6,38},{8,40},{10,42},{12,44},{14,46},{16,48}... | collective-permute-start | bytes 786440 | tf_op jit(solution)/shard_map/ppermute | solution.py:323
  49.0 73.9 %copy-start.2 = (s32[1025]{0:T(1024)}, s32[1025]{0:T(1024)S(1)}, u32[]{:S(2)}) copy-start(s32[1025]{0:T(1024)S(1)} %get-tuple-element.147.moved.refs_1_) | copy-start | bytes 12304
  50.0 72.9 %copy-start.5 = (f32[2,128,128]{2,1,0:T(8,128)S(1)}, f32[2,128,128]{2,1,0:T(8,128)}, u32[]{:S(2)}) copy-start(f32[2,128,128]{2,1,0:T(8,128)} %upper_inverse.1) | copy-start | bytes 393220
  50.1 72.9 %copy-start.6 = (f32[2,128,128]{2,1,0:T(8,128)S(1)}, f32[2,128,128]{2,1,0:T(8,128)}, u32[]{:S(2)}) copy-start(f32[2,128,128]{2,1,0:T(8,128)} %lower_inverse.1) | copy-start | bytes 393220
  53.8 10.8 %collective-permute-start.12 = (f32[32,16,128]{2,1,0:T(8,128)S(1)}, f32[32,16,128]{2,1,0:T(8,128)S(1)}, u32[]{:S(2)}, u32[]{:S(2)}) collective-permute-start(f32[32,16,128]{2,1,0:T(8,128)S(1)} %get-tuple-element.156), channel_id=1, source_target_pairs={{0,8},{2,10},{4,12},{6,14},{8,16},{10,18},{12,20},{14,22},{16,24},... | collective-permute-start | bytes 786440 | tf_op jit(solution)/shard_map/ppermute | solution.py:323
  57.7 17.5 %collective-permute-start.9 = (f32[32,16,128]{2,1,0:T(8,128)S(1)}, f32[32,16,128]{2,1,0:T(8,128)S(1)}, u32[]{:S(2)}, u32[]{:S(2)}) collective-permute-start(f32[32,16,128]{2,1,0:T(8,128)S(1)} %get-tuple-element.155), channel_id=1, source_target_pairs={{0,4},{2,6},{4,0},{6,2},{8,12},{10,14},{12,8},{14,10},{16,20},{18,... | collective-permute-start | bytes 786440 | tf_op jit(solution)/shard_map/ppermute | solution.py:323
  61.4 13.8 %collective-permute-start.8 = (f32[32,16,128]{2,1,0:T(8,128)S(1)}, f32[32,16,128]{2,1,0:T(8,128)S(1)}, u32[]{:S(2)}, u32[]{:S(2)}) collective-permute-start(f32[32,16,128]{2,1,0:T(8,128)S(1)} %get-tuple-element.155), channel_id=1, source_target_pairs={{0,6},{2,0},{4,2},{6,4},{8,14},{10,8},{12,10},{14,12},{16,22},{18,... | collective-permute-start | bytes 786440 | tf_op jit(solution)/shard_map/ppermute | solution.py:323
  62.0 11.6 %collective-permute-start.14 = (f32[32,16,128]{2,1,0:T(8,128)S(1)}, f32[32,16,128]{2,1,0:T(8,128)S(1)}, u32[]{:S(2)}, u32[]{:S(2)}) collective-permute-start(f32[32,16,128]{2,1,0:T(8,128)S(1)} %get-tuple-element.156), channel_id=1, source_target_pairs={{0,16},{2,18},{4,20},{6,22},{8,24},{10,26},{12,28},{14,30},{16,0},... | collective-permute-start | bytes 786440 | tf_op jit(solution)/shard_map/ppermute | solution.py:323
  64.4 9.1 %collective-permute-start.13 = (f32[32,16,128]{2,1,0:T(8,128)S(1)}, f32[32,16,128]{2,1,0:T(8,128)S(1)}, u32[]{:S(2)}, u32[]{:S(2)}) collective-permute-start(f32[32,16,128]{2,1,0:T(8,128)S(1)} %get-tuple-element.156), channel_id=1, source_target_pairs={{0,24},{2,26},{4,28},{6,30},{8,0},{10,2},{12,4},{14,6},{16,8},{18,... | collective-permute-start | bytes 786440 | tf_op jit(solution)/shard_map/ppermute | solution.py:323
  64.7 10.5 %collective-permute-start.7 = (f32[32,16,128]{2,1,0:T(8,128)S(1)}, f32[32,16,128]{2,1,0:T(8,128)S(1)}, u32[]{:S(2)}, u32[]{:S(2)}) collective-permute-start(f32[32,16,128]{2,1,0:T(8,128)S(1)} %get-tuple-element.155), channel_id=1, source_target_pairs={{0,2},{2,4},{4,6},{6,0},{8,10},{10,12},{12,14},{14,8},{16,18},{18,... | collective-permute-start | bytes 786440 | tf_op jit(solution)/shard_map/ppermute | solution.py:323
  73.6 32.8 %copy-start.12 = (f32[128,16,128]{2,1,0:T(8,128)}, f32[128,16,128]{2,1,0:T(8,128)S(1)}, u32[]{:S(2)}) copy-start(f32[128,16,128]{2,1,0:T(8,128)S(1)} %constant_dynamic-update-slice_fusion.4) | copy-start | bytes 3145732
  73.6 29.8 %collective-permute-start.16 = (f32[128,16,128]{2,1,0:T(8,128)S(1)}, f32[128,16,128]{2,1,0:T(8,128)S(1)}, u32[]{:S(2)}, u32[]{:S(2)}) collective-permute-start(f32[128,16,128]{2,1,0:T(8,128)S(1)} %constant_dynamic-update-slice_fusion.4), channel_id=1, source_target_pairs={{0,6},{2,0},{4,2},{6,4},{8,14},{10,8},{12,10},{14,12},{16,22},{18,... | collective-permute-start | bytes 3145736 | tf_op jit(solution)/shard_map/ppermute | solution.py:323
  74.1 29.3 %collective-permute-start.15 = (f32[128,16,128]{2,1,0:T(8,128)S(1)}, f32[128,16,128]{2,1,0:T(8,128)S(1)}, u32[]{:S(2)}, u32[]{:S(2)}) collective-permute-start(f32[128,16,128]{2,1,0:T(8,128)S(1)} %constant_dynamic-update-slice_fusion.4), channel_id=1, source_target_pairs={{0,2},{2,4},{4,6},{6,0},{8,10},{10,12},{12,14},{14,8},{16,18},{18,... | collective-permute-start | bytes 3145736 | tf_op jit(solution)/shard_map/ppermute | solution.py:323
  75.3 30.3 %copy-start.11 = (f32[128,16,128]{2,1,0:T(8,128)}, f32[128,16,128]{2,1,0:T(8,128)S(1)}, u32[]{:S(2)}) copy-start(f32[128,16,128]{2,1,0:T(8,128)S(1)} %constant_dynamic-update-slice_fusion) | copy-start | bytes 3145732
  75.3 28.2 %collective-permute-start.11 = (f32[128,16,128]{2,1,0:T(8,128)S(1)}, f32[128,16,128]{2,1,0:T(8,128)S(1)}, u32[]{:S(2)}, u32[]{:S(2)}) collective-permute-start(f32[128,16,128]{2,1,0:T(8,128)S(1)} %constant_dynamic-update-slice_fusion), channel_id=1, source_target_pairs={{0,24},{2,26},{4,28},{6,30},{8,0},{10,2},{12,4},{14,6},{16,8},{18,... | collective-permute-start | bytes 3145736 | tf_op jit(solution)/shard_map/ppermute | solution.py:323
  78.9 24.6 %collective-permute-start.10 = (f32[128,16,128]{2,1,0:T(8,128)S(1)}, f32[128,16,128]{2,1,0:T(8,128)S(1)}, u32[]{:S(2)}, u32[]{:S(2)}) collective-permute-start(f32[128,16,128]{2,1,0:T(8,128)S(1)} %constant_dynamic-update-slice_fusion), channel_id=1, source_target_pairs={{0,8},{2,10},{4,12},{6,14},{8,16},{10,18},{12,20},{14,22},{16,24},... | collective-permute-start | bytes 3145736 | tf_op jit(solution)/shard_map/ppermute | solution.py:323
  103.4 25.7 %copy-start.7 = (f32[128,16,128]{2,1,0:T(8,128)}, f32[128,16,128]{2,1,0:T(8,128)S(1)}, u32[]{:S(2)}) copy-start(f32[128,16,128]{2,1,0:T(8,128)S(1)} %collective-permute-done.16) | copy-start | bytes 3145732
  103.4 25.7 %copy-start.8 = (f32[128,16,128]{2,1,0:T(8,128)}, f32[128,16,128]{2,1,0:T(8,128)S(1)}, u32[]{:S(2)}) copy-start(f32[128,16,128]{2,1,0:T(8,128)S(1)} %collective-permute-done.15) | copy-start | bytes 3145732
  103.5 8.9 %copy-start.9 = (f32[128,16,128]{2,1,0:T(8,128)}, f32[128,16,128]{2,1,0:T(8,128)S(1)}, u32[]{:S(2)}) copy-start(f32[128,16,128]{2,1,0:T(8,128)S(1)} %collective-permute-done.11) | copy-start | bytes 3145732
  103.5 1.0 copy-start.10
  108.1 21.0 %collective-permute-start.20 = (f32[64,16,128]{2,1,0:T(8,128)}, f32[64,16,128]{2,1,0:T(8,128)}, u32[]{:S(2)}, u32[]{:S(2)}) collective-permute-start(f32[64,16,128]{2,1,0:T(8,128)} %slice.65), channel_id=1, source_target_pairs={{0,6},{2,0},{4,2},{6,4},{8,14},{10,8},{12,10},{14,12},{16,22},{18,... | collective-permute-start | bytes 1572872 | tf_op jit(solution)/shard_map/ppermute | solution.py:323
  110.9 18.2 %collective-permute-start.19 = (f32[64,16,128]{2,1,0:T(8,128)}, f32[64,16,128]{2,1,0:T(8,128)}, u32[]{:S(2)}, u32[]{:S(2)}) collective-permute-start(f32[64,16,128]{2,1,0:T(8,128)} %slice.64), channel_id=1, source_target_pairs={{0,2},{2,4},{4,6},{6,0},{8,10},{10,12},{12,14},{14,8},{16,18},{18,... | collective-permute-start | bytes 1572872 | tf_op jit(solution)/shard_map/ppermute | solution.py:323
  110.9 18.2 %collective-permute-start.18 = (f32[64,16,128]{2,1,0:T(8,128)}, f32[64,16,128]{2,1,0:T(8,128)}, u32[]{:S(2)}, u32[]{:S(2)}) collective-permute-start(f32[64,16,128]{2,1,0:T(8,128)} %slice.63), channel_id=1, source_target_pairs={{0,24},{2,26},{4,28},{6,30},{8,0},{10,2},{12,4},{14,6},{16,8},{18,... | collective-permute-start | bytes 1572872 | tf_op jit(solution)/shard_map/ppermute | solution.py:323
  110.9 18.2 %collective-permute-start.17 = (f32[64,16,128]{2,1,0:T(8,128)}, f32[64,16,128]{2,1,0:T(8,128)}, u32[]{:S(2)}, u32[]{:S(2)}) collective-permute-start(f32[64,16,128]{2,1,0:T(8,128)} %slice.62), channel_id=1, source_target_pairs={{0,8},{2,10},{4,12},{6,14},{8,16},{10,18},{12,20},{14,22},{16,24},... | collective-permute-start | bytes 1572872 | tf_op jit(solution)/shard_map/ppermute | solution.py:323
  (3 other events, 2.4 us)

commit v4 on v3

--- a/solution.py
+++ b/solution.py
@@ -259,30 +259,37 @@
     return lax.all_to_all(rows, "prow", 0, 0, tiled=True)
 
 
-def crowded(place, pick_row, hub_source, rows, received):
+def crowded(place, pick_row, hub_source, rows):
     def step(t, held):
         sent = send_round(jnp.full((1,), t, jnp.int32), place, pick_row, rows)
         row = lax.dynamic_slice_in_dim(swap_all(sent), hub_source[t], 1, axis=0)
         return lax.dynamic_update_slice_in_dim(held, row, t, axis=0)
 
-    held = lax.fori_loop(0, SHARE, step, jnp.zeros_like(received))
-    return held, jnp.arange(SHARE, dtype=jnp.int32)
-
-
-def pack_kernel(place, index, received, *refs):
+    return lax.fori_loop(0, SHARE, step, jnp.zeros((SHARE,) + rows.shape[1:], rows.dtype))
+
+
+def pack_kernel(place, index, received, spare, *refs):
     copies, left, right, heads, buffer, edge, sems, out_sems = refs[:SIDE], *refs[SIDE:]
     z = place[0] // PLANE
 
     def pick(t):
-        return pltpu.make_async_copy(received.at[index[t]], buffer.at[t], sems.at[t])
+        return pltpu.make_async_copy(received.at[jnp.maximum(index[t], 0)], buffer.at[t], sems.at[t])
 
     def previous(held):
         return pltpu.make_async_copy(held, buffer.at[pl.ds(SHARE, SHARE)], sems.at[SHARE])
 
-    each(SHARE, lambda t: pick(t).start())
+    balanced = index[0] >= 0
+    pl.when(balanced)(lambda: each(SHARE, lambda t: pick(t).start()))
+
+    @pl.when(jnp.logical_not(balanced))
+    def _():
+        whole = pltpu.make_async_copy(spare, buffer.at[pl.ds(0, SHARE)], sems.at[0])
+        whole.start()
+        whole.wait()
+
     for level, held in enumerate(copies):
         pl.when(z == level)(lambda held=held: previous(held).start())
-    each(SHARE, lambda t: pick(t).wait())
+    pl.when(balanced)(lambda: each(SHARE, lambda t: pick(t).wait()))
     previous(copies[0]).wait()
     edge[...] = buffer[:, 0, :]
     half = left.shape[1]
@@ -300,13 +307,13 @@
         out.wait()
 
 
-def pack(place, index, received, copies):
+def pack(place, index, received, spare, copies):
     blocks, width = received.shape[1:]
     half = jax.ShapeDtypeStruct((2 * SHARE, blocks // 2, width), received.dtype)
     return pl.pallas_call(
         pack_kernel,
         out_shape=(half, half, jax.ShapeDtypeStruct((PLANE * 2 * SHARE, width), received.dtype)),
-        in_specs=[SMEM, SMEM] + [HBM] * (1 + SIDE),
+        in_specs=[SMEM, SMEM] + [HBM] * (2 + SIDE),
         out_specs=(HBM,) * 3,
         scratch_shapes=[
             pltpu.VMEM((2 * SHARE, blocks, width), received.dtype),
@@ -316,7 +323,7 @@
         ],
         compiler_params=SMALL,
         name="pack",
-    )(place, index, received, *copies)
+    )(place, index, received, spare, *copies)
 
 
 def permute(value, pairs):
@@ -459,7 +466,7 @@
             pltpu.VMEM((local_rows, NB), jnp.float32),
             pltpu.SemaphoreType.DMA((2,)),
         ],
-        compiler_params=pltpu.CompilerParams(vmem_limit_bytes=24 << 20),
+        compiler_params=pltpu.CompilerParams(vmem_limit_bytes=61 << 20),
         cost_estimate=pl.CostEstimate(flops=1_200_000_000, transcendentals=0, bytes_accessed=20_000_000),
         name="weigh",
     )(place, moved, panel, head, orders.reshape(3, PICKS), upper_inverse, lower_inverse)
@@ -468,8 +475,8 @@
 def update_kernel(*refs):
     place, moved, weights_hbm, edge_hbm, rows_hbm = refs[:5]
     pieces, out_hbm = (refs[5:10], refs[10:15]), refs[15]
-    rows, plane, kept, result, weights, edge = refs[16:22]
-    row_sems, piece_sems, kept_sems, out_sems, weight_sems = refs[22:]
+    rows, plane, result, weights, edge = refs[16:21]
+    row_sems, piece_sems, out_sems, weight_sems = refs[21:]
     groups, half = rows.shape[0], plane.shape[3]
     is_home = place[0] < 2
     found = moved[4 * PICKS]
@@ -479,31 +486,14 @@
         columns = pl.ds(group * GROUP, GROUP)
         return pltpu.make_async_copy(rows_hbm.at[:, columns, :], rows.at[group], row_sems.at[group])
 
-    def fetch_piece(side, n):
-        source = pieces[side][n].at[:, pl.ds(0, SHARE)]
-        target = plane.at[side, pl.ds(begins[n], begins[n + 1] - begins[n])]
-        return pltpu.make_async_copy(source, target, piece_sems.at[side, n])
-
-    def kept_half(i, side, source):
-        return pltpu.make_async_copy(source, kept.at[side, i], kept_sems.at[side, i])
-
-    def start_kept(i, carry):
-        for side in range(2):
-            at = moved[(1 + side) * PICKS + i]
-            there = at // SHARE
-            for n, piece in enumerate(pieces[side]):
-
-                @pl.when(jnp.logical_and(there >= begins[n], there < begins[n + 1]))
-                def _():
-                    chunk = jnp.clip(there - begins[n], 0, begins[n + 1] - begins[n] - 1)
-                    kept_half(i, side, piece.at[chunk, SHARE + at % SHARE]).start()
-
-        return carry
-
-    def wait_kept(i, carry):
-        for side in range(2):
-            kept_half(i, side, pieces[side][0].at[0, 0]).wait()
-        return carry
+    def fetch_piece(side, n, kind):
+        count = begins[n + 1] - begins[n]
+        part = pl.ds(kind * SHARE, SHARE)
+        return pltpu.make_async_copy(
+            pieces[side][n].at[:, part],
+            plane.at[side, pl.ds(begins[n], count), part],
+            piece_sems.at[side, n, kind],
+        )
 
     def write(group, slot):
         return pltpu.make_async_copy(
@@ -516,34 +506,31 @@
     ]
     for factor in factors:
         factor.start()
-    for side in range(2):
+    def start_pieces(side, kind):
         for n in range(5):
-            fetch_piece(side, n).start()
-        for group in range(side * groups // 2, (side + 1) * groups // 2):
-            fetch_rows(group).start()
-        if side == 0:
-            lax.fori_loop(0, found, start_kept, 0)
+            fetch_piece(side, n, kind).start()
+
+    start_pieces(0, 0)
+    fetch_rows(0).start()
+    start_pieces(0, 1)
+    fetch_rows(1).start()
 
     for group in range(groups):
         slot, side = group % 2, group * GROUP // half
         begin = group * GROUP % half
         if begin == 0:
             for n in range(5):
-                fetch_piece(side, n).wait()
+                fetch_piece(side, n, 0).wait()
         if group == 0:
-            lax.fori_loop(0, found, wait_kept, 0)
             for factor in factors:
                 factor.wait()
-        fetch_rows(group).wait()
-
-        def patch(i, carry):
-            rows[group, moved[i], :, :] = kept[side, i, begin : begin + GROUP, :]
-            return carry
-
-        lax.fori_loop(0, found, patch, 0)
+            start_pieces(1, 0)
+            start_pieces(1, 1)
+        if group + 2 < groups:
+            fetch_rows(group + 2).start()
         if group >= 2:
             write(group - 2, slot).wait()
-        picked = plane[side, :, :, begin : begin + GROUP, :].reshape(PICKS, GROUP, NB)
+        picked = plane[side, :, :SHARE, begin : begin + GROUP, :].reshape(PICKS, GROUP, NB)
         picked = pltpu.einshape("rcl->crl", picked)
         products = []
         for pair in range(GROUP // 2):
@@ -553,6 +540,17 @@
             product += single(weights[2 * side + 1], right_high)
             products += [product[:, :NB], product[:, NB:]]
         product = pltpu.einshape("crl->rcl", jnp.stack(products, axis=0))
+        if begin == 0:
+            for n in range(5):
+                fetch_piece(side, n, 1).wait()
+        fetch_rows(group).wait()
+
+        def patch(i, carry):
+            at = moved[(1 + side) * PICKS + i]
+            rows[group, moved[i], :, :] = plane[side, at // SHARE, SHARE + at % SHARE, begin : begin + GROUP, :]
+            return carry
+
+        lax.fori_loop(0, found, patch, 0)
         result[slot, :NB] = jnp.where(is_home, 0.0, rows[group, :NB]) - product[:NB]
         result[slot, NB:] = rows[group, NB:] - product[NB:]
         if group == 0:
@@ -573,14 +571,12 @@
         out_specs=HBM,
         scratch_shapes=[
             pltpu.VMEM((groups, local_rows, GROUP, NB), jnp.float32),
-            pltpu.VMEM((2, PLANE, SHARE, blocks // 2, NB), jnp.float32),
-            pltpu.VMEM((2, PICKS, blocks // 2, NB), jnp.float32),
+            pltpu.VMEM((2, PLANE, 2 * SHARE, blocks // 2, NB), jnp.float32),
             pltpu.VMEM((2, local_rows, GROUP, NB), jnp.float32),
             pltpu.VMEM((4, local_rows, PICKS), jnp.bfloat16),
             pltpu.VMEM((local_rows, NB), jnp.float32),
             pltpu.SemaphoreType.DMA((groups,)),
-            pltpu.SemaphoreType.DMA((2, 5)),
-            pltpu.SemaphoreType.DMA((2, PICKS)),
+            pltpu.SemaphoreType.DMA((2, 5, 2)),
             pltpu.SemaphoreType.DMA((2,)),
             pltpu.SemaphoreType.DMA((2,)),
         ],
@@ -601,15 +597,17 @@
     rank, most = ranks_of(picked)
     sent, pick_row, hub_source = deal(place, picked, rank, rows)
     received = swap_all(sent)
+    held, panel = lax.optimization_barrier((held, panel))
     copies = climb(held, me)
     moved, orders = tables(place, pivots, kept, rank)
-    received, index = lax.cond(
+    spare = lax.cond(
         most <= SHARE,
-        lambda: (received, hub_source),
-        lambda: crowded(place, pick_row, hub_source, rows, received),
+        lambda: jnp.zeros((SHARE,) + rows.shape[1:], rows.dtype),
+        lambda: crowded(place, pick_row, hub_source, rows),
     )
+    index = jnp.where(most <= SHARE, hub_source, -1)
     index, orders = lax.optimization_barrier((index, orders))
-    left, right, head = pack(place, index, received, copies)
+    left, right, head = pack(place, index, received, spare, copies)
     planes = [list(range(z * PLANE, (z + 1) * PLANE)) for z in range(SIDE)]
     head = lax.all_to_all(head, "prow", 0, 0, tiled=True, axis_index_groups=planes)
     lines = gather_line(left, "x"), gather_line(right, "y")

time: 146 us -> 143 us (0.979)
  Pallas kernels: 33.5 us -> 31.2 us
  blocking collectives: 33.4 us -> 35.3 us
  local copies, waits for them, and re-layouts: 12.3 us -> 10.8 us
    all_gather x1, blocking collectives: 2.17 us -> 6.06 us  [local(): head = lax.all_gather(head, 'pcol', axis=0)]
    all_gather x1, blocking collectives: 6.69 us -> 2.9 us  [local(): panel = lax.all_gather(rows[:, 0, :], 'pcol', axis=0)]
    pallas_call x1, Pallas kernels: 15.6 us -> 12.4 us  [update(): pl.pallas_call(update_kernel, out_shape=jax.ShapeDtypeStruct(rows.shape,...]
    all_to_all x1, blocking collectives: 24.5 us -> 26.3 us  [local(): lax.all_to_all(head, 'prow', 0, 0, tiled=True, axis_index_groups=planes)]
    pallas_call x1, Pallas kernels: 4.46 us -> 6.06 us  [weigh(): pl.pallas_call(weigh_kernel, out_shape=(jax.ShapeDtypeStruct((4, local_ro...]
    unnamed x32 -> x28, local copies, waits for them, and re-layouts: 3.51 us -> 2.41 us
  transfers between devices with their start and end apart: 22 -> 22, of which waited for: 4 -> 4; matrix products, arithmetic and copies ran while one was open for 4% -> 3% of each run, Pallas kernels for 11% -> 12%
where the time goes in v4:
time: 143 us; the launch traced here: 142 us
  starting transfers between devices  41.6 us (29%)
  blocking collectives  35.3 us (25%)
  Pallas kernels  31.2 us (22%)
  waiting for transfers between devices  19.6 us (14%)
  local copies, waits for them, and re-layouts  10.8 us (8%)
  other arithmetic  2.23 us (2%)
    ppermute x21, starting transfers between devices, permute(): return lax.ppermute(value, 'prow', pairs)  35.2 us
    all_to_all x1, blocking collectives, local(): lax.all_to_all(head, 'prow', 0, 0, tiled=True, axis_index_groups=planes)  26.3 us
    ppermute x21, waiting for transfers between devices, permute(): return lax.ppermute(value, 'prow', pairs)  19.6 us
    pallas_call x1, Pallas kernels, update(): pl.pallas_call(update_kernel, out_shape=jax.ShapeDtypeStruct(rows.shape,...  12.4 us
    all_to_all x1, starting transfers between devices, swap_all(): return lax.all_to_all(rows, 'prow', 0, 0, tiled=True)  6.38 us
    pallas_call x1, Pallas kernels, weigh(): pl.pallas_call(weigh_kernel, out_shape=(jax.ShapeDtypeStruct((4, local_ro...  6.06 us
    all_gather x1, blocking collectives, local(): head = lax.all_gather(head, 'pcol', axis=0)  6.06 us
    pallas_call x1, Pallas kernels, deal(): pl.pallas_call(deal_kernel, out_shape=(jax.ShapeDtypeStruct((chips,) + ro...  4.19 us
  transfers between devices with their start and end apart: 22, of which 4 were waited for; matrix products, arithmetic and copies ran while one was open for 3% of the time, Pallas kernels for 12%

profile of v4, /device:TPU:1, one launch (start us, length us, event | category | flops | bytes accessed | tf_op | source)
XLA Modules:
  0.0 142.0 jit_solution(10201462119201918003)
XLA Ops:
  0.0 2.3 %slice_bitcast_fusion.1 = (f32[32,32,128]{2,1,0:T(8,128)}, f32[32,32,128]{2,1,0:T(8,128)S(1)}, f32[32,32,128]{2,1,0:T(8,128)S(1)}) fusion(f32[4,1,128,32,1,128]{5,3,2,4,1,0:T(8,128)} %bitcast.45), kind=kLoop, calls=%fused_computation.5 | loop fusion | bytes 3145728 | tf_op jit(solution)/shard_map/slice | solution.py:341
  2.3 4.0 %collective-permute-start.2 = (f32[32,32,128]{2,1,0:T(8,128)}, f32[32,32,128]{2,1,0:T(8,128)S(1)}, u32[]{:S(2)}, u32[]{:S(2)}) collective-permute-start(f32[32,32,128]{2,1,0:T(8,128)} %get-tuple-element.179), channel_id=1, source_target_pairs={{0,8},{2,10},{1,9},{3,11}} | collective-permute-start | bytes 1572872 | tf_op jit(solution)/shard_map/ppermute | solution.py:330
  6.3 2.3 %collective-permute-start.1 = (f32[32,32,128]{2,1,0:T(8,128)S(1)}, f32[32,32,128]{2,1,0:T(8,128)S(1)}, u32[]{:S(2)}, u32[]{:S(2)}) collective-permute-start(f32[32,32,128]{2,1,0:T(8,128)S(1)} %get-tuple-element.180), channel_id=1, source_target_pairs={{0,16},{2,18},{1,17},{3,19}} | collective-permute-start | bytes 1572872 | tf_op jit(solution)/shard_map/ppermute | solution.py:330
  8.6 2.1 %collective-permute-start = (f32[32,32,128]{2,1,0:T(8,128)S(1)}, f32[32,32,128]{2,1,0:T(8,128)}, u32[]{:S(2)}, u32[]{:S(2)}) collective-permute-start(f32[32,32,128]{2,1,0:T(8,128)S(1)} %get-tuple-element.181), channel_id=1, source_target_pairs={{0,24},{2,26},{1,25},{3,27}} | collective-permute-start | bytes 1572872 | tf_op jit(solution)/shard_map/ppermute | solution.py:330
  11.4 3.7 %exchange.1 = (s32[256]{0:T(256)S(1)}, s32[256]{0:T(256)S(1)}) custom-call(s32[256]{0:T(256)S(1)} %bitcast.43), custom_call_target="tpu_custom_call" | custom-call | bytes 60000000 | tf_op jit(solution)/shard_map/exchange/pallas_call | solution.py:73
  16.9 4.2 %deal.1 = (f32[64,32,128]{2,1,0:T(8,128)}, s32[256]{0:T(256)S(1)}, s32[16]{0:T(128)S(1)}) custom-call(s32[2]{0:T(128)S(1)} %pad_add_fusion.place.refs_0_, s32[256]{0:T(256)S(1)} %get-tuple-element.145.picked, s32[256]{0:T(256)S(1)} %get-tuple-element.166.rank, f32[512,32,128]{2,1,0:T(8,128)} %bitcast.46), custom_call_target="tpu_custom_call" | custom-call | bytes 30000000 | tf_op jit(solution)/shard_map/deal/pallas_call | solution.py:142
  21.1 6.4 %all-to-all-start.1 = ((f32[64,32,128]{2,1,0:T(8,128)}), f32[64,32,128]{2,1,0:T(8,128)S(1)}, u32[]{:S(2)}, u32[]{:S(2)}) async-start(f32[64,32,128]{2,1,0:T(8,128)} %get-tuple-element.151), calls=%async_computation.1 | async-start | bytes 2097152 | tf_op jit(solution)/shard_map/all_to_all | solution.py:259
  27.6 1.7 %slice.70 = f32[512,1,128]{2,1,0:T(1,128)S(1)} slice(f32[512,32,128]{2,1,0:T(8,128)} %bitcast.48), slice={[0:512], [0:1], [0:128]} | slice | bytes 524288 | tf_op jit(solution)/shard_map/slice | solution.py:594
  29.3 2.9 %all-gather = f32[1024,1,128]{2,1,0:T(1,128)} all-gather(f32[512,1,128]{2,1,0:T(1,128)S(1)} %slice.70), channel_id=2, replica_groups=mesh['prow'=64,'pcol'=2] {'pcol'}, dimensions={0}, use_global_device_ids=true | all-gather | bytes 786432 | tf_op jit(solution)/shard_map/all_gather | solution.py:594
  32.2 1.2 fusion.2
  33.4 4.7 %collective-permute-start.3 = (f32[16,32,128]{2,1,0:T(8,128)S(1)}, f32[16,32,128]{2,1,0:T(8,128)S(1)}, u32[]{:S(2)}, u32[]{:S(2)}) collective-permute-start(f32[16,32,128]{2,1,0:T(8,128)S(1)} %slice.61), channel_id=1, source_target_pairs={{0,4},{2,6},{8,12},{10,14},{16,20},{18,22},{24,28},{26,30},{1,5},{... | collective-permute-start | bytes 786440 | tf_op jit(solution)/shard_map/ppermute | solution.py:330
  38.2 6.0 %collective-permute-done.3 = f32[16,32,128]{2,1,0:T(8,128)S(1)} collective-permute-done((f32[16,32,128]{2,1,0:T(8,128)S(1)}, f32[16,32,128]{2,1,0:T(8,128)S(1)}, u32[]{:S(2)}, u32[]{:S(2)}) %collective-permute-start.3) | collective-permute-done | bytes 262176 | tf_op jit(solution)/shard_map/ppermute | solution.py:330
  44.2 1.3 collective-permute-start.6
  45.5 1.3 collective-permute-start.5
  46.8 1.3 collective-permute-start.4
  48.2 3.0 %tables.1 = (s32[1025]{0:T(1024)S(1)}, s32[768]{0:T(1024)S(1)}) custom-call(s32[2]{0:T(128)S(1)} %pad_add_fusion.place.refs_0_, s32[256]{0:T(256)S(1)} %bitcast.44, s32[256]{0:T(256)S(1)} %get-tuple-element.144.kept, s32[256]{0:T(256)S(1)} %get-tuple-element.166.rank), custom_call_target="tpu_custom_call" | custom-call | bytes 20000000 | tf_op jit(solution)/shard_map/tables/pallas_call | solution.py:209
  51.9 5.6 %collective-permute-done.4.refs_1_ = f32[16,32,128]{2,1,0:T(8,128)S(1)} collective-permute-done((f32[16,32,128]{2,1,0:T(8,128)S(1)}, f32[16,32,128]{2,1,0:T(8,128)S(1)}, u32[]{:S(2)}, u32[]{:S(2)}) %collective-permute-start.4) | collective-permute-done | bytes 262176 | tf_op jit(solution)/shard_map/ppermute | solution.py:330
  57.5 1.8 %pack.1 = (f32[32,16,128]{2,1,0:T(8,128)S(1)}, f32[32,16,128]{2,1,0:T(8,128)S(1)}, f32[512,128]{1,0:T(8,128)S(1)}) custom-call(s32[2]{0:T(128)S(1)} %pad_add_fusion.place.refs_0_, s32[16]{0:T(128)S(1)} %broadcast_select_fusion.index, f32[64,32,128]{2,1,0:T(8,128)S(1)} %all-to-all-done.1.received, f32[16,32,128]{2,1,0:T(8,128)} %copy-done.10, ...), custom_call_target="tpu_custom_call" | custom-call | tf_op jit(solution)/shard_map/pack/pallas_call | solution.py:313
  59.3 1.1 collective-permute-start.12
  60.4 3.7 %collective-permute-start.9 = (f32[32,16,128]{2,1,0:T(8,128)S(1)}, f32[32,16,128]{2,1,0:T(8,128)S(1)}, u32[]{:S(2)}, u32[]{:S(2)}) collective-permute-start(f32[32,16,128]{2,1,0:T(8,128)S(1)} %get-tuple-element.154), channel_id=1, source_target_pairs={{0,4},{2,6},{4,0},{6,2},{8,12},{10,14},{12,8},{14,10},{16,20},{18,... | collective-permute-start | bytes 786440 | tf_op jit(solution)/shard_map/ppermute | solution.py:330
  64.1 2.1 %collective-permute-start.14 = (f32[32,16,128]{2,1,0:T(8,128)S(1)}, f32[32,16,128]{2,1,0:T(8,128)S(1)}, u32[]{:S(2)}, u32[]{:S(2)}) collective-permute-start(f32[32,16,128]{2,1,0:T(8,128)S(1)} %get-tuple-element.155), channel_id=1, source_target_pairs={{0,16},{2,18},{4,20},{6,22},{8,24},{10,26},{12,28},{14,30},{16,0},... | collective-permute-start | bytes 786440 | tf_op jit(solution)/shard_map/ppermute | solution.py:330
  66.2 1.5 %collective-permute-start.13 = (f32[32,16,128]{2,1,0:T(8,128)S(1)}, f32[32,16,128]{2,1,0:T(8,128)S(1)}, u32[]{:S(2)}, u32[]{:S(2)}) collective-permute-start(f32[32,16,128]{2,1,0:T(8,128)S(1)} %get-tuple-element.155), channel_id=1, source_target_pairs={{0,24},{2,26},{4,28},{6,30},{8,0},{10,2},{12,4},{14,6},{16,8},{18,... | collective-permute-start | bytes 786440 | tf_op jit(solution)/shard_map/ppermute | solution.py:330
  67.8 1.5 %collective-permute-start.7 = (f32[32,16,128]{2,1,0:T(8,128)S(1)}, f32[32,16,128]{2,1,0:T(8,128)S(1)}, u32[]{:S(2)}, u32[]{:S(2)}) collective-permute-start(f32[32,16,128]{2,1,0:T(8,128)S(1)} %get-tuple-element.154), channel_id=1, source_target_pairs={{0,2},{2,4},{4,6},{6,0},{8,10},{10,12},{12,14},{14,8},{16,18},{18,... | collective-permute-start | bytes 786440 | tf_op jit(solution)/shard_map/ppermute | solution.py:330
  69.3 7.8 %collective-permute-done.13 = f32[32,16,128]{2,1,0:T(8,128)S(1)} collective-permute-done((f32[32,16,128]{2,1,0:T(8,128)S(1)}, f32[32,16,128]{2,1,0:T(8,128)S(1)}, u32[]{:S(2)}, u32[]{:S(2)}) %collective-permute-start.13) | collective-permute-done | bytes 262176 | tf_op jit(solution)/shard_map/ppermute | solution.py:330
  77.5 1.2 collective-permute-start.15
  78.8 3.5 %collective-permute-start.11 = (f32[128,16,128]{2,1,0:T(8,128)S(1)}, f32[128,16,128]{2,1,0:T(8,128)S(1)}, u32[]{:S(2)}, u32[]{:S(2)}) collective-permute-start(f32[128,16,128]{2,1,0:T(8,128)S(1)} %constant_dynamic-update-slice_fusion), channel_id=1, source_target_pairs={{0,24},{2,26},{4,28},{6,30},{8,0},{10,2},{12,4},{14,6},{16,8},{18,... | collective-permute-start | bytes 3145736 | tf_op jit(solution)/shard_map/ppermute | solution.py:330
  82.3 26.3 %all_to_all.27 = f32[16,32,128]{2,1,0:T(8,128)S(1)} all-to-all(f32[16,32,128]{2,1,0:T(8,128)S(1)} %bitcast.42), channel_id=1, replica_groups={{0,2,4,6,8,10,12,14,16,18,20,22,24,26,28,30},{32,34,36,38,40,42,44,46,4..., dimensions={0} | all-to-all | bytes 524288 | tf_op jit(solution)/shard_map/all_to_all | solution.py:612
  112.6 1.7 %collective-permute-start.20 = (f32[64,16,128]{2,1,0:T(8,128)}, f32[64,16,128]{2,1,0:T(8,128)S(1)}, u32[]{:S(2)}, u32[]{:S(2)}) collective-permute-start(f32[64,16,128]{2,1,0:T(8,128)} %slice.65), channel_id=1, source_target_pairs={{0,6},{2,0},{4,2},{6,4},{8,14},{10,8},{12,10},{14,12},{16,22},{18,... | collective-permute-start | bytes 1572872 | tf_op jit(solution)/shard_map/ppermute | solution.py:330
  114.3 1.5 %collective-permute-start.17 = (f32[64,16,128]{2,1,0:T(8,128)}, f32[64,16,128]{2,1,0:T(8,128)}, u32[]{:S(2)}, u32[]{:S(2)}) collective-permute-start(f32[64,16,128]{2,1,0:T(8,128)} %slice.62), channel_id=1, source_target_pairs={{0,8},{2,10},{4,12},{6,14},{8,16},{10,18},{12,20},{14,22},{16,24},... | collective-permute-start | bytes 1572872 | tf_op jit(solution)/shard_map/ppermute | solution.py:330
  116.4 6.1 %all-gather.1 = f32[1024,128]{1,0:T(8,128)} all-gather(f32[512,128]{1,0:T(8,128)S(1)} %bitcast.57), channel_id=3, replica_groups=mesh['prow'=64,'pcol'=2] {'pcol'}, dimensions={0}, use_global_device_ids=true | all-gather | bytes 786432 | tf_op jit(solution)/shard_map/all_gather | solution.py:616
  122.5 6.1 %weigh.1 = (bf16[4,512,256]{2,1,0:T(8,128)(2,1)}, f32[512,128]{1,0:T(8,128)}) custom-call(s32[2]{0:T(128)S(1)} %pad_add_fusion.place.refs_0_, s32[1025]{0:T(1024)} %copy-done, f32[2,512,128]{2,1,0:T(8,128)} %bitcast.59, f32[2,512,128]{2,1,0:T(8,128)} %bitcast.60, s32[3,256]{1,0:T(4,128)} %reshape.53.orders, f32[2,128,128]{2,1,0:T(8,128)} %upper_inverse.1, ...), custom_call_target="tpu_custom_call" | custom-call | flops 1200000000 | bytes 20000000 | tf_op jit(solution)/shard_map/weigh/pallas_call | solution.py:455
  129.4 12.4 %update.1 = f32[512,32,128]{2,1,0:T(8,128)} custom-call(s32[2]{0:T(128)S(1)} %pad_add_fusion.place.refs_0_, s32[1025]{0:T(1024)} %copy-done, bf16[4,512,256]{2,1,0:T(8,128)(2,1)} %get-tuple-element.159.refs_2_, f32[512,128]{1,0:T(8,128)} %get-tuple-element.160.refs_3_, f32[512,32,128]{2,1,0:T(8,128)} %bitcast.50, f32[4,32,16,128]{3,2,1,0:T(8,128)} %bitcast.55, ...), custom_call_target="tpu_custom_call" | custom-call | flops 3300000000 | bytes 26000000 | tf_op jit(solution)/shard_map/update/pallas_call | solution.py:567
  (68 shorter events, 8.4 us)
Async XLA Ops:
  2.3 29.9 %collective-permute-start.2 = (f32[32,32,128]{2,1,0:T(8,128)}, f32[32,32,128]{2,1,0:T(8,128)S(1)}, u32[]{:S(2)}, u32[]{:S(2)}) collective-permute-start(f32[32,32,128]{2,1,0:T(8,128)} %get-tuple-element.179), channel_id=1, source_target_pairs={{0,8},{2,10},{1,9},{3,11}} | collective-permute-start | bytes 1572872 | tf_op jit(solution)/shard_map/ppermute | solution.py:330
  6.3 25.9 %collective-permute-start.1 = (f32[32,32,128]{2,1,0:T(8,128)S(1)}, f32[32,32,128]{2,1,0:T(8,128)S(1)}, u32[]{:S(2)}, u32[]{:S(2)}) collective-permute-start(f32[32,32,128]{2,1,0:T(8,128)S(1)} %get-tuple-element.180), channel_id=1, source_target_pairs={{0,16},{2,18},{1,17},{3,19}} | collective-permute-start | bytes 1572872 | tf_op jit(solution)/shard_map/ppermute | solution.py:330
  8.6 23.6 %collective-permute-start = (f32[32,32,128]{2,1,0:T(8,128)S(1)}, f32[32,32,128]{2,1,0:T(8,128)}, u32[]{:S(2)}, u32[]{:S(2)}) collective-permute-start(f32[32,32,128]{2,1,0:T(8,128)S(1)} %get-tuple-element.181), channel_id=1, source_target_pairs={{0,24},{2,26},{1,25},{3,27}} | collective-permute-start | bytes 1572872 | tf_op jit(solution)/shard_map/ppermute | solution.py:330
  10.7 0.7 copy-start.1
  21.1 27.1 %copy-start.2 = (s32[2,128]{1,0:T(2,128)S(1)}, s32[2,128]{1,0:T(2,128)}, u32[]{:S(2)}) copy-start(s32[2,128]{1,0:T(2,128)} %param.9) | copy-start | bytes 3076
  21.1 11.1 %copy-start.10 = (f32[16,32,128]{2,1,0:T(8,128)}, f32[16,32,128]{2,1,0:T(8,128)S(1)}, u32[]{:S(2)}) copy-start(f32[16,32,128]{2,1,0:T(8,128)S(1)} %get-tuple-element.246.spare) | copy-start | bytes 786436
  21.1 30.6 %all-to-all-start.1 = ((f32[64,32,128]{2,1,0:T(8,128)}), f32[64,32,128]{2,1,0:T(8,128)S(1)}, u32[]{:S(2)}, u32[]{:S(2)}) async-start(f32[64,32,128]{2,1,0:T(8,128)} %get-tuple-element.151), calls=%async_computation.1 | async-start | bytes 2097152 | tf_op jit(solution)/shard_map/all_to_all | solution.py:259
  33.4 10.7 %collective-permute-start.3 = (f32[16,32,128]{2,1,0:T(8,128)S(1)}, f32[16,32,128]{2,1,0:T(8,128)S(1)}, u32[]{:S(2)}, u32[]{:S(2)}) collective-permute-start(f32[16,32,128]{2,1,0:T(8,128)S(1)} %slice.61), channel_id=1, source_target_pairs={{0,4},{2,6},{8,12},{10,14},{16,20},{18,22},{24,28},{26,30},{1,5},{... | collective-permute-start | bytes 786440 | tf_op jit(solution)/shard_map/ppermute | solution.py:330
  44.2 7.6 %collective-permute-start.6 = (f32[16,32,128]{2,1,0:T(8,128)S(1)}, f32[16,32,128]{2,1,0:T(8,128)S(1)}, u32[]{:S(2)}, u32[]{:S(2)}) collective-permute-start(f32[16,32,128]{2,1,0:T(8,128)S(1)} %slice_select_fusion.refs_0_), channel_id=1, source_target_pairs={{0,96},{2,98},{4,100},{6,102},{8,104},{10,106},{12,108},{14,110},{... | collective-permute-start | bytes 786440 | tf_op jit(solution)/shard_map/ppermute | solution.py:330
  45.5 6.4 %collective-permute-start.5 = (f32[16,32,128]{2,1,0:T(8,128)S(1)}, f32[16,32,128]{2,1,0:T(8,128)S(1)}, u32[]{:S(2)}, u32[]{:S(2)}) collective-permute-start(f32[16,32,128]{2,1,0:T(8,128)S(1)} %slice_select_fusion.refs_0_), channel_id=1, source_target_pairs={{0,64},{2,66},{4,68},{6,70},{8,72},{10,74},{12,76},{14,78},{16,80}... | collective-permute-start | bytes 786440 | tf_op jit(solution)/shard_map/ppermute | solution.py:330
  46.8 10.7 %collective-permute-start.4 = (f32[16,32,128]{2,1,0:T(8,128)S(1)}, f32[16,32,128]{2,1,0:T(8,128)S(1)}, u32[]{:S(2)}, u32[]{:S(2)}) collective-permute-start(f32[16,32,128]{2,1,0:T(8,128)S(1)} %slice_select_fusion.refs_0_), channel_id=1, source_target_pairs={{0,32},{2,34},{4,36},{6,38},{8,40},{10,42},{12,44},{14,46},{16,48}... | collective-permute-start | bytes 786440 | tf_op jit(solution)/shard_map/ppermute | solution.py:330
  59.3 8.4 %collective-permute-start.12 = (f32[32,16,128]{2,1,0:T(8,128)S(1)}, f32[32,16,128]{2,1,0:T(8,128)S(1)}, u32[]{:S(2)}, u32[]{:S(2)}) collective-permute-start(f32[32,16,128]{2,1,0:T(8,128)S(1)} %get-tuple-element.155), channel_id=1, source_target_pairs={{0,8},{2,10},{4,12},{6,14},{8,16},{10,18},{12,20},{14,22},{16,24},... | collective-permute-start | bytes 786440 | tf_op jit(solution)/shard_map/ppermute | solution.py:330
  60.4 18.4 %collective-permute-start.9 = (f32[32,16,128]{2,1,0:T(8,128)S(1)}, f32[32,16,128]{2,1,0:T(8,128)S(1)}, u32[]{:S(2)}, u32[]{:S(2)}) collective-permute-start(f32[32,16,128]{2,1,0:T(8,128)S(1)} %get-tuple-element.154), channel_id=1, source_target_pairs={{0,4},{2,6},{4,0},{6,2},{8,12},{10,14},{12,8},{14,10},{16,20},{18,... | collective-permute-start | bytes 786440 | tf_op jit(solution)/shard_map/ppermute | solution.py:330
  64.1 14.6 %collective-permute-start.8 = (f32[32,16,128]{2,1,0:T(8,128)S(1)}, f32[32,16,128]{2,1,0:T(8,128)S(1)}, u32[]{:S(2)}, u32[]{:S(2)}) collective-permute-start(f32[32,16,128]{2,1,0:T(8,128)S(1)} %get-tuple-element.154), channel_id=1, source_target_pairs={{0,6},{2,0},{4,2},{6,4},{8,14},{10,8},{12,10},{14,12},{16,22},{18,... | collective-permute-start | bytes 786440 | tf_op jit(solution)/shard_map/ppermute | solution.py:330
  64.1 13.0 %collective-permute-start.14 = (f32[32,16,128]{2,1,0:T(8,128)S(1)}, f32[32,16,128]{2,1,0:T(8,128)S(1)}, u32[]{:S(2)}, u32[]{:S(2)}) collective-permute-start(f32[32,16,128]{2,1,0:T(8,128)S(1)} %get-tuple-element.155), channel_id=1, source_target_pairs={{0,16},{2,18},{4,20},{6,22},{8,24},{10,26},{12,28},{14,30},{16,0},... | collective-permute-start | bytes 786440 | tf_op jit(solution)/shard_map/ppermute | solution.py:330
  66.2 10.9 %collective-permute-start.13 = (f32[32,16,128]{2,1,0:T(8,128)S(1)}, f32[32,16,128]{2,1,0:T(8,128)S(1)}, u32[]{:S(2)}, u32[]{:S(2)}) collective-permute-start(f32[32,16,128]{2,1,0:T(8,128)S(1)} %get-tuple-element.155), channel_id=1, source_target_pairs={{0,24},{2,26},{4,28},{6,30},{8,0},{10,2},{12,4},{14,6},{16,8},{18,... | collective-permute-start | bytes 786440 | tf_op jit(solution)/shard_map/ppermute | solution.py:330
  67.8 10.9 %collective-permute-start.7 = (f32[32,16,128]{2,1,0:T(8,128)S(1)}, f32[32,16,128]{2,1,0:T(8,128)S(1)}, u32[]{:S(2)}, u32[]{:S(2)}) collective-permute-start(f32[32,16,128]{2,1,0:T(8,128)S(1)} %get-tuple-element.154), channel_id=1, source_target_pairs={{0,2},{2,4},{4,6},{6,0},{8,10},{10,12},{12,14},{14,8},{16,18},{18,... | collective-permute-start | bytes 786440 | tf_op jit(solution)/shard_map/ppermute | solution.py:330
  77.2 35.4 %copy-start.8 = (f32[128,16,128]{2,1,0:T(8,128)}, f32[128,16,128]{2,1,0:T(8,128)S(1)}, u32[]{:S(2)}) copy-start(f32[128,16,128]{2,1,0:T(8,128)S(1)} %constant_dynamic-update-slice_fusion.4) | copy-start | bytes 3145732
  77.2 31.4 %collective-permute-start.16 = (f32[128,16,128]{2,1,0:T(8,128)S(1)}, f32[128,16,128]{2,1,0:T(8,128)S(1)}, u32[]{:S(2)}, u32[]{:S(2)}) collective-permute-start(f32[128,16,128]{2,1,0:T(8,128)S(1)} %constant_dynamic-update-slice_fusion.4), channel_id=1, source_target_pairs={{0,6},{2,0},{4,2},{6,4},{8,14},{10,8},{12,10},{14,12},{16,22},{18,... | collective-permute-start | bytes 3145736 | tf_op jit(solution)/shard_map/ppermute | solution.py:330
  77.5 31.1 %collective-permute-start.15 = (f32[128,16,128]{2,1,0:T(8,128)S(1)}, f32[128,16,128]{2,1,0:T(8,128)S(1)}, u32[]{:S(2)}, u32[]{:S(2)}) collective-permute-start(f32[128,16,128]{2,1,0:T(8,128)S(1)} %constant_dynamic-update-slice_fusion.4), channel_id=1, source_target_pairs={{0,2},{2,4},{4,6},{6,0},{8,10},{10,12},{12,14},{14,8},{16,18},{18,... | collective-permute-start | bytes 3145736 | tf_op jit(solution)/shard_map/ppermute | solution.py:330
  78.8 33.0 %copy-start.7 = (f32[128,16,128]{2,1,0:T(8,128)}, f32[128,16,128]{2,1,0:T(8,128)S(1)}, u32[]{:S(2)}) copy-start(f32[128,16,128]{2,1,0:T(8,128)S(1)} %constant_dynamic-update-slice_fusion) | copy-start | bytes 3145732
  78.8 29.8 %collective-permute-start.11 = (f32[128,16,128]{2,1,0:T(8,128)S(1)}, f32[128,16,128]{2,1,0:T(8,128)S(1)}, u32[]{:S(2)}, u32[]{:S(2)}) collective-permute-start(f32[128,16,128]{2,1,0:T(8,128)S(1)} %constant_dynamic-update-slice_fusion), channel_id=1, source_target_pairs={{0,24},{2,26},{4,28},{6,30},{8,0},{10,2},{12,4},{14,6},{16,8},{18,... | collective-permute-start | bytes 3145736 | tf_op jit(solution)/shard_map/ppermute | solution.py:330
  82.3 26.4 %collective-permute-start.10 = (f32[128,16,128]{2,1,0:T(8,128)S(1)}, f32[128,16,128]{2,1,0:T(8,128)S(1)}, u32[]{:S(2)}, u32[]{:S(2)}) collective-permute-start(f32[128,16,128]{2,1,0:T(8,128)S(1)} %constant_dynamic-update-slice_fusion), channel_id=1, source_target_pairs={{0,8},{2,10},{4,12},{6,14},{8,16},{10,18},{12,20},{14,22},{16,24},... | collective-permute-start | bytes 3145736 | tf_op jit(solution)/shard_map/ppermute | solution.py:330
  108.6 20.0 %copy-start.3 = (f32[128,16,128]{2,1,0:T(8,128)}, f32[128,16,128]{2,1,0:T(8,128)S(1)}, u32[]{:S(2)}) copy-start(f32[128,16,128]{2,1,0:T(8,128)S(1)} %collective-permute-done.16) | copy-start | bytes 3145732
  108.6 20.0 %copy-start.4 = (f32[128,16,128]{2,1,0:T(8,128)}, f32[128,16,128]{2,1,0:T(8,128)S(1)}, u32[]{:S(2)}) copy-start(f32[128,16,128]{2,1,0:T(8,128)S(1)} %collective-permute-done.15) | copy-start | bytes 3145732
  108.7 1.2 copy-start.5
  108.7 2.2 %copy-start.6 = (f32[128,16,128]{2,1,0:T(8,128)}, f32[128,16,128]{2,1,0:T(8,128)S(1)}, u32[]{:S(2)}) copy-start(f32[128,16,128]{2,1,0:T(8,128)S(1)} %collective-permute-done.10) | copy-start | bytes 3145732
  112.6 15.9 %collective-permute-start.20 = (f32[64,16,128]{2,1,0:T(8,128)}, f32[64,16,128]{2,1,0:T(8,128)S(1)}, u32[]{:S(2)}, u32[]{:S(2)}) collective-permute-start(f32[64,16,128]{2,1,0:T(8,128)} %slice.65), channel_id=1, source_target_pairs={{0,6},{2,0},{4,2},{6,4},{8,14},{10,8},{12,10},{14,12},{16,22},{18,... | collective-permute-start | bytes 1572872 | tf_op jit(solution)/shard_map/ppermute | solution.py:330
  114.3 14.2 %collective-permute-start.19 = (f32[64,16,128]{2,1,0:T(8,128)}, f32[64,16,128]{2,1,0:T(8,128)}, u32[]{:S(2)}, u32[]{:S(2)}) collective-permute-start(f32[64,16,128]{2,1,0:T(8,128)} %slice.64), channel_id=1, source_target_pairs={{0,2},{2,4},{4,6},{6,0},{8,10},{10,12},{12,14},{14,8},{16,18},{18,... | collective-permute-start | bytes 1572872 | tf_op jit(solution)/shard_map/ppermute | solution.py:330
  114.3 14.2 %collective-permute-start.18 = (f32[64,16,128]{2,1,0:T(8,128)}, f32[64,16,128]{2,1,0:T(8,128)}, u32[]{:S(2)}, u32[]{:S(2)}) collective-permute-start(f32[64,16,128]{2,1,0:T(8,128)} %slice.63), channel_id=1, source_target_pairs={{0,24},{2,26},{4,28},{6,30},{8,0},{10,2},{12,4},{14,6},{16,8},{18,... | collective-permute-start | bytes 1572872 | tf_op jit(solution)/shard_map/ppermute | solution.py:330
  114.3 14.2 %collective-permute-start.17 = (f32[64,16,128]{2,1,0:T(8,128)}, f32[64,16,128]{2,1,0:T(8,128)}, u32[]{:S(2)}, u32[]{:S(2)}) collective-permute-start(f32[64,16,128]{2,1,0:T(8,128)} %slice.62), channel_id=1, source_target_pairs={{0,8},{2,10},{4,12},{6,14},{8,16},{10,18},{12,20},{14,22},{16,24},... | collective-permute-start | bytes 1572872 | tf_op jit(solution)/shard_map/ppermute | solution.py:330
  128.5 0.8 copy-start.9
  (1 other events, 0.6 us)

commit v5 on v4

--- a/solution.py
+++ b/solution.py
@@ -346,10 +346,11 @@
     return held
 
 
-def climb(held, me):
+def climb(held, me, panel):
     across = permute(held[SHARE:], [(chip(0, n, h), chip(0, n, h + 2)) for n in range(SIDE) for h in range(2)])
+    across, panel = lax.optimization_barrier((across, panel))
     own = jnp.where(me % SIDE < 2, held[:SHARE], across)
-    return [own] + [permute(own, [(n, z * PLANE + n) for n in range(PLANE)]) for z in range(1, SIDE)]
+    return [own] + [permute(own, [(n, z * PLANE + n) for n in range(PLANE)]) for z in range(1, SIDE)], panel
 
 
 def gather_line(value, axis):
@@ -466,7 +467,7 @@
             pltpu.VMEM((local_rows, NB), jnp.float32),
             pltpu.SemaphoreType.DMA((2,)),
         ],
-        compiler_params=pltpu.CompilerParams(vmem_limit_bytes=61 << 20),
+        compiler_params=pltpu.CompilerParams(vmem_limit_bytes=24 << 20),
         cost_estimate=pl.CostEstimate(flops=1_200_000_000, transcendentals=0, bytes_accessed=20_000_000),
         name="weigh",
     )(place, moved, panel, head, orders.reshape(3, PICKS), upper_inverse, lower_inverse)
@@ -580,7 +581,7 @@
             pltpu.SemaphoreType.DMA((2,)),
             pltpu.SemaphoreType.DMA((2,)),
         ],
-        compiler_params=pltpu.CompilerParams(vmem_limit_bytes=56 << 20),
+        compiler_params=pltpu.CompilerParams(vmem_limit_bytes=48 << 20),
         cost_estimate=pl.CostEstimate(flops=3_300_000_000, transcendentals=0, bytes_accessed=26_000_000),
         name="update",
     )(place, moved, weights, edge, rows, *pieces)
@@ -597,8 +598,7 @@
     rank, most = ranks_of(picked)
     sent, pick_row, hub_source = deal(place, picked, rank, rows)
     received = swap_all(sent)
-    held, panel = lax.optimization_barrier((held, panel))
-    copies = climb(held, me)
+    copies, panel = climb(held, me, panel)
     moved, orders = tables(place, pivots, kept, rank)
     spare = lax.cond(
         most <= SHARE,
@@ -611,8 +611,9 @@
     planes = [list(range(z * PLANE, (z + 1) * PLANE)) for z in range(SIDE)]
     head = lax.all_to_all(head, "prow", 0, 0, tiled=True, axis_index_groups=planes)
     lines = gather_line(left, "x"), gather_line(right, "y")
-    hops = neighbours(lines[0], "y"), neighbours(lines[1], "x")
-    *hops, head = lax.optimization_barrier((*hops, head))
+    last = neighbours(lines[1], "x")
+    last, head = lax.optimization_barrier((last, head))
+    hops = neighbours(lines[0], "y"), last
     head = lax.all_gather(head, "pcol", axis=0)
     pieces = [gather_across(*parts) for parts in zip(lines, hops, "yx")]
     weights, edge = weigh(place, moved, panel, head, orders, upper_inverse, lower_inverse)

time: 143 us -> 139 us (0.972)
  blocking collectives: 35.3 us -> 11.6 us
  waiting for transfers between devices: 19.6 us -> 34.4 us
  local copies, waits for them, and re-layouts: 10.8 us -> 15.3 us
  starting transfers between devices: 41.6 us -> 44.9 us
  Pallas kernels: 31.2 us -> 28.3 us
    all_to_all x1 -> x0, blocking collectives: 26.3 us -> none  [local(): lax.all_to_all(head, 'prow', 0, 0, tiled=True, axis_index_groups=planes)]
    ppermute x21, waiting for transfers between devices: 19.6 us -> 27.4 us  [permute(): return lax.ppermute(value, 'prow', pairs)]
    all_to_all x0 -> x1, waiting for transfers between devices: none -> 6.93 us  [local(): lax.all_to_all(head, 'prow', 0, 0, tiled=True, axis_index_groups=planes)]
    all_to_all x0 -> x1, starting transfers between devices: none -> 5.15 us  [local(): lax.all_to_all(head, 'prow', 0, 0, tiled=True, axis_index_groups=planes)]
    unnamed x28 -> x18, local copies, waits for them, and re-layouts: 2.41 us -> 4.95 us
    pallas_call x1, Pallas kernels: 12.4 us -> 10.6 us  [update(): pl.pallas_call(update_kernel, out_shape=jax.ShapeDtypeStruct(rows.shape,...]
    ppermute x21, starting transfers between devices: 35.2 us -> 33.4 us  [permute(): return lax.ppermute(value, 'prow', pairs)]
    all_gather x1, blocking collectives: 6.06 us -> 7.78 us  [local(): head = lax.all_gather(head, 'pcol', axis=0)]
  transfers between devices with their start and end apart: 22 -> 23, of which waited for: 4 -> 6; matrix products, arithmetic and copies ran while one was open for 3% -> 9% of each run, Pallas kernels for 12% -> 11%
where the time goes in v5:
time: 139 us; the launch traced here: 138 us
  starting transfers between devices  44.9 us (32%)
  waiting for transfers between devices  34.4 us (25%)
  Pallas kernels  28.3 us (20%)
  local copies, waits for them, and re-layouts  15.3 us (11%)
  blocking collectives  11.6 us (8%)
  other arithmetic  2.31 us (2%)
    ppermute x21, starting transfers between devices, permute(): return lax.ppermute(value, 'prow', pairs)  33.4 us
    ppermute x21, waiting for transfers between devices, permute(): return lax.ppermute(value, 'prow', pairs)  27.4 us
    pallas_call x1, Pallas kernels, update(): pl.pallas_call(update_kernel, out_shape=jax.ShapeDtypeStruct(rows.shape,...  10.6 us
    all_gather x1, blocking collectives, local(): head = lax.all_gather(head, 'pcol', axis=0)  7.78 us
    all_to_all x1, waiting for transfers between devices, local(): lax.all_to_all(head, 'prow', 0, 0, tiled=True, axis_index_groups=planes)  6.93 us
    all_to_all x1, starting transfers between devices, swap_all(): return lax.all_to_all(rows, 'prow', 0, 0, tiled=True)  6.34 us
    all_to_all x1, starting transfers between devices, local(): lax.all_to_all(head, 'prow', 0, 0, tiled=True, axis_index_groups=planes)  5.15 us
    unnamed x18, local copies, waits for them, and re-layouts  4.95 us
  transfers between devices with their start and end apart: 23, of which 6 were waited for; matrix products, arithmetic and copies ran while one was open for 9% of the time, Pallas kernels for 11%

profile of v5, /device:TPU:1, one launch (start us, length us, event | category | flops | bytes accessed | tf_op | source)
XLA Modules:
  0.0 137.9 jit_solution(15311821433826927995)
XLA Ops:
  0.0 2.4 %slice_bitcast_fusion.1 = (f32[32,32,128]{2,1,0:T(8,128)}, f32[32,32,128]{2,1,0:T(8,128)}, f32[32,32,128]{2,1,0:T(8,128)S(1)}) fusion(f32[4,1,128,32,1,128]{5,3,2,4,1,0:T(8,128)} %bitcast.50), kind=kLoop, calls=%fused_computation.5 | loop fusion | bytes 3145728 | tf_op jit(solution)/shard_map/slice | solution.py:341
  2.4 4.0 %collective-permute-start.2 = (f32[32,32,128]{2,1,0:T(8,128)}, f32[32,32,128]{2,1,0:T(8,128)S(1)}, u32[]{:S(2)}, u32[]{:S(2)}) collective-permute-start(f32[32,32,128]{2,1,0:T(8,128)} %get-tuple-element.175), channel_id=1, source_target_pairs={{0,8},{2,10},{1,9},{3,11}} | collective-permute-start | bytes 1572872 | tf_op jit(solution)/shard_map/ppermute | solution.py:330
  6.5 2.3 %collective-permute-start.1 = (f32[32,32,128]{2,1,0:T(8,128)}, f32[32,32,128]{2,1,0:T(8,128)S(1)}, u32[]{:S(2)}, u32[]{:S(2)}) collective-permute-start(f32[32,32,128]{2,1,0:T(8,128)} %get-tuple-element.176), channel_id=1, source_target_pairs={{0,16},{2,18},{1,17},{3,19}} | collective-permute-start | bytes 1572872 | tf_op jit(solution)/shard_map/ppermute | solution.py:330
  8.8 2.1 %collective-permute-start = (f32[32,32,128]{2,1,0:T(8,128)S(1)}, f32[32,32,128]{2,1,0:T(8,128)}, u32[]{:S(2)}, u32[]{:S(2)}) collective-permute-start(f32[32,32,128]{2,1,0:T(8,128)S(1)} %get-tuple-element.177), channel_id=1, source_target_pairs={{0,24},{2,26},{1,25},{3,27}} | collective-permute-start | bytes 1572872 | tf_op jit(solution)/shard_map/ppermute | solution.py:330
  11.6 3.7 %exchange.1 = (s32[256]{0:T(256)S(1)}, s32[256]{0:T(256)S(1)}) custom-call(s32[256]{0:T(256)S(1)} %bitcast.48), custom_call_target="tpu_custom_call" | custom-call | bytes 60000000 | tf_op jit(solution)/shard_map/exchange/pallas_call | solution.py:73
  16.9 4.3 %deal.1 = (f32[64,32,128]{2,1,0:T(8,128)}, s32[256]{0:T(256)S(1)}, s32[16]{0:T(128)S(1)}) custom-call(s32[2]{0:T(128)S(1)} %pad_add_fusion.place.refs_0_, s32[256]{0:T(256)S(1)} %get-tuple-element.143.picked, s32[256]{0:T(256)S(1)} %get-tuple-element.162.rank, f32[512,32,128]{2,1,0:T(8,128)} %bitcast.51), custom_call_target="tpu_custom_call" | custom-call | bytes 30000000 | tf_op jit(solution)/shard_map/deal/pallas_call | solution.py:142
  21.3 6.3 %all-to-all-start.1 = ((f32[64,32,128]{2,1,0:T(8,128)}), f32[64,32,128]{2,1,0:T(8,128)S(1)}, u32[]{:S(2)}, u32[]{:S(2)}) async-start(f32[64,32,128]{2,1,0:T(8,128)} %get-tuple-element.149), calls=%async_computation.1 | async-start | bytes 2097152 | tf_op jit(solution)/shard_map/all_to_all | solution.py:259
  28.6 1.3 fusion.2
  29.9 3.6 %collective-permute-start.3 = (f32[16,32,128]{2,1,0:T(8,128)S(1)}, f32[16,32,128]{2,1,0:T(8,128)S(1)}, u32[]{:S(2)}, u32[]{:S(2)}) collective-permute-start(f32[16,32,128]{2,1,0:T(8,128)S(1)} %slice.70), channel_id=1, source_target_pairs={{0,4},{2,6},{8,12},{10,14},{16,20},{18,22},{24,28},{26,30},{1,5},{... | collective-permute-start | bytes 786440 | tf_op jit(solution)/shard_map/ppermute | solution.py:330
  33.5 1.7 %slice.71 = f32[512,1,128]{2,1,0:T(1,128)S(1)} slice(f32[512,32,128]{2,1,0:T(8,128)} %bitcast.54), slice={[0:512], [0:1], [0:128]} | slice | bytes 524288 | tf_op jit(solution)/shard_map/slice | solution.py:595
  35.3 3.8 %all-gather = f32[1024,1,128]{2,1,0:T(1,128)} all-gather(f32[512,1,128]{2,1,0:T(1,128)S(1)} %slice.71), channel_id=2, replica_groups=mesh['prow'=64,'pcol'=2] {'pcol'}, dimensions={0}, use_global_device_ids=true | all-gather | bytes 786432 | tf_op jit(solution)/shard_map/all_gather | solution.py:595
  39.1 4.5 %collective-permute-done.3 = f32[16,32,128]{2,1,0:T(8,128)S(1)} collective-permute-done((f32[16,32,128]{2,1,0:T(8,128)S(1)}, f32[16,32,128]{2,1,0:T(8,128)S(1)}, u32[]{:S(2)}, u32[]{:S(2)}) %collective-permute-start.3) | collective-permute-done | bytes 262176 | tf_op jit(solution)/shard_map/ppermute | solution.py:330
  43.6 1.3 collective-permute-start.6
  44.9 1.3 collective-permute-start.5
  46.2 1.3 collective-permute-start.4
  47.5 3.2 %tables.1 = (s32[1025]{0:T(1024)S(1)}, s32[768]{0:T(1024)S(1)}) custom-call(s32[2]{0:T(128)S(1)} %pad_add_fusion.place.refs_0_, s32[256]{0:T(256)S(1)} %bitcast.49, s32[256]{0:T(256)S(1)} %get-tuple-element.142.kept, s32[256]{0:T(256)S(1)} %get-tuple-element.162.rank), custom_call_target="tpu_custom_call" | custom-call | bytes 20000000 | tf_op jit(solution)/shard_map/tables/pallas_call | solution.py:209
  50.7 5.4 %collective-permute-done.4.refs_1_ = f32[16,32,128]{2,1,0:T(8,128)S(1)} collective-permute-done((f32[16,32,128]{2,1,0:T(8,128)S(1)}, f32[16,32,128]{2,1,0:T(8,128)S(1)}, u32[]{:S(2)}, u32[]{:S(2)}) %collective-permute-start.4) | collective-permute-done | bytes 262176 | tf_op jit(solution)/shard_map/ppermute | solution.py:330
  56.1 2.1 %pack.1 = (f32[32,16,128]{2,1,0:T(8,128)S(1)}, f32[32,16,128]{2,1,0:T(8,128)S(1)}, f32[512,128]{1,0:T(8,128)}) custom-call(s32[2]{0:T(128)S(1)} %pad_add_fusion.place.refs_0_, s32[16]{0:T(128)S(1)} %broadcast_select_fusion.index, f32[64,32,128]{2,1,0:T(8,128)S(1)} %all-to-all-done.1.received, f32[16,32,128]{2,1,0:T(8,128)S(1)} %get-tuple-element.242.spare, ...), custom_call_target="tpu_custom_call" | custom-call | tf_op jit(solution)/shard_map/pack/pallas_call | solution.py:313
  58.8 4.8 %collective-permute-start.9 = (f32[32,16,128]{2,1,0:T(8,128)S(1)}, f32[32,16,128]{2,1,0:T(8,128)S(1)}, u32[]{:S(2)}, u32[]{:S(2)}) collective-permute-start(f32[32,16,128]{2,1,0:T(8,128)S(1)} %get-tuple-element.152), channel_id=1, source_target_pairs={{0,16},{2,18},{4,20},{6,22},{8,24},{10,26},{12,28},{14,30},{16,0},... | collective-permute-start | bytes 786440 | tf_op jit(solution)/shard_map/ppermute | solution.py:330
  63.7 3.1 %collective-permute-start.14 = (f32[32,16,128]{2,1,0:T(8,128)S(1)}, f32[32,16,128]{2,1,0:T(8,128)S(1)}, u32[]{:S(2)}, u32[]{:S(2)}) collective-permute-start(f32[32,16,128]{2,1,0:T(8,128)S(1)} %get-tuple-element.158), channel_id=1, source_target_pairs={{0,4},{2,6},{4,0},{6,2},{8,12},{10,14},{12,8},{14,10},{16,20},{18,... | collective-permute-start | bytes 786440 | tf_op jit(solution)/shard_map/ppermute | solution.py:330
  68.5 7.4 %collective-permute-done.13 = f32[32,16,128]{2,1,0:T(8,128)S(1)} collective-permute-done((f32[32,16,128]{2,1,0:T(8,128)S(1)}, f32[32,16,128]{2,1,0:T(8,128)S(1)}, u32[]{:S(2)}, u32[]{:S(2)}) %collective-permute-start.13) | collective-permute-done | bytes 262176 | tf_op jit(solution)/shard_map/ppermute | solution.py:330
  76.1 1.3 collective-permute-start.15
  79.7 3.6 %collective-permute-start.11 = (f32[128,16,128]{2,1,0:T(8,128)}, f32[128,16,128]{2,1,0:T(8,128)}, u32[]{:S(2)}, u32[]{:S(2)}) collective-permute-start(f32[128,16,128]{2,1,0:T(8,128)} %constant_dynamic-update-slice_fusion), channel_id=1, source_target_pairs={{0,6},{2,0},{4,2},{6,4},{8,14},{10,8},{12,10},{14,12},{16,22},{18,... | collective-permute-start | bytes 3145736 | tf_op jit(solution)/shard_map/ppermute | solution.py:330
  83.2 5.1 %all-to-all-start.2 = ((f32[16,32,128]{2,1,0:T(8,128)}), f32[16,32,128]{2,1,0:T(8,128)}, u32[]{:S(2)}, u32[]{:S(2)}) async-start(f32[16,32,128]{2,1,0:T(8,128)} %bitcast.12), calls=%async_computation.2 | async-start | bytes 524288 | tf_op jit(solution)/shard_map/all_to_all | solution.py:612
  88.4 9.2 %collective-permute-done.16 = f32[128,16,128]{2,1,0:T(8,128)S(1)} collective-permute-done((f32[128,16,128]{2,1,0:T(8,128)S(1)}, f32[128,16,128]{2,1,0:T(8,128)S(1)}, u32[]{:S(2)}, u32[]{:S(2)}) %collective-permute-start.16) | collective-permute-done | bytes 1048608 | tf_op jit(solution)/shard_map/ppermute | solution.py:330
  99.4 1.5 %collective-permute-start.18 = (f32[64,16,128]{2,1,0:T(8,128)}, f32[64,16,128]{2,1,0:T(8,128)S(1)}, u32[]{:S(2)}, u32[]{:S(2)}) collective-permute-start(f32[64,16,128]{2,1,0:T(8,128)} %slice.74), channel_id=1, source_target_pairs={{0,24},{2,26},{4,28},{6,30},{8,0},{10,2},{12,4},{14,6},{16,8},{18,... | collective-permute-start | bytes 1572872 | tf_op jit(solution)/shard_map/ppermute | solution.py:330
  101.7 6.9 %all-to-all-done.2 = f32[16,32,128]{2,1,0:T(8,128)} async-done(((f32[16,32,128]{2,1,0:T(8,128)}), f32[16,32,128]{2,1,0:T(8,128)}, u32[]{:S(2)}, u32[]{:S(2)}) %all-to-all-start.2) | async-done | bytes 262176 | tf_op jit(solution)/shard_map/all_to_all | solution.py:612
  108.6 1.9 %slice.64 = f32[64,16,128]{2,1,0:T(8,128)} slice(f32[128,16,128]{2,1,0:T(8,128)} %collective-permute-done.10), slice={[0:64], [0:16], [0:128]} | slice | bytes 1048576 | tf_op jit(solution)/shard_map/slice | solution.py:367
  110.5 1.9 %slice.65 = f32[64,16,128]{2,1,0:T(8,128)} slice(f32[128,16,128]{2,1,0:T(8,128)} %collective-permute-done.11), slice={[64:128], [0:16], [0:128]} | slice | bytes 1048576 | tf_op jit(solution)/shard_map/slice | solution.py:367
  113.9 7.8 %all-gather.1 = f32[1024,128]{1,0:T(8,128)S(1)} all-gather(f32[512,128]{1,0:T(8,128)} %bitcast.13), channel_id=3, replica_groups=mesh['prow'=64,'pcol'=2] {'pcol'}, dimensions={0}, use_global_device_ids=true | all-gather | bytes 786432 | tf_op jit(solution)/shard_map/all_gather | solution.py:617
  122.7 4.5 %weigh.1 = (bf16[4,512,256]{2,1,0:T(8,128)(2,1)S(1)}, f32[512,128]{1,0:T(8,128)S(1)}) custom-call(s32[2]{0:T(128)S(1)} %pad_add_fusion.place.refs_0_, s32[1025]{0:T(1024)S(1)} %get-tuple-element.144.moved.refs_1_, f32[2,512,128]{2,1,0:T(8,128)S(1)} %bitcast.46, f32[2,512,128]{2,1,0:T(8,128)S(1)} %bitcast.47, s32[3,256]{1,0:T(4,128)S(1)} %reshape.53.orders, ...), custom_call_target="tpu_custom_call" | custom-call | flops 1200000000 | bytes 20000000 | tf_op jit(solution)/shard_map/weigh/pallas_call | solution.py:456
  127.2 10.6 %update.1 = f32[512,32,128]{2,1,0:T(8,128)} custom-call(s32[2]{0:T(128)S(1)} %pad_add_fusion.place.refs_0_, s32[1025]{0:T(1024)S(1)} %get-tuple-element.144.moved.refs_1_, bf16[4,512,256]{2,1,0:T(8,128)(2,1)S(1)} %get-tuple-element.156.refs_2_, f32[512,128]{1,0:T(8,128)S(1)} %get-tuple-element.157.refs_3_, f32[512,32,128]{2,1,0:T(8,128)} %bitcast.55, ...), custom_call_target="tpu_custom_call" | custom-call | flops 3300000000 | bytes 26000000 | tf_op jit(solution)/shard_map/update/pallas_call | solution.py:568
  (59 shorter events, 12.6 us)
Async XLA Ops:
  2.4 25.2 %collective-permute-start.2 = (f32[32,32,128]{2,1,0:T(8,128)}, f32[32,32,128]{2,1,0:T(8,128)S(1)}, u32[]{:S(2)}, u32[]{:S(2)}) collective-permute-start(f32[32,32,128]{2,1,0:T(8,128)} %get-tuple-element.175), channel_id=1, source_target_pairs={{0,8},{2,10},{1,9},{3,11}} | collective-permute-start | bytes 1572872 | tf_op jit(solution)/shard_map/ppermute | solution.py:330
  6.5 22.1 %collective-permute-start.1 = (f32[32,32,128]{2,1,0:T(8,128)}, f32[32,32,128]{2,1,0:T(8,128)S(1)}, u32[]{:S(2)}, u32[]{:S(2)}) collective-permute-start(f32[32,32,128]{2,1,0:T(8,128)} %get-tuple-element.176), channel_id=1, source_target_pairs={{0,16},{2,18},{1,17},{3,19}} | collective-permute-start | bytes 1572872 | tf_op jit(solution)/shard_map/ppermute | solution.py:330
  8.8 19.8 %collective-permute-start = (f32[32,32,128]{2,1,0:T(8,128)S(1)}, f32[32,32,128]{2,1,0:T(8,128)}, u32[]{:S(2)}, u32[]{:S(2)}) collective-permute-start(f32[32,32,128]{2,1,0:T(8,128)S(1)} %get-tuple-element.177), channel_id=1, source_target_pairs={{0,24},{2,26},{1,25},{3,27}} | collective-permute-start | bytes 1572872 | tf_op jit(solution)/shard_map/ppermute | solution.py:330
  10.9 0.7 copy-start.1
  21.2 26.3 %copy-start.2 = (s32[2,128]{1,0:T(2,128)S(1)}, s32[2,128]{1,0:T(2,128)}, u32[]{:S(2)}) copy-start(s32[2,128]{1,0:T(2,128)} %param.9) | copy-start | bytes 3076
  21.3 29.4 %all-to-all-start.1 = ((f32[64,32,128]{2,1,0:T(8,128)}), f32[64,32,128]{2,1,0:T(8,128)S(1)}, u32[]{:S(2)}, u32[]{:S(2)}) async-start(f32[64,32,128]{2,1,0:T(8,128)} %get-tuple-element.149), calls=%async_computation.1 | async-start | bytes 2097152 | tf_op jit(solution)/shard_map/all_to_all | solution.py:259
  27.7 94.0 %copy-start.3 = (f32[2,128,128]{2,1,0:T(8,128)S(1)}, f32[2,128,128]{2,1,0:T(8,128)}, u32[]{:S(2)}) copy-start(f32[2,128,128]{2,1,0:T(8,128)} %upper_inverse.1) | copy-start | bytes 393220
  27.7 94.0 %copy-start.4 = (f32[2,128,128]{2,1,0:T(8,128)S(1)}, f32[2,128,128]{2,1,0:T(8,128)}, u32[]{:S(2)}) copy-start(f32[2,128,128]{2,1,0:T(8,128)} %lower_inverse.1) | copy-start | bytes 393220
  29.9 13.6 %collective-permute-start.3 = (f32[16,32,128]{2,1,0:T(8,128)S(1)}, f32[16,32,128]{2,1,0:T(8,128)S(1)}, u32[]{:S(2)}, u32[]{:S(2)}) collective-permute-start(f32[16,32,128]{2,1,0:T(8,128)S(1)} %slice.70), channel_id=1, source_target_pairs={{0,4},{2,6},{8,12},{10,14},{16,20},{18,22},{24,28},{26,30},{1,5},{... | collective-permute-start | bytes 786440 | tf_op jit(solution)/shard_map/ppermute | solution.py:330
  43.6 7.1 %collective-permute-start.6 = (f32[16,32,128]{2,1,0:T(8,128)S(1)}, f32[16,32,128]{2,1,0:T(8,128)S(1)}, u32[]{:S(2)}, u32[]{:S(2)}) collective-permute-start(f32[16,32,128]{2,1,0:T(8,128)S(1)} %slice_select_fusion.refs_0_), channel_id=1, source_target_pairs={{0,96},{2,98},{4,100},{6,102},{8,104},{10,106},{12,108},{14,110},{... | collective-permute-start | bytes 786440 | tf_op jit(solution)/shard_map/ppermute | solution.py:330
  44.9 5.8 %collective-permute-start.5 = (f32[16,32,128]{2,1,0:T(8,128)S(1)}, f32[16,32,128]{2,1,0:T(8,128)S(1)}, u32[]{:S(2)}, u32[]{:S(2)}) collective-permute-start(f32[16,32,128]{2,1,0:T(8,128)S(1)} %slice_select_fusion.refs_0_), channel_id=1, source_target_pairs={{0,64},{2,66},{4,68},{6,70},{8,72},{10,74},{12,76},{14,78},{16,80}... | collective-permute-start | bytes 786440 | tf_op jit(solution)/shard_map/ppermute | solution.py:330
  46.2 9.9 %collective-permute-start.4 = (f32[16,32,128]{2,1,0:T(8,128)S(1)}, f32[16,32,128]{2,1,0:T(8,128)S(1)}, u32[]{:S(2)}, u32[]{:S(2)}) collective-permute-start(f32[16,32,128]{2,1,0:T(8,128)S(1)} %slice_select_fusion.refs_0_), channel_id=1, source_target_pairs={{0,32},{2,34},{4,36},{6,38},{8,40},{10,42},{12,44},{14,46},{16,48}... | collective-permute-start | bytes 786440 | tf_op jit(solution)/shard_map/ppermute | solution.py:330
  58.3 9.5 %collective-permute-start.12 = (f32[32,16,128]{2,1,0:T(8,128)S(1)}, f32[32,16,128]{2,1,0:T(8,128)S(1)}, u32[]{:S(2)}, u32[]{:S(2)}) collective-permute-start(f32[32,16,128]{2,1,0:T(8,128)S(1)} %get-tuple-element.158), channel_id=1, source_target_pairs={{0,2},{2,4},{4,6},{6,0},{8,10},{10,12},{12,14},{14,8},{16,18},{18,... | collective-permute-start | bytes 786440 | tf_op jit(solution)/shard_map/ppermute | solution.py:330
  58.8 20.1 %collective-permute-start.9 = (f32[32,16,128]{2,1,0:T(8,128)S(1)}, f32[32,16,128]{2,1,0:T(8,128)S(1)}, u32[]{:S(2)}, u32[]{:S(2)}) collective-permute-start(f32[32,16,128]{2,1,0:T(8,128)S(1)} %get-tuple-element.152), channel_id=1, source_target_pairs={{0,16},{2,18},{4,20},{6,22},{8,24},{10,26},{12,28},{14,30},{16,0},... | collective-permute-start | bytes 786440 | tf_op jit(solution)/shard_map/ppermute | solution.py:330
  63.7 14.6 %collective-permute-start.8 = (f32[32,16,128]{2,1,0:T(8,128)S(1)}, f32[32,16,128]{2,1,0:T(8,128)S(1)}, u32[]{:S(2)}, u32[]{:S(2)}) collective-permute-start(f32[32,16,128]{2,1,0:T(8,128)S(1)} %get-tuple-element.152), channel_id=1, source_target_pairs={{0,24},{2,26},{4,28},{6,30},{8,0},{10,2},{12,4},{14,6},{16,8},{18,... | collective-permute-start | bytes 786440 | tf_op jit(solution)/shard_map/ppermute | solution.py:330
  63.7 12.3 %collective-permute-start.14 = (f32[32,16,128]{2,1,0:T(8,128)S(1)}, f32[32,16,128]{2,1,0:T(8,128)S(1)}, u32[]{:S(2)}, u32[]{:S(2)}) collective-permute-start(f32[32,16,128]{2,1,0:T(8,128)S(1)} %get-tuple-element.158), channel_id=1, source_target_pairs={{0,4},{2,6},{4,0},{6,2},{8,12},{10,14},{12,8},{14,10},{16,20},{18,... | collective-permute-start | bytes 786440 | tf_op jit(solution)/shard_map/ppermute | solution.py:330
  66.7 9.2 %collective-permute-start.13 = (f32[32,16,128]{2,1,0:T(8,128)S(1)}, f32[32,16,128]{2,1,0:T(8,128)S(1)}, u32[]{:S(2)}, u32[]{:S(2)}) collective-permute-start(f32[32,16,128]{2,1,0:T(8,128)S(1)} %get-tuple-element.158), channel_id=1, source_target_pairs={{0,6},{2,0},{4,2},{6,4},{8,14},{10,8},{12,10},{14,12},{16,22},{18,... | collective-permute-start | bytes 786440 | tf_op jit(solution)/shard_map/ppermute | solution.py:330
  67.8 9.7 %collective-permute-start.7 = (f32[32,16,128]{2,1,0:T(8,128)S(1)}, f32[32,16,128]{2,1,0:T(8,128)S(1)}, u32[]{:S(2)}, u32[]{:S(2)}) collective-permute-start(f32[32,16,128]{2,1,0:T(8,128)S(1)} %get-tuple-element.152), channel_id=1, source_target_pairs={{0,8},{2,10},{4,12},{6,14},{8,16},{10,18},{12,20},{14,22},{16,24},... | collective-permute-start | bytes 786440 | tf_op jit(solution)/shard_map/ppermute | solution.py:330
  76.0 21.6 %collective-permute-start.16 = (f32[128,16,128]{2,1,0:T(8,128)S(1)}, f32[128,16,128]{2,1,0:T(8,128)S(1)}, u32[]{:S(2)}, u32[]{:S(2)}) collective-permute-start(f32[128,16,128]{2,1,0:T(8,128)S(1)} %constant_dynamic-update-slice_fusion.4), channel_id=1, source_target_pairs={{0,24},{2,26},{4,28},{6,30},{8,0},{10,2},{12,4},{14,6},{16,8},{18,... | collective-permute-start | bytes 3145736 | tf_op jit(solution)/shard_map/ppermute | solution.py:330
  76.1 24.7 %collective-permute-start.15 = (f32[128,16,128]{2,1,0:T(8,128)S(1)}, f32[128,16,128]{2,1,0:T(8,128)S(1)}, u32[]{:S(2)}, u32[]{:S(2)}) collective-permute-start(f32[128,16,128]{2,1,0:T(8,128)S(1)} %constant_dynamic-update-slice_fusion.4), channel_id=1, source_target_pairs={{0,8},{2,10},{4,12},{6,14},{8,16},{10,18},{12,20},{14,22},{16,24},... | collective-permute-start | bytes 3145736 | tf_op jit(solution)/shard_map/ppermute | solution.py:330
  79.7 29.0 %collective-permute-start.11 = (f32[128,16,128]{2,1,0:T(8,128)}, f32[128,16,128]{2,1,0:T(8,128)}, u32[]{:S(2)}, u32[]{:S(2)}) collective-permute-start(f32[128,16,128]{2,1,0:T(8,128)} %constant_dynamic-update-slice_fusion), channel_id=1, source_target_pairs={{0,6},{2,0},{4,2},{6,4},{8,14},{10,8},{12,10},{14,12},{16,22},{18,... | collective-permute-start | bytes 3145736 | tf_op jit(solution)/shard_map/ppermute | solution.py:330
  83.2 25.4 %collective-permute-start.10 = (f32[128,16,128]{2,1,0:T(8,128)}, f32[128,16,128]{2,1,0:T(8,128)}, u32[]{:S(2)}, u32[]{:S(2)}) collective-permute-start(f32[128,16,128]{2,1,0:T(8,128)} %constant_dynamic-update-slice_fusion), channel_id=1, source_target_pairs={{0,2},{2,4},{4,6},{6,0},{8,10},{10,12},{12,14},{14,8},{16,18},{18,... | collective-permute-start | bytes 3145736 | tf_op jit(solution)/shard_map/ppermute | solution.py:330
  83.2 25.4 %all-to-all-start.2 = ((f32[16,32,128]{2,1,0:T(8,128)}), f32[16,32,128]{2,1,0:T(8,128)}, u32[]{:S(2)}, u32[]{:S(2)}) async-start(f32[16,32,128]{2,1,0:T(8,128)} %bitcast.12), calls=%async_computation.2 | async-start | bytes 524288 | tf_op jit(solution)/shard_map/all_to_all | solution.py:612
  97.6 1.0 copy-start.5
  99.4 27.8 %collective-permute-start.18 = (f32[64,16,128]{2,1,0:T(8,128)}, f32[64,16,128]{2,1,0:T(8,128)S(1)}, u32[]{:S(2)}, u32[]{:S(2)}) collective-permute-start(f32[64,16,128]{2,1,0:T(8,128)} %slice.74), channel_id=1, source_target_pairs={{0,24},{2,26},{4,28},{6,30},{8,0},{10,2},{12,4},{14,6},{16,8},{18,... | collective-permute-start | bytes 1572872 | tf_op jit(solution)/shard_map/ppermute | solution.py:330
  101.7 25.5 %collective-permute-start.17 = (f32[64,16,128]{2,1,0:T(8,128)}, f32[64,16,128]{2,1,0:T(8,128)S(1)}, u32[]{:S(2)}, u32[]{:S(2)}) collective-permute-start(f32[64,16,128]{2,1,0:T(8,128)} %slice.73), channel_id=1, source_target_pairs={{0,8},{2,10},{4,12},{6,14},{8,16},{10,18},{12,20},{14,22},{16,24},... | collective-permute-start | bytes 1572872 | tf_op jit(solution)/shard_map/ppermute | solution.py:330
  112.4 14.8 %collective-permute-start.20 = (f32[64,16,128]{2,1,0:T(8,128)}, f32[64,16,128]{2,1,0:T(8,128)}, u32[]{:S(2)}, u32[]{:S(2)}) collective-permute-start(f32[64,16,128]{2,1,0:T(8,128)} %slice.65), channel_id=1, source_target_pairs={{0,6},{2,0},{4,2},{6,4},{8,14},{10,8},{12,10},{14,12},{16,22},{18,... | collective-permute-start | bytes 1572872 | tf_op jit(solution)/shard_map/ppermute | solution.py:330
  112.8 14.4 %collective-permute-start.19 = (f32[64,16,128]{2,1,0:T(8,128)}, f32[64,16,128]{2,1,0:T(8,128)}, u32[]{:S(2)}, u32[]{:S(2)}) collective-permute-start(f32[64,16,128]{2,1,0:T(8,128)} %slice.64), channel_id=1, source_target_pairs={{0,2},{2,4},{4,6},{6,0},{8,10},{10,12},{12,14},{14,8},{16,18},{18,... | collective-permute-start | bytes 1572872 | tf_op jit(solution)/shard_map/ppermute | solution.py:330
  121.6 1.0 copy-start
